TPU v7x, 32 devices: a whole 2x2x4 slice. The times are simulated.
32 devices in a mesh: batch: 8 (over y, x, core), head: 4 (over z).
Axes of the slice: x: 2, y: 2, z: 4, core: 2. Of those that a mesh axis runs over, the one named last changes fastest.
Arguments:
- layer_input: bfloat16 [16, 512, 768], P('batch', 'head'), may hold values from -6 to 6
- memory: bfloat16 [16, 512, 768], P('batch', 'head'), may hold values from -6 to 6
- dec_lengths: int32 [16], P('batch'), may hold values from 1 to 512, as said below
- enc_lengths: int32 [16], P('batch'), may hold values from 1 to 512, as said below
- self_gain: bfloat16 [768], replicated, may hold values from 0.099609375 to 1.8984375
- self_query: bfloat16 [768, 768], P(None, 'head'), may hold values from -0.0546875 to 0.0546875
- self_key_value: bfloat16 [2, 768, 768], P(None, None, 'head'), may hold values from -0.21875 to 0.21875
- self_out: bfloat16 [768, 768], P('head'), may hold values from -0.875 to 0.875
- rel_bias: bfloat16 [32, 12], P(None, 'head'), may hold values from -4 to 4
- cross_gain: bfloat16 [768], replicated, may hold values from 0.099609375 to 1.8984375
- cross_query: bfloat16 [768, 768], P(None, 'head'), may hold values from -0.0546875 to 0.0546875
- cross_key_value: bfloat16 [2, 768, 768], P(None, None, 'head'), may hold values from -0.21875 to 0.21875
- cross_out: bfloat16 [768, 768], P('head'), may hold values from -0.875 to 0.875
- feed_gain: bfloat16 [768], replicated, may hold values from 0.099609375 to 1.8984375
- feed_in: bfloat16 [2, 768, 2048], replicated, may hold values from -0.21875 to 0.21875
- feed_out: bfloat16 [2048, 768], replicated, may hold values from -0.125 to 0.125
- out_cotangent: bfloat16 [16, 512, 768], P('batch', 'head'), may hold values from -6 to 6
Outputs:
- layer_output: bfloat16 [16, 512, 768], P('batch', 'head')
- input_grad: float32 [16, 512, 768], P('batch', 'head')
- memory_grad: float32 [16, 512, 768], P('batch', 'head')
- self_gain_grad: float32 [768], replicated
- self_query_grad: float32 [768, 768], P('batch', 'head')
- self_key_value_grad: float32 [2, 768, 768], P(None, 'batch', 'head')
- self_out_grad: float32 [768, 768], P('head', 'batch')
- rel_bias_grad: float32 [32, 12], P(None, 'head')
- cross_gain_grad: float32 [768], replicated
- cross_query_grad: float32 [768, 768], P('batch', 'head')
- cross_key_value_grad: float32 [2, 768, 768], P(None, 'batch', 'head')
- cross_out_grad: float32 [768, 768], P('head', 'batch')
- feed_gain_grad: float32 [768], replicated
- feed_in_grad: float32 [2, 768, 2048], P(None, 'batch', 'head')
- feed_out_grad: float32 [2048, 768], P('head', 'batch')
Inputs may be any that keep to these rules, and one draw needn't show every extreme that they name: `dec_lengths`: some sequence has exactly 512 decoder positions. `enc_lengths`: some sequence has exactly 512 encoder positions.
All inputs are finite; a program needn't handle non-finite values.
Results may differ from a plain program's by a relative error of at most 0.023.
The roundings to bfloat16 on the way count: a program that leaves them out, or rounds other values in their place, can miss the bound.
Values may be sent and summed in bfloat16 or wider, within the bound.
A program may use at most 256 MiB of HBM per device.

v0:
```python
import math

import jax
import jax.numpy as jnp
from jax import lax
from jax.sharding import PartitionSpec as P

NB = 32
MAX_DIST = 128


highest = lax.Precision.HIGHEST


def bucket_edges(num_buckets, max_distance):
    exact_part = num_buckets // 2
    edge_list = []
    for target in range(1, num_buckets - exact_part):
        distance = exact_part
        while (
            math.floor(
                math.log(distance / exact_part)
                / math.log(max_distance / exact_part)
                * (num_buckets - exact_part)
            )
            < target
        ):
            distance += 1
        edge_list.append(distance)
    return edge_list


def bucket_of(distance, num_buckets, max_distance):
    exact_part = num_buckets // 2
    counted = jnp.zeros(distance.shape, jnp.int32)
    for edge_value in bucket_edges(num_buckets, max_distance):
        counted = counted + (distance >= edge_value).astype(jnp.int32)
    return jnp.where(distance < exact_part, distance, exact_part + counted).astype(jnp.int32)


def normalize(activations, gain_vector):
    return (
        activations
        * lax.rsqrt(jnp.mean(activations * activations, axis=-1, keepdims=True) + 1e-06)
        * gain_vector
    )


def norm_backward(activations, gain_vector, grad_normed):
    outcome, pullback = jax.vjp(normalize, activations, gain_vector)
    return pullback(grad_normed)


def bias_matrix(offset_table, length):
    num_heads = offset_table.shape[0]
    padded_row = jnp.concatenate(
        [jnp.zeros((num_heads, length - 1), jnp.float32), offset_table], axis=1
    )
    spread = jnp.broadcast_to(padded_row[:, None, :], (num_heads, length, 2 * length - 1)).reshape(
        num_heads, length * (2 * length - 1)
    )
    spread = jnp.concatenate([spread, jnp.zeros((num_heads, length), jnp.float32)], axis=1).reshape(
        num_heads, length, 2 * length
    )
    return jnp.flip(spread[:, :, :length], axis=2)


def diagonal_sums(score_grid):
    num_heads, length = (score_grid.shape[0], score_grid.shape[1])
    flipped = jnp.flip(score_grid, axis=2)
    padded = jnp.concatenate(
        [flipped, jnp.zeros((num_heads, length, length), jnp.float32)], axis=2
    ).reshape(num_heads, 2 * length * length)
    skewed = padded[:, : length * (2 * length - 1)].reshape(num_heads, length, 2 * length - 1)
    return jnp.sum(skewed, axis=1)[:, length - 1 :]


def attend_forward(queries, key_block, value_block, score_bias, keep_mask):
    scores = (
        jnp.einsum("sqhd,skhd->shqk", queries, key_block, preferred_element_type=jnp.float32)
        + score_bias
    )
    scores = jnp.where(keep_mask, scores, -1e30)
    row_max = jnp.max(scores, axis=-1, keepdims=True)
    exponent = jnp.exp(scores - row_max)
    row_total = jnp.sum(exponent, axis=-1, keepdims=True)
    attn_probs = (exponent / row_total).astype(jnp.bfloat16)
    context = jnp.einsum(
        "shqk,skhd->sqhd", attn_probs, value_block, preferred_element_type=jnp.float32
    ).astype(jnp.bfloat16)
    return (context, row_max + jnp.log(row_total))


def attend_backward(
    queries, key_block, value_block, score_bias, keep_mask, log_total, grad_context
):
    scores = (
        jnp.einsum("sqhd,skhd->shqk", queries, key_block, preferred_element_type=jnp.float32)
        + score_bias
    )
    scores = jnp.where(keep_mask, scores, -1e30)
    attn_probs = jnp.exp(scores - log_total)
    grad_probs = jnp.einsum(
        "sqhd,skhd->shqk", grad_context, value_block, preferred_element_type=jnp.float32
    )
    grad_scores = (
        attn_probs * (grad_probs - jnp.sum(attn_probs * grad_probs, axis=-1, keepdims=True))
    ).astype(jnp.bfloat16)
    grad_values = jnp.einsum(
        "shqk,sqhd->skhd",
        attn_probs.astype(jnp.bfloat16),
        grad_context,
        preferred_element_type=jnp.float32,
    ).astype(jnp.bfloat16)
    grad_queries = jnp.einsum(
        "shqk,skhd->sqhd", grad_scores, key_block, preferred_element_type=jnp.float32
    ).astype(jnp.bfloat16)
    grad_keys = jnp.einsum(
        "shqk,sqhd->skhd", grad_scores, queries, preferred_element_type=jnp.float32
    ).astype(jnp.bfloat16)
    return (grad_queries, grad_keys, grad_values, grad_scores)


def feed_forward(row_block, weight_in, weight_out):
    gate_up = jnp.einsum("std,cdf->cstf", row_block, weight_in, preferred_element_type=jnp.float32)
    activated, pullback = jax.vjp(
        lambda gate_part, up_part: jax.nn.gelu(gate_part, approximate=True) * up_part,
        gate_up[0],
        gate_up[1],
    )
    hidden = activated.astype(jnp.bfloat16)
    return (
        hidden,
        pullback,
        jnp.einsum("stf,fd->std", hidden, weight_out, preferred_element_type=jnp.float32),
    )


def feed_backward(pullback, grad_rows, weight_in, weight_out):
    grad_hidden = jnp.einsum(
        "std,fd->stf", grad_rows, weight_out, preferred_element_type=jnp.float32
    )
    grad_gate, grad_up = pullback(grad_hidden)
    grad_gates = jnp.stack([grad_gate, grad_up]).astype(jnp.bfloat16)
    grad_normed = jnp.einsum(
        "cstf,cdf->std", grad_gates, weight_in, preferred_element_type=jnp.float32
    )
    return (grad_gates, grad_normed)


def per_device(
    layer_input,
    memory,
    dec_lengths,
    enc_lengths,
    self_gain,
    self_query,
    self_key_value,
    self_out,
    rel_bias,
    cross_gain,
    cross_query,
    cross_key_value,
    cross_out,
    feed_gain,
    feed_in,
    feed_out,
    out_cotangent,
):
    head_count = lax.axis_size("head")
    head_index = lax.axis_index("head")
    batch_count = lax.axis_size("batch")
    seq_count, local_len, model_width = layer_input.shape
    enc_local = memory.shape[1]
    num_heads = rel_bias.shape[1]
    head_size = self_query.shape[1] // num_heads
    local_width = num_heads * head_size
    full_len = local_len * head_count
    enc_full = enc_local * head_count
    part_width = feed_in.shape[2] // head_count
    slice_width = model_width // batch_count

    def project(row_block, weight):
        product = jnp.einsum("std,de->ste", row_block, weight, preferred_element_type=jnp.float32)
        return product.astype(jnp.bfloat16).reshape(
            row_block.shape[0], row_block.shape[1], num_heads, head_size
        )

    def flatten(tensor):
        return tensor.reshape(tensor.shape[0], tensor.shape[1], local_width)

    def attention_backward(
        query_rows,
        pair_rows,
        queries,
        key_block,
        value_block,
        context,
        score_bias,
        keep_mask,
        log_total,
        grad_rows,
        weight_out,
    ):
        out_part = jnp.einsum("std,ste->de", grad_rows, context, preferred_element_type=jnp.float32)
        grad_context = jnp.einsum(
            "std,ed->ste", grad_rows, weight_out, preferred_element_type=jnp.float32
        ).astype(jnp.bfloat16)
        grad_context = grad_context.reshape(
            grad_rows.shape[0], grad_rows.shape[1], num_heads, head_size
        )
        grad_queries, grad_keys, grad_values, grad_scores = attend_backward(
            queries, key_block, value_block, score_bias, keep_mask, log_total, grad_context
        )
        grad_queries = flatten(grad_queries)
        grad_pairs = jnp.stack([flatten(grad_keys), flatten(grad_values)])
        query_part = jnp.einsum(
            "std,ste->de", query_rows, grad_queries, preferred_element_type=jnp.float32
        )
        pair_part = jnp.einsum(
            "std,cste->dce", pair_rows, grad_pairs, preferred_element_type=jnp.float32
        )
        return (query_part, pair_part, out_part, grad_queries, grad_pairs, grad_scores)

    positions = jnp.arange(full_len)
    onehot_buckets = (
        bucket_of(positions, NB, MAX_DIST)[:, None] == jnp.arange(NB)[None, :]
    ).astype(jnp.float32)
    offset_table = jnp.einsum(
        "nb,bh->hn", onehot_buckets, rel_bias.astype(jnp.float32), precision=highest
    )
    self_bias = bias_matrix(offset_table, full_len)[None]
    self_mask = (positions[:, None] >= positions[None, :])[None, None] & (
        positions[None, None, None, :] < dec_lengths[:, None, None, None]
    )
    cross_mask = jnp.arange(enc_full)[None, None, None, :] < enc_lengths[:, None, None, None]
    self_gain32 = self_gain.astype(jnp.float32)
    cross_gain32 = cross_gain.astype(jnp.float32)
    feed_gain32 = feed_gain.astype(jnp.float32)
    inputs = layer_input.astype(jnp.float32)
    normed_one = normalize(inputs, self_gain32).astype(jnp.bfloat16)
    rows_one, memory_rows = (
        lax.all_gather(normed_one, "head", axis=1, tiled=True),
        lax.all_gather(memory, "head", axis=1, tiled=True),
    )
    query_one = project(rows_one, self_query)
    key_one = project(rows_one, self_key_value[0])
    value_one = project(rows_one, self_key_value[1])
    context_one, lse_one = attend_forward(query_one, key_one, value_one, self_bias, self_mask)
    context_one = flatten(context_one)
    partial_one = jnp.einsum(
        "ste,ed->std", context_one, self_out, preferred_element_type=jnp.float32
    )
    after_self = inputs + lax.psum_scatter(partial_one, "head", scatter_dimension=1, tiled=True)
    normed_two = normalize(after_self, cross_gain32).astype(jnp.bfloat16)
    rows_two = lax.all_gather(normed_two, "head", axis=1, tiled=True)
    query_two = project(rows_two, cross_query)
    key_two = project(memory_rows, cross_key_value[0])
    value_two = project(memory_rows, cross_key_value[1])
    context_two, lse_two = attend_forward(query_two, key_two, value_two, 0.0, cross_mask)
    context_two = flatten(context_two)
    partial_two = jnp.einsum(
        "ste,ed->std", context_two, cross_out, preferred_element_type=jnp.float32
    )
    after_cross = after_self + lax.psum_scatter(
        partial_two, "head", scatter_dimension=1, tiled=True
    )
    normed_three = normalize(after_cross, feed_gain32).astype(jnp.bfloat16)
    hidden, pullback, feed_part = feed_forward(normed_three, feed_in, feed_out)
    result = after_cross + feed_part
    grad_gates, grad_normed_three = feed_backward(pullback, out_cotangent, feed_in, feed_out)
    rows_split = normed_three.reshape(seq_count, local_len, batch_count, slice_width)
    gates_split = grad_gates.reshape(2, seq_count, local_len, head_count, part_width)
    in_blocks = jnp.einsum(
        "stbr,cstgf->bgcrf", rows_split, gates_split, preferred_element_type=jnp.float32
    )
    hidden_split = hidden.reshape(seq_count, local_len, head_count, part_width)
    cot_split = out_cotangent.reshape(seq_count, local_len, batch_count, slice_width)
    out_blocks = jnp.einsum(
        "stgf,stbr->bgfr", hidden_split, cot_split, preferred_element_type=jnp.float32
    )
    in_summed, out_summed = (
        lax.psum_scatter(in_blocks, "head", scatter_dimension=1, tiled=True),
        lax.psum_scatter(out_blocks, "head", scatter_dimension=1, tiled=True),
    )
    feed_in_blocks = in_summed.reshape(batch_count, 2, slice_width, part_width)
    feed_out_blocks = out_summed.reshape(batch_count, part_width, slice_width)
    grad_cross_part, grad_feed_gain = norm_backward(after_cross, feed_gain32, grad_normed_three)
    grad_after_cross = out_cotangent.astype(jnp.float32) + grad_cross_part
    grad_rows_two = lax.all_gather(
        grad_after_cross.astype(jnp.bfloat16), "head", axis=1, tiled=True
    )
    (
        cross_query_part,
        cross_pair_part,
        cross_out_part,
        grad_queries_two,
        grad_pairs_two,
        unused_scores,
    ) = attention_backward(
        rows_two,
        memory_rows,
        query_two,
        key_two,
        value_two,
        context_two,
        0.0,
        cross_mask,
        lse_two,
        grad_rows_two,
        cross_out,
    )
    grad_query_two = jnp.einsum(
        "ste,de->std", grad_queries_two, cross_query, preferred_element_type=jnp.float32
    )
    memory_partial = jnp.einsum(
        "cste,cde->std", grad_pairs_two, cross_key_value, preferred_element_type=jnp.float32
    )
    grad_normed_two = lax.psum_scatter(grad_query_two, "head", scatter_dimension=1, tiled=True)
    grad_self_part, grad_cross_gain = norm_backward(after_self, cross_gain32, grad_normed_two)
    grad_after_self = grad_after_cross + grad_self_part
    grad_rows_one = lax.all_gather(grad_after_self.astype(jnp.bfloat16), "head", axis=1, tiled=True)
    (
        self_query_part,
        self_pair_part,
        self_out_part,
        grad_queries_one,
        grad_pairs_one,
        grad_scores_one,
    ) = attention_backward(
        rows_one,
        rows_one,
        query_one,
        key_one,
        value_one,
        context_one,
        self_bias,
        self_mask,
        lse_one,
        grad_rows_one,
        self_out,
    )
    diagonals = diagonal_sums(jnp.sum(grad_scores_one.astype(jnp.float32), axis=0))
    bias_local = jnp.einsum("nb,hn->bh", onehot_buckets, diagonals, precision=highest)
    row_terms = jnp.einsum(
        "ste,de->std", grad_queries_one, self_query, preferred_element_type=jnp.float32
    ) + jnp.einsum(
        "cste,cde->std", grad_pairs_one, self_key_value, preferred_element_type=jnp.float32
    )
    grad_normed_one, memory_grad = (
        lax.psum_scatter(row_terms, "head", scatter_dimension=1, tiled=True),
        lax.psum_scatter(memory_partial, "head", scatter_dimension=1, tiled=True),
    )
    grad_input_part, grad_self_gain = norm_backward(inputs, self_gain32, grad_normed_one)
    input_grad = grad_after_self + grad_input_part
    bias_full = lax.dynamic_update_slice_in_dim(
        jnp.zeros((NB, num_heads * head_count), jnp.float32), bias_local, head_index * num_heads, 1
    )
    gain_sums, bias_sums = lax.psum(
        (jnp.stack([grad_self_gain, grad_cross_gain, grad_feed_gain]), bias_full), ("batch", "head")
    )
    rel_bias_grad = lax.dynamic_slice_in_dim(bias_sums, head_index * num_heads, num_heads, 1)
    summed = (
        lax.psum_scatter(self_query_part, "batch", scatter_dimension=0, tiled=True),
        lax.psum_scatter(self_pair_part, "batch", scatter_dimension=0, tiled=True),
        lax.psum_scatter(self_out_part, "batch", scatter_dimension=0, tiled=True),
        lax.psum_scatter(cross_query_part, "batch", scatter_dimension=0, tiled=True),
        lax.psum_scatter(cross_pair_part, "batch", scatter_dimension=0, tiled=True),
        lax.psum_scatter(cross_out_part, "batch", scatter_dimension=0, tiled=True),
        lax.psum_scatter(feed_in_blocks, "batch", scatter_dimension=0, tiled=True),
        lax.psum_scatter(feed_out_blocks, "batch", scatter_dimension=0, tiled=True),
    )
    return (
        result.astype(jnp.bfloat16),
        input_grad,
        memory_grad,
        gain_sums[0],
        summed[0],
        jnp.transpose(summed[1], (1, 0, 2)),
        jnp.transpose(summed[2]),
        rel_bias_grad,
        gain_sums[1],
        summed[3],
        jnp.transpose(summed[4], (1, 0, 2)),
        jnp.transpose(summed[5]),
        gain_sums[2],
        summed[6][0],
        summed[7][0],
    )


def solution(mesh):
    return jax.shard_map(
        per_device,
        mesh=mesh,
        in_specs=(
            P("batch", "head", None),
            P("batch", "head", None),
            P("batch"),
            P("batch"),
            P(),
            P(None, "head"),
            P(None, None, "head"),
            P("head", None),
            P(None, "head"),
            P(),
            P(None, "head"),
            P(None, None, "head"),
            P("head", None),
            P(),
            P(),
            P(),
            P("batch", "head", None),
        ),
        out_specs=(
            P("batch", "head", None),
            P("batch", "head", None),
            P("batch", "head", None),
            P(),
            P("batch", "head"),
            P(None, "batch", "head"),
            P("head", "batch"),
            P(None, "head"),
            P(),
            P("batch", "head"),
            P(None, "batch", "head"),
            P("head", "batch"),
            P(),
            P(None, "batch", "head"),
            P("head", "batch"),
        ),
        check_vma=False,
    )
```

profile of v0, /device:TPU:0, one launch (start us, length us, event | category | flops | bytes accessed | tf_op | source)
XLA Modules:
  0.0 1491.1 jit_solution(14355543970304761380)
XLA Ops:
  14.0 3.5 broadcast_in_dim.41
  17.5 13.4 reshape.317
  31.0 4.9 concatenate.12
  35.9 3.6 copy.197
  41.6 26.0 %rev.7 = f32[3,512,512]{2,1,0:T(8,128)} reverse(f32[3,512,512]{2,1,0:T(8,128)} %slice.48), dimensions={2} | reverse | bytes 6291456 | tf_op jit(solution)/shard_map/jit(_flip)/rev | solution.py:65
  67.7 3.6 copy.120
  87.5 62.3 %reduce-scatter.22.cloned.1.call-done = f32[2,128,768]{2,1,0:T(8,128)} async-done(((f32[2,512,768]{2,1,0:T(8,128)}), f32[2,128,768]{2,1,0:T(8,128)}) %reduce-scatter.22.cloned.1.call-update) | async-done | bytes 786448 | tf_op jit(solution)/shard_map/reduce_scatter | solution.py:254
  154.1 34.5 %all-gather.8.cloned.1.call-done = bf16[2,512,768]{2,1,0:T(8,128)(2,1)} async-done(((bf16[2,128,768]{2,1,0:T(8,128)(2,1)}), bf16[2,512,768]{2,1,0:T(8,128)(2,1)}) %all-gather.8.cloned.1.call-update) | async-done | bytes 1572880 | tf_op jit(solution)/shard_map/all_gather | solution.py:244
  194.3 32.3 %all-gather.10.cloned.1.call-done = bf16[2,512,768]{2,1,0:T(8,128)(2,1)} async-done(((bf16[2,128,768]{2,1,0:T(8,128)(2,1)}), bf16[2,512,768]{2,1,0:T(8,128)(2,1)}) %all-gather.10.cloned.1.call-update) | async-done | bytes 1572880 | tf_op jit(solution)/shard_map/all_gather | solution.py:256
  239.9 58.0 %reduce-scatter.24.cloned.1.call-done = f32[2,128,768]{2,1,0:T(8,128)} async-done(((f32[2,512,768]{2,1,0:T(8,128)}), f32[2,128,768]{2,1,0:T(8,128)}) %reduce-scatter.24.cloned.1.call-update) | async-done | bytes 786448 | tf_op jit(solution)/shard_map/reduce_scatter | solution.py:265
  300.3 4.7 fusion.8
  314.5 35.5 %all-gather.12.cloned.1.call-done = bf16[2,512,768]{2,1,0:T(8,128)(2,1)} async-done(((bf16[2,128,768]{2,1,0:T(8,128)(2,1)}), bf16[2,512,768]{2,1,0:T(8,128)(2,1)}) %all-gather.12.cloned.1.call-update) | async-done | bytes 1572880 | tf_op jit(solution)/shard_map/all_gather | solution.py:290
  352.2 5.0 multiply_reduce_fusion.1
  364.2 59.2 %reduce-scatter.26.cloned.1.call-done = f32[2,128,768]{2,1,0:T(8,128)} async-done(((f32[2,512,768]{2,1,0:T(8,128)}), f32[2,128,768]{2,1,0:T(8,128)}) %reduce-scatter.26.cloned.1.call-update) | async-done | bytes 786448 | tf_op jit(solution)/shard_map/reduce_scatter | solution.py:319
  426.3 3.4 fusion.133
  439.9 5.7 convolution_bitcast_fusion
  447.6 3.9 fusion.40
  454.1 5.0 convolution_bitcast_fusion.1
  459.2 3.0 convolution_bitcast_fusion.3
  462.4 3.1 convolution_convert_fusion
  465.6 4.3 fusion.73
  481.2 7.1 multiply_reduce_fusion
  488.3 8.1 convert_reduce_fusion
  496.3 398.1 %all-reduce.9.cloned.1.call-done = f32[8,4,2,96,512]{4,3,0,1,2:T(8,128)} async-done(((f32[8,4,2,96,512]{4,3,0,1,2:T(8,128)}), f32[8,4,2,96,512]{4,3,0,1,2:T(8,128)}) %all-reduce.9.cloned.1.call-update) | async-done | bytes 12582928
  894.5 4.6 dynamic-slice_bitcast_fusion
  899.2 3.1 convolution_convert_fusion.1
  902.3 4.2 fusion.70
  912.5 3.0 convolution_bitcast_fusion.4
  915.7 4.0 convolution_bitcast_fusion.2
  919.8 3.0 convolution_bitcast_fusion.6
  922.8 3.7 fusion.55
  926.7 79.7 %reduce-scatter.42.cloned.1.call-done = f32[8,1,512,96]{2,3,0,1:T(8,128)} async-done(((f32[8,4,512,96]{2,3,0,1:T(8,128)}), f32[8,1,512,96]{2,3,0,1:T(8,128)}) %reduce-scatter.42.cloned.1.call-update) | async-done | bytes 1572880 | tf_op jit(solution)/shard_map/reduce_scatter | solution.py:284
  1007.6 4.6 fusion.67
  1012.1 32.9 %reduce-scatter.40.cloned.1.call-done = f32[96,192]{1,0:T(8,128)} async-done(((f32[768,192]{1,0:T(8,128)}), f32[96,192]{1,0:T(8,128)}) %reduce-scatter.40.cloned.1.call-update) | async-done | bytes 73744 | tf_op jit(solution)/shard_map/reduce_scatter | solution.py:369
  1046.7 38.3 %reduce-scatter.46.cloned.1.call-done = f32[96,384]{1,0:T(8,128)} async-done(((f32[768,384]{1,0:T(8,128)}), f32[96,384]{1,0:T(8,128)}) %reduce-scatter.46.cloned.1.call-update) | async-done | bytes 147472
  1089.0 24.6 %rev.8 = f32[3,512,512]{1,2,0:T(8,128)} reverse(f32[3,512,512]{1,2,0:T(8,128)} %get-tuple-element.86), dimensions={2} | reverse | bytes 6291456 | tf_op jit(solution)/shard_map/jit(_flip)/rev | solution.py:70
  1113.6 3.6 copy.187
  1119.9 7.6 copy.189
  1127.5 8.0 slice.52
  1135.5 13.3 reshape.329
  1148.9 3.8 reduce_sum.155
  1156.7 39.7 %all-reduce.11.cloned.1.call-done = f32[8,2,96,512]{3,2,0,1:T(8,128)} async-done(((f32[8,2,96,512]{3,2,0,1:T(8,128)}), f32[8,2,96,512]{3,2,0,1:T(8,128)}) %all-reduce.11.cloned.1.call-update) | async-done | bytes 3145744
  1198.8 60.1 %reduce-scatter.28.cloned.1.call-done = f32[2,128,768]{2,1,0:T(8,128)} async-done(((f32[2,512,768]{2,1,0:T(8,128)}), f32[2,128,768]{2,1,0:T(8,128)}) %reduce-scatter.28.cloned.1.call-update) | async-done | bytes 786448 | tf_op jit(solution)/shard_map/reduce_scatter | solution.py:351
  1261.6 40.9 %all-reduce.5 = (f32[3,768]{1,0:T(4,128)}, f32[32,12]{0,1:T(8,128)}) all-reduce(f32[3,768]{1,0:T(4,128)S(1)} %pad_maximum_fusion.6, f32[32,12]{0,1:T(8,128)} %copy-done.55), channel_id=1, replica_groups=mesh['batch'=8,'head'=4] {'batch','head'}, use_global_device_ids=true, to_apply=%region_20.21 | all-reduce | flops 2688 | bytes 21504 | tf_op jit(solution)/shard_map/psum | solution.py:359
  1308.7 51.9 %reduce-scatter.30.cloned.1.call-done = f32[2,128,768]{2,1,0:T(8,128)} async-done(((f32[2,512,768]{2,1,0:T(8,128)}), f32[2,128,768]{2,1,0:T(8,128)}) %reduce-scatter.30.cloned.1.call-update) | async-done | bytes 786448 | tf_op jit(solution)/shard_map/reduce_scatter | solution.py:352
  1360.6 38.6 %reduce-scatter.32.cloned.1.call-done = f32[96,192]{1,0:T(8,128)} async-done(((f32[768,192]{1,0:T(8,128)}), f32[96,192]{1,0:T(8,128)}) %reduce-scatter.32.cloned.1.call-update) | async-done | bytes 73744 | tf_op jit(solution)/shard_map/reduce_scatter | solution.py:364
  1399.2 42.4 %reduce-scatter.34.cloned.1.call-done = f32[96,2,192]{2,0,1:T(8,128)} async-done(((f32[768,2,192]{2,0,1:T(8,128)}), f32[96,2,192]{2,0,1:T(8,128)}) %reduce-scatter.34.cloned.1.call-update) | async-done | bytes 147472 | tf_op jit(solution)/shard_map/reduce_scatter | solution.py:365
  1441.6 42.2 %reduce-scatter.44.cloned.1.call-done = f32[1,512,96]{1,2,0:T(8,128)} async-done(((f32[8,512,96]{1,2,0:T(8,128)}), f32[1,512,96]{1,2,0:T(8,128)}) %reduce-scatter.44.cloned.1.call-update) | async-done | bytes 196624 | tf_op jit(solution)/shard_map/reduce_scatter | solution.py:371
  (285 shorter events, 129.0 us)
Async XLA Ops:
  7.2 297.9 %copy-start = (bf16[2048,768]{1,0:T(8,128)(2,1)S(1)}, bf16[2048,768]{1,0:T(8,128)(2,1)}, u32[]{:S(2)}) copy-start(bf16[2048,768]{1,0:T(8,128)(2,1)} %param.32) | copy-start | bytes 9437188
  7.2 65.3 %all-gather.6.cloned.1.call-start = ((), (), s32[]{:S(2)}) async-start(), calls=%async_computation.13 | async-start | bytes 1966080 | tf_op jit(solution)/shard_map/all_gather | solution.py:243
  12.3 137.5 %reduce-scatter.22.cloned.1.call-start = ((), (), s32[]{:S(2)}) async-start(), calls=%async_computation.14 | async-start | bytes 3932160 | tf_op jit(solution)/shard_map/reduce_scatter | solution.py:254
  72.5 4.5 copy-start.4
  72.5 4.5 copy-start.15
  84.4 65.4 %copy-start.9 = (bf16[2,128,768]{2,1,0:T(8,128)(2,1)S(1)}, bf16[2,128,768]{2,1,0:T(8,128)(2,1)}, u32[]{:S(2)}) copy-start(bf16[2,128,768]{2,1,0:T(8,128)(2,1)} %param.17) | copy-start | bytes 1179652
  86.7 66.8 %copy-start.69 = (s32[2]{0:T(128)S(1)}, s32[2]{0:T(128)}, u32[]{:S(2)}) copy-start(s32[2]{0:T(128)} %param.20) | copy-start | bytes 28
  86.7 101.9 %all-gather.8.cloned.1.call-start = ((), (), s32[]{:S(2)}) async-start(), calls=%async_computation.15 | async-start | bytes 1966080 | tf_op jit(solution)/shard_map/all_gather | solution.py:244
  87.5 139.1 %all-gather.10.cloned.1.call-start = ((), (), s32[]{:S(2)}) async-start(), calls=%async_computation.16 | async-start | bytes 1966080 | tf_op jit(solution)/shard_map/all_gather | solution.py:256
  87.5 106.8 %copy-start.53 = (f32[768]{0:T(1024)}, f32[768]{0:T(1024)S(1)}, u32[]{:S(2)}) copy-start(f32[768]{0:T(1024)S(1)} %convert_element_type.299) | copy-start | bytes 9220
  153.2 144.6 %reduce-scatter.24.cloned.1.call-start = ((), (), s32[]{:S(2)}) async-start(), calls=%async_computation.17 | async-start | bytes 3932160 | tf_op jit(solution)/shard_map/reduce_scatter | solution.py:265
  238.6 111.5 %all-gather.12.cloned.1.call-start = ((), (), s32[]{:S(2)}) async-start(), calls=%async_computation.18 | async-start | bytes 1966080 | tf_op jit(solution)/shard_map/all_gather | solution.py:290
  299.4 11.5 copy-start.8
  299.4 11.4 copy-start.60
  300.3 4.8 copy-start.10
  300.3 4.8 copy-start.12
  300.3 7.2 slice-start.4
  312.7 110.7 %reduce-scatter.26.cloned.1.call-start = ((), (), s32[]{:S(2)}) async-start(), calls=%async_computation.19 | async-start | bytes 3932160 | tf_op jit(solution)/shard_map/reduce_scatter | solution.py:319
  352.1 5.1 copy-start.34
  352.1 5.1 slice-start.2
  352.1 5.1 slice-start.3
  352.1 5.1 copy-start.45
  352.2 5.1 copy-start.47
  364.1 111.8 %all-gather.14.cloned.1.call-start = ((), (), s32[]{:S(2)}) async-start(), calls=%async_computation.20 | async-start | bytes 1966080 | tf_op jit(solution)/shard_map/all_gather | solution.py:322
  429.7 464.8 %all-reduce.9.cloned.1.call-start = ((), (), s32[]{:S(2)}) async-start(), calls=%async_computation.31 | async-start | bytes 25165824
  445.6 560.8 %reduce-scatter.42.cloned.1.call-start = ((), (), s32[]{:S(2)}) async-start(), calls=%async_computation.28 | async-start | bytes 7864320 | tf_op jit(solution)/shard_map/reduce_scatter | solution.py:284
  459.2 585.9 %reduce-scatter.40.cloned.1.call-start = ((), (), s32[]{:S(2)}) async-start(), calls=%async_computation.27 | async-start | bytes 884736 | tf_op jit(solution)/shard_map/reduce_scatter | solution.py:369
  462.2 622.8 %reduce-scatter.46.cloned.1.call-start = ((), (), s32[]{:S(2)}) async-start(), calls=%async_computation.30 | async-start | bytes 1327104
  465.6 4.4 copy-start.23
  465.6 4.4 copy-start.70
  470.0 4.6 copy-start.72
  474.5 680.5 %reduce-scatter.36.cloned.1.call-start = ((), (), s32[]{:S(2)}) async-start(), calls=%async_computation.25 | async-start | bytes 884736 | tf_op jit(solution)/shard_map/reduce_scatter | solution.py:366
  479.0 717.4 %all-reduce.11.cloned.1.call-start = ((), (), s32[]{:S(2)}) async-start(), calls=%async_computation.32 | async-start | bytes 6291456
  481.1 7.1 copy-start.16
  481.1 7.1 slice-start
  481.1 7.1 slice-start.1
  899.1 359.8 %reduce-scatter.28.cloned.1.call-start = ((), (), s32[]{:S(2)}) async-start(), calls=%async_computation.21 | async-start | bytes 3932160 | tf_op jit(solution)/shard_map/reduce_scatter | solution.py:351
  912.4 396.3 %reduce-scatter.38.cloned.1.call-start = ((), (), s32[]{:S(2)}) async-start(), calls=%async_computation.26 | async-start | bytes 884736 | tf_op jit(solution)/shard_map/reduce_scatter | solution.py:367
  915.5 445.1 %reduce-scatter.30.cloned.1.call-start = ((), (), s32[]{:S(2)}) async-start(), calls=%async_computation.22 | async-start | bytes 3932160 | tf_op jit(solution)/shard_map/reduce_scatter | solution.py:352
  919.7 479.5 %reduce-scatter.32.cloned.1.call-start = ((), (), s32[]{:S(2)}) async-start(), calls=%async_computation.23 | async-start | bytes 884736 | tf_op jit(solution)/shard_map/reduce_scatter | solution.py:364
  922.8 518.8 %reduce-scatter.34.cloned.1.call-start = ((), (), s32[]{:S(2)}) async-start(), calls=%async_computation.24 | async-start | bytes 1769472 | tf_op jit(solution)/shard_map/reduce_scatter | solution.py:365
  926.6 79.8 %copy-start.71 = (u32[32]{0:T(128)S(1)}, u32[32]{0:T(128)}, u32[]{:S(2)}) copy-start(u32[32]{0:T(128)} %constant.94) | copy-start | bytes 388
  926.6 80.4 %copy-start.64 = (f32[768]{0:T(1024)S(1)}, f32[768]{0:T(1024)}, u32[]{:S(2)}) copy-start(f32[768]{0:T(1024)} %get-tuple-element.77) | copy-start | bytes 9220
  926.6 557.2 %reduce-scatter.44.cloned.1.call-start = ((), (), s32[]{:S(2)}) async-start(), calls=%async_computation.29 | async-start | bytes 1769472 | tf_op jit(solution)/shard_map/reduce_scatter | solution.py:371
  1007.6 80.8 %copy-start.58 = (f32[768]{0:T(1024)S(1)}, f32[768]{0:T(1024)}, u32[]{:S(2)}) copy-start(f32[768]{0:T(1024)} %get-tuple-element.75) | copy-start | bytes 9220
  1148.9 110.0 %copy-start.50 = (f32[768]{0:T(1024)S(1)}, f32[768]{0:T(1024)}, u32[]{:S(2)}) copy-start(f32[768]{0:T(1024)} %copy-done.49) | copy-start | bytes 9220
  1148.9 110.0 %copy-start.57 = (f32[2,128]{1,0:T(2,128)S(1)}, f32[2,128]{1,0:T(2,128)}, u32[]{:S(2)}) copy-start(f32[2,128]{1,0:T(2,128)} %copy-done.56) | copy-start | bytes 3076
  1155.0 105.9 %copy-start.55 = (f32[32,12]{0,1:T(8,128)}, f32[32,12]{0,1:T(8,128)S(1)}, u32[]{:S(2)}) copy-start(f32[32,12]{0,1:T(8,128)S(1)} %dynamic_update_slice.3) | copy-start | bytes 4612
  (51 other events, 117.7 us)
Sparse Core Ops, SparseCore 0:
  12.5 39.7 all-gather.5
  86.8 62.9 reduce-scatter.21
  151.4 37.1 all-gather.7
  190.6 35.9 all-gather.9
  238.7 59.1 reduce-scatter.23
  312.9 37.0 all-gather.11
  364.3 59.0 reduce-scatter.25
  429.8 37.1 all-gather.13
  469.5 424.9 all-reduce.8
  896.6 109.6 reduce-scatter.41
  1009.5 35.4 reduce-scatter.39
  1048.1 36.7 reduce-scatter.45
  1088.4 34.9 reduce-scatter.35
  1126.9 69.4 all-reduce.10
  1198.5 60.2 reduce-scatter.27
  1262.5 35.0 reduce-scatter.37
  1300.2 60.2 reduce-scatter.29
  1364.2 35.0 reduce-scatter.31
  1403.1 38.4 reduce-scatter.33
  1445.3 38.4 reduce-scatter.43
where the time goes:
time: 1500 us; the launch traced here: 1490 us
  waiting for transfers between devices  1110 us (74%)
  local copies, waits for them, and re-layouts  168 us (11%)
  matrix products  111 us (7%)
  other arithmetic  46.8 us (3%)
  blocking collectives  40.9 us (3%)
  between operations  15.9 us (1%)
    unnamed x23, waiting for transfers between devices  477 us
    reduce_scatter x1, waiting for transfers between devices, per_device(): lax.psum_scatter(out_blocks, 'head', scatter_dimension=1, tiled=True)  79.7 us
    reduce_scatter x1, waiting for transfers between devices, per_device(): lax.psum_scatter(partial_one, 'head', scatter_dimension=1, tiled=True)  62.3 us
    reduce_scatter x1, waiting for transfers between devices, per_device(): lax.psum_scatter(row_terms, 'head', scatter_dimension=1, tiled=True)  60.1 us
    reduce_scatter x1, waiting for transfers between devices, per_device(): lax.psum_scatter(grad_query_two, 'head', scatter_dimension=1, tiled=True)  59.2 us
    reduce_scatter x1, waiting for transfers between devices, per_device(): lax.psum_scatter(partial_two, 'head', scatter_dimension=1, tiled=True)  58 us
    reduce_scatter x1, waiting for transfers between devices, per_device(): lax.psum_scatter(memory_partial, 'head', scatter_dimension=1, tiled=True)  51.9 us
    unnamed x170, local copies, waits for them, and re-layouts  44 us
  transfers between devices with their start and end apart: 20, of which 16 were waited for; matrix products, arithmetic and copies ran while one was open for 17% of the time, Pallas kernels for 0%

commit v1 on v0

v1 whole, which is shorter than its diff:
```python
import functools
import math

import jax
import jax.numpy as jnp
from jax import lax
from jax.experimental import pallas as pl
from jax.experimental.pallas import tpu as pltpu
from jax.sharding import PartitionSpec as P

NB = 32
MAX_DIST = 128
NEG = -1e30
VMEM_LIMIT = 56 * 1024 * 1024
F32 = jnp.float32
BF16 = jnp.bfloat16

highest = lax.Precision.HIGHEST


def bucket_edges(num_buckets, max_distance):
    exact_part = num_buckets // 2
    edge_list = []
    for target in range(1, num_buckets - exact_part):
        distance = exact_part
        while (
            math.floor(
                math.log(distance / exact_part)
                / math.log(max_distance / exact_part)
                * (num_buckets - exact_part)
            )
            < target
        ):
            distance += 1
        edge_list.append(distance)
    return edge_list


def bucket_of(distance, num_buckets, max_distance):
    exact_part = num_buckets // 2
    counted = jnp.zeros(distance.shape, jnp.int32)
    for edge_value in bucket_edges(num_buckets, max_distance):
        counted = counted + (distance >= edge_value).astype(jnp.int32)
    return jnp.where(distance < exact_part, distance, exact_part + counted).astype(jnp.int32)


def near_onehot(block):
    distance = block - jnp.arange(2 * block)
    distance = jnp.where(distance < 0, 2 * MAX_DIST, distance)
    return (
        bucket_of(distance, NB, MAX_DIST)[:, None] == jnp.arange(NB)[None, :]
    ).astype(F32)


def nn(a, b):
    return lax.dot_general(a, b, (((1,), (0,)), ((), ())), preferred_element_type=F32)


def nt(a, b):
    return lax.dot_general(a, b, (((1,), (1,)), ((), ())), preferred_element_type=F32)


def tn(a, b):
    return lax.dot_general(a, b, (((0,), (0,)), ((), ())), preferred_element_type=F32)


def rms(v):
    return lax.rsqrt(jnp.mean(v * v, axis=-1, keepdims=True) + 1e-06)


def norm_grads(y, gain, e):
    r = rms(y)
    xhat = y * r
    eg = e * gain
    dy = r * (eg - xhat * jnp.mean(eg * xhat, axis=-1, keepdims=True))
    return dy, jnp.sum(e * xhat, axis=0, keepdims=True)


def padded(v, width):
    extra = width - v.shape[1]
    if extra == 0:
        return v
    return jnp.concatenate([v, jnp.zeros((v.shape[0], extra), v.dtype)], axis=1)


def vmem():
    return pl.BlockSpec(memory_space=pltpu.VMEM)


def smem():
    return pl.BlockSpec(memory_space=pltpu.SMEM)


def params():
    return pltpu.CompilerParams(vmem_limit_bytes=VMEM_LIMIT)


def sds(shape, dtype):
    return jax.ShapeDtypeStruct(shape, dtype)


def bias_kernel(me_ref, w_ref, b_ref, ext_ref):
    heads, block, full = b_ref.shape
    me = me_ref[0]
    start = pl.multiple_of(me * block, block)
    width = 2 * block
    row_i = lax.broadcasted_iota(jnp.int32, (block, width), 0)
    col_i = lax.broadcasted_iota(jnp.int32, (block, width), 1)
    masked = (col_i - row_i) > block
    far = lax.broadcasted_iota(jnp.int32, ext_ref.shape, 1) < start

    def body(head, carry):
        row = w_ref[pl.ds(head, 1), :]
        tile = pltpu.roll(
            jnp.broadcast_to(row, (block, width)), 0, 1, stride=1, stride_axis=0
        )
        ext_ref[...] = jnp.where(far, row[:, width - 1 : width], NEG)
        ext_ref[:, pl.ds(start, width)] = jnp.where(masked, NEG, tile)
        b_ref[head] = ext_ref[:, block:]
        return carry

    lax.fori_loop(0, heads, body, 0)


def bias_tiles(me, table, block, full):
    heads = table.shape[0]
    return pl.pallas_call(
        bias_kernel,
        out_shape=sds((heads, block, full), F32),
        in_specs=[smem(), vmem()],
        out_specs=vmem(),
        scratch_shapes=[pltpu.VMEM((block, full + block), F32)],
        compiler_params=params(),
        name="bias_tiles",
    )(me, table)


def lane_groups(width, group, size):
    lane = lax.broadcasted_iota(jnp.int32, (1, width), 1)
    return [(lane // size) == a for a in range(group)]


def stack_heads(win, lanes):
    return jnp.concatenate([jnp.where(m, win, jnp.zeros_like(win)) for m in lanes], axis=0)


def join_heads(tall, lanes, rows):
    total = jnp.where(lanes[0], tall[:rows], 0.0)
    for a in range(1, len(lanes)):
        total = total + jnp.where(lanes[a], tall[a * rows : (a + 1) * rows], 0.0)
    return total


def forward_kernel(
    biased, group, size, len_ref, nq_ref, nk_ref, res_ref, wq_ref, wkv_ref, wo_ref, gain_ref, *rest
):
    if biased:
        b_ref, *rest = rest
    q_ref, k_ref, v_ref, c_ref, lse_ref, y_ref, n_ref = rest
    shards, rows, pw = q_ref.shape
    seqs = len_ref.shape[0]
    block = rows // seqs
    full = k_ref.shape[1] // seqs
    win = group * size
    lanes = lane_groups(pw, group, size)
    lane128 = lax.broadcasted_iota(jnp.int32, (block, 128), 1)
    key = lax.broadcasted_iota(jnp.int32, (1, full), 1)

    def body(h, carry):
        q_ref[h] = padded(nn(nq_ref[...], wq_ref[h]).astype(BF16), pw)
        kv = nn(nk_ref[...], wkv_ref[h]).astype(BF16)
        k_ref[h] = padded(kv[:, :win], pw)
        v_ref[h] = padded(kv[:, win:], pw)
        for s in range(seqs):
            kw = k_ref[h, s * full : (s + 1) * full, :]
            vw = v_ref[h, s * full : (s + 1) * full, :]
            qcat = stack_heads(q_ref[h, s * block : (s + 1) * block, :], lanes)
            sc = nt(qcat, kw)
            if biased:
                sc = sc + b_ref[pl.ds(h * group, group)].reshape(group * block, full)
            sc = jnp.where(key < len_ref[s], sc, NEG)
            top = jnp.max(sc, axis=-1, keepdims=True)
            e = jnp.exp(sc - top)
            total = jnp.sum(e, axis=-1, keepdims=True)
            p = (e * (1.0 / total)).astype(BF16)
            c = join_heads(nn(p, vw), lanes, block)
            c_ref[h, s * block : (s + 1) * block, :] = c.astype(BF16)
            lse = top + jnp.log(total)
            tile = jnp.zeros((block, 128), F32)
            for a in range(group):
                tile = jnp.where(lane128 == a, lse[a * block : (a + 1) * block], tile)
            lse_ref[h, s] = tile
        return carry

    lax.fori_loop(0, shards, body, 0)
    joined = jnp.concatenate([c_ref[h][:, :win] for h in range(shards)], axis=1)
    y = res_ref[...].astype(F32) + nn(joined, wo_ref[...])
    y_ref[...] = y
    n_ref[...] = (y * rms(y) * gain_ref[...]).astype(BF16)


def attend_forward(lens, nq, nk, res, wq, wkv, wo, gain, bias, group, size):
    rows, width = nq.shape
    shards = wq.shape[0]
    pw = -(-group * size // 128) * 128
    seqs = lens.shape[0]
    args = [lens, nq, nk, res, wq, wkv, wo, gain] + ([bias] if bias is not None else [])
    keys = nk.shape[0]
    flops = 2 * (rows + 2 * keys + rows) * width * width + 4 * rows * keys * width
    return pl.pallas_call(
        functools.partial(forward_kernel, bias is not None, group, size),
        out_shape=[
            sds((shards, rows, pw), BF16),
            sds((shards, keys, pw), BF16),
            sds((shards, keys, pw), BF16),
            sds((shards, rows, pw), BF16),
            sds((shards, seqs, rows // seqs, 128), F32),
            sds((rows, width), F32),
            sds((rows, width), BF16),
        ],
        in_specs=[smem()] + [vmem()] * (len(args) - 1),
        out_specs=[vmem()] * 7,
        compiler_params=params(),
        cost_estimate=pl.CostEstimate(
            flops=flops, bytes_accessed=16 << 20, transcendentals=rows * keys * 6
        ),
        name="attend_forward",
    )(*args)


def backward_kernel(
    biased,
    group,
    size,
    len_ref,
    me_ref,
    nq_ref,
    nk_ref,
    q_ref,
    k_ref,
    v_ref,
    c_ref,
    lse_ref,
    wq_ref,
    wkv_ref,
    wo_ref,
    dy_ref,
    gain_ref,
    *rest,
):
    if biased:
        b_ref, part_ref, gg_ref, w_ref, diag_ref, dc_ref, dq_ref, dkv_ref, acc_ref, nqt_ref, nkt_ref, dat_ref, sum_ref, ext_ref = rest
    else:
        y_ref, part_ref, gg_ref, w_ref, dprev_ref, dc_ref, dq_ref, dkv_ref, acc_ref, nqt_ref, nkt_ref, dat_ref = rest
    shards, rows, pw = q_ref.shape
    seqs = len_ref.shape[0]
    block = rows // seqs
    full = k_ref.shape[1] // seqs
    win = group * size
    lanes = lane_groups(pw, group, size)
    key = lax.broadcasted_iota(jnp.int32, (1, full), 1)
    me = me_ref[0]

    da = dy_ref[...].astype(BF16)
    nqt_ref[...] = nq_ref[...].T
    nkt_ref[...] = nk_ref[...].T
    dat_ref[...] = da.T
    if biased:
        ext_ref[:, :block] = jnp.zeros((block, block), F32)
        start = pl.multiple_of(me * block, block)
        far = lax.broadcasted_iota(jnp.int32, ext_ref.shape, 1) < start
        row8 = lax.broadcasted_iota(jnp.int32, (8, 2 * block), 0)
        lane_near = lax.broadcasted_iota(jnp.int32, (1, 2 * block), 1)

    def body(h, carry):
        wo_h = wo_ref[pl.ds(pl.multiple_of(h * win, size), win), :]
        dc_ref[...] = padded(nt(da, wo_h).astype(BF16), pw)
        for s in range(seqs):
            kw = k_ref[h, s * full : (s + 1) * full, :]
            vw = v_ref[h, s * full : (s + 1) * full, :]
            qcat = stack_heads(q_ref[h, s * block : (s + 1) * block, :], lanes)
            dcat = stack_heads(dc_ref[s * block : (s + 1) * block, :], lanes)
            sc = nt(qcat, kw)
            if biased:
                sc = sc + b_ref[pl.ds(h * group, group)].reshape(group * block, full)
            sc = jnp.where(key < len_ref[s], sc, NEG)
            lse_tile = lse_ref[h, s]
            lse = jnp.concatenate([lse_tile[:, a : a + 1] for a in range(group)], axis=0)
            p = jnp.exp(sc - lse)
            dp = nt(dcat, vw)
            ds = p * (dp - jnp.sum(p * dp, axis=-1, keepdims=True))
            ds = ds.astype(BF16)
            pb = p.astype(BF16)
            if biased:
                if s == 0:
                    sum_ref[...] = ds.astype(F32)
                else:
                    sum_ref[...] += ds.astype(F32)
            dq = join_heads(nn(ds, kw), lanes, block)
            dq_ref[s * block : (s + 1) * block, :] = dq.astype(BF16)
            dk = tn(ds, qcat).astype(BF16)
            dv = tn(pb, dcat).astype(BF16)
            dkv_ref[s * full : (s + 1) * full, :] = jnp.concatenate(
                [dk[:, :win], dv[:, :win]], axis=1
            )
        if biased:
            for a in range(group):
                ext_ref[:, block:] = sum_ref[a * block : (a + 1) * block, :]
                far_sum = jnp.sum(jnp.where(far, ext_ref[...], 0.0))
                fold = ext_ref[:, pl.ds(start, 2 * block)]
                half = block // 2
                while half >= 8:
                    fold = fold[:half] + pltpu.roll(fold[half:], 2 * block - half, 1)
                    half //= 2
                for bit in (4, 2, 1):
                    fold = jnp.where(
                        (row8 & bit) != 0, pltpu.roll(fold, 2 * block - bit, 1), fold
                    )
                line = jnp.sum(fold, axis=0, keepdims=True)
                line = line + jnp.where(lane_near == 2 * block - 1, far_sum, 0.0)
                diag_ref[pl.ds(h * group + a, 1), :] = line
        dkv = dkv_ref[...]
        dq_h = dq_ref[...][:, :win]
        kv_term = nt(dkv, wkv_ref[h])
        q_term = nt(dq_h, wq_ref[h])
        w_ref[h] = jnp.concatenate(
            [
                nn(nkt_ref[...], dkv).astype(BF16),
                nn(nqt_ref[...], dq_h).astype(BF16),
                nn(dat_ref[...], c_ref[h][:, :win]).astype(BF16),
            ],
            axis=1,
        )

        @pl.when(h == 0)
        def _():
            acc_ref[: seqs * full, :] = kv_term
            acc_ref[seqs * full :, :] = q_term

        @pl.when(h != 0)
        def _():
            acc_ref[: seqs * full, :] += kv_term
            acc_ref[seqs * full :, :] += q_term

        return carry

    lax.fori_loop(0, shards, body, 0)
    if biased:
        for s in range(seqs):
            own = pl.ds(pl.multiple_of(s * full + me * block, block), block)
            acc_ref[own, :] += acc_ref[seqs * full + s * block : seqs * full + (s + 1) * block, :]
        total = acc_ref[: seqs * full, :]
        part_ref[...] = total.astype(BF16)
        gg_ref[...] = (
            jnp.sum(total * nk_ref[...].astype(F32), axis=0, keepdims=True) / gain_ref[...]
        )
    else:
        part_ref[...] = acc_ref[: seqs * full, :].astype(BF16)
        dy, gg = norm_grads(y_ref[...], gain_ref[...], acc_ref[seqs * full :, :])
        dprev_ref[...] = dy_ref[...] + dy
        gg_ref[...] = gg


def attend_backward(lens, me, nq, nk, saved, wq, wkv, wo, dy, gain, extra, biased, group, size):
    q, k, v, c, lse = saved
    rows, width = nq.shape
    shards, keys, pw = k.shape
    block = rows // lens.shape[0]
    full = keys // lens.shape[0]
    win = group * size
    args = [lens, me, nq, nk, q, k, v, c, lse, wq, wkv, wo, dy, gain, extra]
    out_shape = [
        sds((keys, width), BF16),
        sds((1, width), F32),
        sds((shards, width, 4 * win), BF16),
        sds((shards * group, 2 * block), F32) if biased else sds((rows, width), F32),
    ]
    scratch = [
        pltpu.VMEM((rows, pw), BF16),
        pltpu.VMEM((rows, pw), BF16),
        pltpu.VMEM((keys, 2 * win), BF16),
        pltpu.VMEM((keys + rows, width), F32),
        pltpu.VMEM((width, rows), BF16),
        pltpu.VMEM((width, keys), BF16),
        pltpu.VMEM((width, rows), BF16),
    ]
    if biased:
        scratch += [
            pltpu.VMEM((group * block, full), F32),
            pltpu.VMEM((block, full + block), F32),
        ]
    flops = 4 * (rows + 2 * keys + rows) * width * width + 10 * rows * full * width
    return pl.pallas_call(
        functools.partial(backward_kernel, biased, group, size),
        out_shape=out_shape,
        in_specs=[smem(), smem()] + [vmem()] * (len(args) - 2),
        out_specs=[vmem()] * 4,
        scratch_shapes=scratch,
        compiler_params=params(),
        cost_estimate=pl.CostEstimate(
            flops=flops, bytes_accessed=24 << 20, transcendentals=rows * full * 12
        ),
        name="attend_backward",
    )(*args)


def feed_kernel(
    y_ref, n_ref, cot_ref, win_ref, wout_ref, gain_ref, out_ref, dy_ref, gg_ref, w_ref,
    acc_ref, dn_ref, nt_ref, ct_ref,
):
    step = pl.program_id(0)
    part = wout_ref.shape[0]

    @pl.when(step == 0)
    def _():
        nt_ref[...] = n_ref[...].T
        ct_ref[...] = cot_ref[...].T
        acc_ref[...] = y_ref[...]
        dn_ref[...] = jnp.zeros_like(dn_ref)

    n = n_ref[...]
    cot = cot_ref[...]
    g = nn(n, win_ref[0])
    u = nn(n, win_ref[1])
    dh = nt(cot, wout_ref[...])
    scale = math.sqrt(2.0 / math.pi)
    square = g * g
    t = jnp.tanh(scale * (g + 0.044715 * square * g))
    half = 0.5 * (1.0 + t)
    gelu = g * half
    hid = (gelu * u).astype(BF16)
    slope = half + 0.5 * g * (1.0 - t * t) * (scale * (1.0 + 3 * 0.044715 * square))
    dg = (dh * u * slope).astype(BF16)
    du = (dh * gelu).astype(BF16)
    acc_ref[...] += nn(hid, wout_ref[...])
    dn_ref[...] += nt(dg, win_ref[0]) + nt(du, win_ref[1])
    w_ref[0, :, :part] = nn(nt_ref[...], dg).astype(BF16)
    w_ref[0, :, part : 2 * part] = nn(nt_ref[...], du).astype(BF16)
    w_ref[0, :, 2 * part :] = nn(ct_ref[...], hid).astype(BF16)

    @pl.when(step == pl.num_programs(0) - 1)
    def _():
        out_ref[...] = acc_ref[...].astype(BF16)
        dy, gg = norm_grads(y_ref[...], gain_ref[...], dn_ref[...])
        dy_ref[...] = cot_ref[...].astype(F32) + dy
        gg_ref[...] = gg


def feed(y, n, cot, w_in, w_out, gain, shards):
    rows, width = y.shape
    hidden = w_out.shape[0]
    part = hidden // shards
    fixed = lambda shape: pl.BlockSpec(shape, lambda j: (0,) * len(shape))
    return pl.pallas_call(
        feed_kernel,
        grid=(shards,),
        out_shape=[
            sds((rows, width), BF16),
            sds((rows, width), F32),
            sds((1, width), F32),
            sds((shards, width, 3 * part), BF16),
        ],
        in_specs=[
            fixed((rows, width)),
            fixed((rows, width)),
            fixed((rows, width)),
            pl.BlockSpec((2, width, part), lambda j: (0, 0, j)),
            pl.BlockSpec((part, width), lambda j: (j, 0)),
            fixed((1, width)),
        ],
        out_specs=[
            fixed((rows, width)),
            fixed((rows, width)),
            fixed((1, width)),
            pl.BlockSpec((1, width, 3 * part), lambda j: (j, 0, 0)),
        ],
        scratch_shapes=[
            pltpu.VMEM((rows, width), F32),
            pltpu.VMEM((rows, width), F32),
            pltpu.VMEM((width, rows), BF16),
            pltpu.VMEM((width, rows), BF16),
        ],
        compiler_params=params(),
        cost_estimate=pl.CostEstimate(
            flops=18 * rows * width * hidden, bytes_accessed=24 << 20, transcendentals=rows * hidden
        ),
        name="feed",
    )(y, n, cot, w_in, w_out, gain)


def per_device(
    layer_input,
    memory,
    dec_lengths,
    enc_lengths,
    self_gain,
    self_query,
    self_key_value,
    self_out,
    rel_bias,
    cross_gain,
    cross_query,
    cross_key_value,
    cross_out,
    feed_gain,
    feed_in,
    feed_out,
    out_cotangent,
):
    shards = lax.axis_size("head")
    me = lax.axis_index("head").astype(jnp.int32).reshape(1)
    batch_count = lax.axis_size("batch")
    batch_index = lax.axis_index("batch")
    seqs, block, width = layer_input.shape
    group = rel_bias.shape[1]
    size = self_query.shape[1] // group
    win = group * size
    full = block * shards
    enc_full = memory.shape[1] * shards
    rows = seqs * block
    slice_width = width // batch_count
    part = feed_in.shape[2] // shards
    sg, cg, fg = (g.astype(F32).reshape(1, width) for g in (self_gain, cross_gain, feed_gain))

    x = layer_input.reshape(rows, width)
    x32 = x.astype(F32)
    n1 = (x32 * rms(x32) * sg).astype(BF16)
    n1_all = lax.all_gather(n1.reshape(seqs, block, width), "head", axis=1, tiled=True)
    n1_all = n1_all.reshape(seqs * full, width)

    def take(weight, axis):
        length = weight.shape[axis] // batch_count
        return lax.dynamic_slice_in_dim(weight, batch_index * length, length, axis)

    projections = jnp.concatenate(
        [take(self_query, 0), take(self_key_value[0], 0), take(self_key_value[1], 0),
         take(cross_query, 0), take(cross_key_value[0], 0), take(cross_key_value[1], 0)], axis=1
    )
    projections = lax.all_gather(projections, ("head", "batch"), axis=0, tiled=True)
    projections = projections.reshape(shards, width, 6 * win)
    wq1, wkv1 = projections[:, :, :win], projections[:, :, win : 3 * win]
    wq2, wkv2 = projections[:, :, 3 * win : 4 * win], projections[:, :, 4 * win :]
    outs = jnp.concatenate([take(self_out, 1), take(cross_out, 1)], axis=1)
    outs = lax.all_gather(outs, "head", axis=0, tiled=True)
    outs = lax.all_gather(outs.reshape(width, 2, slice_width), "batch", axis=2, tiled=True)
    wo1, wo2 = outs[:, 0], outs[:, 1]
    table = lax.all_gather(rel_bias.T, "head", axis=0, tiled=True).astype(F32)
    onehot = near_onehot(block)
    near = jnp.einsum("hb,tb->ht", table, onehot, precision=highest)
    bias = bias_tiles(me, near, block, full)
    memory_all = lax.all_gather(memory, "head", axis=1, tiled=True).reshape(seqs * enc_full, width)

    *saved1, y1, n2 = attend_forward(
        dec_lengths, n1, n1_all, x, wq1, wkv1, wo1, cg, bias, group, size
    )
    *saved2, y2, n3 = attend_forward(
        enc_lengths, n2, memory_all, y1, wq2, wkv2, wo2, fg, None, group, size
    )
    result, dy2, gain3, feed_w = feed(
        y2, n3, out_cotangent.reshape(rows, width), feed_in, feed_out, fg, shards
    )
    memory_part, gain2, cross_w, dy1 = attend_backward(
        enc_lengths, me, n2, memory_all, saved2, wq2, wkv2, wo2, dy2, cg, y1, False, group, size
    )
    input_part, gain1, self_w, diag = attend_backward(
        dec_lengths, me, n1, n1_all, saved1, wq1, wkv1, wo1, dy1, sg, bias, True, group, size
    )

    feed_w = lax.psum_scatter(
        feed_w.reshape(shards * width, 3 * part), ("head", "batch"), scatter_dimension=0, tiled=True
    ).astype(F32)
    memory_grad = lax.psum_scatter(
        memory_part.reshape(seqs, enc_full, width), "head", scatter_dimension=1, tiled=True
    ).astype(F32)
    dn1 = lax.psum_scatter(
        input_part.reshape(seqs, full, width), "head", scatter_dimension=1, tiled=True
    ).astype(F32)
    pair_w = jnp.concatenate(
        [self_w.reshape(shards * width, 4 * win), cross_w.reshape(shards * width, 4 * win)], axis=1
    )
    pair_w = lax.psum_scatter(
        pair_w, ("head", "batch"), scatter_dimension=0, tiled=True
    ).astype(F32)
    dx, _ = norm_grads(x32, sg, dn1.reshape(rows, width))
    input_grad = (dy1 + dx).reshape(seqs, block, width)
    table_grad = jnp.einsum("tb,ht->bh", onehot, diag, precision=highest)
    gains, table_grad = lax.psum(
        (jnp.concatenate([gain1, gain2, gain3], axis=0), table_grad), ("batch", "head")
    )
    table_grad = lax.dynamic_slice_in_dim(table_grad, me[0] * group, group, 1)

    def split(w):
        kv = jnp.stack([w[:, :win], w[:, win : 2 * win]])
        return w[:, 2 * win : 3 * win], kv, w[:, 3 * win :].T

    self_q, self_kv, self_o = split(pair_w[:, : 4 * win])
    cross_q, cross_kv, cross_o = split(pair_w[:, 4 * win :])
    return (
        result.reshape(seqs, block, width),
        input_grad,
        memory_grad,
        gains[0],
        self_q,
        self_kv,
        self_o,
        table_grad,
        gains[1],
        cross_q,
        cross_kv,
        cross_o,
        gains[2],
        jnp.stack([feed_w[:, :part], feed_w[:, part : 2 * part]]),
        feed_w[:, 2 * part :].T,
    )


def solution(mesh):
    return jax.shard_map(
        per_device,
        mesh=mesh,
        in_specs=(
            P("batch", "head", None),
            P("batch", "head", None),
            P("batch"),
            P("batch"),
            P(),
            P(None, "head"),
            P(None, None, "head"),
            P("head", None),
            P(None, "head"),
            P(),
            P(None, "head"),
            P(None, None, "head"),
            P("head", None),
            P(),
            P(),
            P(),
            P("batch", "head", None),
        ),
        out_specs=(
            P("batch", "head", None),
            P("batch", "head", None),
            P("batch", "head", None),
            P(),
            P("batch", "head"),
            P(None, "batch", "head"),
            P("head", "batch"),
            P(None, "head"),
            P(),
            P("batch", "head"),
            P(None, "batch", "head"),
            P("head", "batch"),
            P(),
            P(None, "batch", "head"),
            P("head", "batch"),
        ),
        check_vma=False,
    )
```

time: 1500 us -> 631 us (0.42)
  waiting for transfers between devices: 1110 us -> 355 us
  matrix products: 111 us -> 1.06 us
  Pallas kernels: 0 us -> 103 us
  local copies, waits for them, and re-layouts: 168 us -> 69.6 us
  other arithmetic: 46.8 us -> 18.6 us
  blocking collectives: 40.9 us -> 67 us
    reduce_scatter x12 -> x3, waiting for transfers between devices: 527 us -> 140 us  [the longest x1 140 us: per_device(): lax.psum_scatter(feed_w.reshape(shards * width, 3 * part), ('head', 'batc...]
    unnamed x23 -> x9, waiting for transfers between devices: 477 us -> 101 us
    dot_general x40 -> x2, matrix products: 111 us -> 1.06 us  [the longest x1 0.83 us: per_device(): near = jnp.einsum('hb,tb->ht', table, onehot, precision=highest)]
    pallas_call x0 -> x6, Pallas kernels: none -> 103 us  [the longest x2 56.1 us: attend_backward(): pl.pallas_call(functools.partial(backward_kernel, biased, group, size), o...]
    rev x3 -> x0, local copies, waits for them, and re-layouts: 54.2 us -> none  [the longest x2 29.6 us: bias_matrix(): return jnp.flip(spread[:, :, :length], axis=2)]
    all_gather x0 -> x2, blocking collectives: none -> 27.9 us  [the longest x1 16.2 us: per_device(): outs = lax.all_gather(outs, 'head', axis=0, tiled=True)]
    all_gather x4 -> x3, waiting for transfers between devices: 67.8 us -> 91.6 us  [the longest x1 57.3 us: per_device(): lax.all_gather(projections, ('head', 'batch'), axis=0, tiled=True)]
    reduce_sum x9 -> x2, other arithmetic: 22.3 us -> 1.44 us  [the longest x1 1.28 us: norm_grads(): dy = r * (eg - xhat * jnp.mean(eg * xhat, axis=-1, keepdims=True))]
  transfers between devices with their start and end apart: 20 -> 8, of which waited for: 16 -> 6; matrix products, arithmetic and copies ran while one was open for 17% -> 13% of each run, Pallas kernels for 0% -> 8%
where the time goes in v1:
time: 631 us; the launch traced here: 629 us
  waiting for transfers between devices  355 us (56%)
  Pallas kernels  103 us (16%)
  local copies, waits for them, and re-layouts  69.6 us (11%)
  blocking collectives  67 us (11%)
  other arithmetic  18.6 us (3%)
  between operations  14.5 us (2%)
    reduce_scatter x1, waiting for transfers between devices, per_device(): lax.psum_scatter(feed_w.reshape(shards * width, 3 * part), ('head', 'batc...  140 us
    unnamed x9, waiting for transfers between devices  101 us
    all_gather x1, waiting for transfers between devices, per_device(): lax.all_gather(projections, ('head', 'batch'), axis=0, tiled=True)  57.3 us
    pallas_call x2, Pallas kernels, attend_backward(): pl.pallas_call(functools.partial(backward_kernel, biased, group, size), o...  56.1 us
    psum x1, blocking collectives, per_device(): lax.psum((jnp.concatenate([gain1, gain2, gain3], axis=0), table_grad), ('...  39.1 us
    pallas_call x2, Pallas kernels, attend_forward(): pl.pallas_call(functools.partial(forward_kernel, bias is not None, group,...  28.7 us
    unnamed x37, local copies, waits for them, and re-layouts  28 us
    all_gather x1, waiting for transfers between devices, per_device(): lax.all_gather(n1.reshape(seqs, block, width), 'head', axis=1, tiled=True)  26.9 us
  transfers between devices with their start and end apart: 8, of which 6 were waited for; matrix products, arithmetic and copies ran while one was open for 13% of the time, Pallas kernels for 8%

profile of v1, /device:TPU:0, one launch (start us, length us, event | category | flops | bytes accessed | tf_op | source)
XLA Modules:
  0.0 629.2 jit_solution(7039113707427503905)
XLA Ops:
  7.3 1.1 constant_dynamic-slice_fusion.1
  8.5 16.2 %all_gather.20 = bf16[768,192]{1,0:T(8,128)(2,1)S(1)} all-gather(bf16[192,192]{1,0:T(8,128)(2,1)S(1)} %pad_maximum_fusion.4), channel_id=1, replica_groups=mesh['batch'=8,'head'=4] {'head'}, dimensions={0}, use_global_device_ids=true | all-gather | bytes 368640 | tf_op jit(solution)/shard_map/all_gather | solution.py:544
  24.9 1.0 copy.56
  26.8 1.0 constant_dynamic-slice_fusion.5
  28.0 0.8 concatenate.12
  29.1 0.9 fusion.2
  30.7 11.7 %all-gather = bf16[4,3,32]{2,1,0:T(4,128)(2,1)S(1)} all-gather(bf16[1,3,32]{2,1,0:T(4,128)(2,1)S(1)} %bitcast.78), channel_id=1, replica_groups=mesh['batch'=8,'head'=4] {'head'}, dimensions={0}, use_global_device_ids=true | all-gather | bytes 960 | tf_op jit(solution)/shard_map/all_gather | solution.py:547
  42.4 0.8 convolution_bitcast_fusion.w_ref
  43.3 0.6 reshape.213.gain_ref
  44.4 4.2 bias_tiles.1.rest_0_
  48.7 0.9 multiply_convert_fusion.nq_ref
  49.6 7.5 %all-gather.10.cloned.1.call-done = bf16[768,2,768]{0,1,2:T(2,128)(2,1)} async-done(((bf16[768,2,96]{0,1,2:T(2,128)(2,1)}), bf16[768,2,768]{0,1,2:T(2,128)(2,1)}) %all-gather.10.cloned.1.call-update) | async-done | bytes 2359312 | tf_op jit(solution)/shard_map/all_gather | solution.py:545
  57.0 7.8 %fusion.29 = (bf16[768,1,768]{0,1,2:T(2,128)(2,1)S(1)}, bf16[768,1,768]{0,1,2:T(2,128)(2,1)}) fusion(bf16[768,2,768]{0,1,2:T(2,128)(2,1)} %all-gather.10.cloned.1.call-done), kind=kLoop, calls=%fused_computation.82 | loop fusion | bytes 4718592 | tf_op jit(solution)/shard_map/slice | solution.py:546
  64.9 6.4 %copy.69 = bf16[768,1,768]{2,0,1:T(8,128)(2,1)} copy(bf16[768,1,768]{0,1,2:T(2,128)(2,1)} %get-tuple-element.122) | data formatting | bytes 2359296
  71.3 4.5 copy.70
  75.8 57.3 %all-gather.8.cloned.1.call-done = bf16[3072,1152]{1,0:T(8,128)(2,1)} async-done(((bf16[96,1152]{1,0:T(8,128)(2,1)}), bf16[3072,1152]{1,0:T(8,128)(2,1)}) %all-gather.8.cloned.1.call-update) | async-done | bytes 7077904 | tf_op jit(solution)/shard_map/all_gather | solution.py:539
  133.0 4.6 fusion.28
  137.7 6.3 %fusion.27 = (bf16[4,768,384]{2,1,0:T(8,128)(2,1)}, bf16[4,768,384]{2,1,0:T(8,128)(2,1)}) fusion(bf16[4,768,1152]{2,1,0:T(8,128)(2,1)} %bitcast.63), kind=kLoop, calls=%fused_computation.80 | loop fusion | bytes 9437184 | tf_op jit(solution)/shard_map/slice | solution.py:542
  144.0 26.9 %all-gather.6.cloned.1.call-done = bf16[2,512,768]{2,1,0:T(8,128)(2,1)} async-done(((bf16[2,128,768]{2,1,0:T(8,128)(2,1)}), bf16[2,512,768]{2,1,0:T(8,128)(2,1)}) %all-gather.6.cloned.1.call-update) | async-done | bytes 1572880 | tf_op jit(solution)/shard_map/all_gather | solution.py:528
  170.9 14.7 %attend_forward.2 = (bf16[4,256,256]{2,1,0:T(8,128)(2,1)}, bf16[4,1024,256]{2,1,0:T(8,128)(2,1)}, bf16[4,1024,256]{2,1,0:T(8,128)(2,1)}, bf16[4,256,256]{2,1,0:T...) custom-call(s32[2]{0:T(128)} %len_ref.7, ...), custom_call_target="tpu_custom_call" | custom-call | flops 3825205248 | bytes 16777216 | tf_op jit(solution)/shard_map/attend_forward/pallas_call | solution.py:210
  185.5 22.7 %all-gather.12.cloned.1.call-done = bf16[2,512,768]{2,1,0:T(8,128)(2,1)} async-done(((bf16[2,128,768]{2,1,0:T(8,128)(2,1)}), bf16[2,512,768]{2,1,0:T(8,128)(2,1)}) %all-gather.12.cloned.1.call-update) | async-done | bytes 1572880 | tf_op jit(solution)/shard_map/all_gather | solution.py:551
  208.3 14.0 %attend_forward.3 = (bf16[4,256,256]{2,1,0:T(8,128)(2,1)}, bf16[4,1024,256]{2,1,0:T(8,128)(2,1)}, bf16[4,1024,256]{2,1,0:T(8,128)(2,1)}, bf16[4,256,256]{2,1,0:T...) custom-call(s32[2]{0:T(128)} %len_ref.6, ...), custom_call_target="tpu_custom_call" | custom-call | flops 3825205248 | bytes 16777216 | tf_op jit(solution)/shard_map/attend_forward/pallas_call | solution.py:210
  222.3 13.8 %feed.1 = (bf16[256,768]{1,0:T(8,128)(2,1)}, f32[256,768]{1,0:T(8,128)}, f32[1,768]{1,0:T(1,128)}, bf16[4,768,1536]{2,1,0:T(8,128)(2,1)}) custom-call(f32[256,768]{1,0:T(8,128)} %get-tuple-element.43.y_ref, bf16[256,768]{1,0:T(8,128)(2,1)} %get-tuple-element.44.n_ref, bf16[256,768]{1,0:T(8,128)(2,1)} %bitcast.83, bf16[2,768,2048]{2,1,0:T(8,128)(2,1)} %win_ref.1, ...), custom_call_target="tpu_custom_call" | custom-call | flops 7247757312 | bytes 25165824 | tf_op jit(solution)/shard_map/feed/pallas_call | solution.py:454
  236.1 27.1 %attend_backward.2 = (bf16[1024,768]{1,0:T(8,128)(2,1)}, f32[1,768]{1,0:T(1,128)}, bf16[4,768,768]{2,1,0:T(8,128)(2,1)}, f32[256,768]{1,0:T(8,128)}) custom-call(s32[2]{0:T(128)} %len_ref.6, s32[1]{0:T(128)} %bitcast.10.me_ref, bf16[256,768]{1,0:T(8,128)(2,1)} %get-tuple-element.41.nq_ref, bf16[1024,768]{1,0:T(8,128)(2,1)} %bitcast.82, ...), custom_call_target="tpu_custom_call" | custom-call | flops 7046430720 | bytes 25165824 | tf_op jit(solution)/shard_map/attend_backward/pallas_call | solution.py:393
  263.3 0.6 reshape.204.gain_ref
  263.9 29.0 %attend_backward.3 = (bf16[1024,768]{1,0:T(8,128)(2,1)}, f32[1,768]{1,0:T(1,128)}, bf16[4,768,768]{2,1,0:T(8,128)(2,1)}, f32[12,256]{1,0:T(8,128)}) custom-call(s32[2]{0:T(128)} %len_ref.7, s32[1]{0:T(128)} %bitcast.10.me_ref, bf16[256,768]{1,0:T(8,128)(2,1)} %multiply_convert_fusion.nq_ref, bf16[1024,768]{1,0:T(8,128)(2,1)} %bitcast.80, ...), custom_call_target="tpu_custom_call" | custom-call | flops 7046430720 | bytes 25165824 | tf_op jit(solution)/shard_map/attend_backward/pallas_call | solution.py:393
  293.0 6.8 %copy.59 = bf16[3072,768]{0,1:T(8,128)(2,1)} copy(bf16[3072,768]{1,0:T(8,128)(2,1)} %bitcast.65) | data formatting | bytes 9437184 | tf_op jit(solution)/shard_map/reshape | solution.py:579
  299.7 6.8 %copy.60 = bf16[3072,768]{0,1:T(8,128)(2,1)} copy(bf16[3072,768]{1,0:T(8,128)(2,1)} %bitcast.64) | data formatting | bytes 9437184 | tf_op jit(solution)/shard_map/reshape | solution.py:579
  306.5 9.3 %pad_maximum_fusion = bf16[3072,1536]{0,1:T(8,128)(2,1)} fusion(bf16[3072,768]{0,1:T(8,128)(2,1)} %copy.60, bf16[3072,768]{0,1:T(8,128)(2,1)} %copy.59), kind=kLoop, calls=%fused_computation | loop fusion | flops 18874368 | bytes 18874368 | tf_op jit(solution)/shard_map/concatenate | solution.py:578
  315.8 12.6 %copy.65 = bf16[3072,1536]{1,0:T(8,128)(2,1)} copy(bf16[3072,1536]{0,1:T(8,128)(2,1)} %pad_maximum_fusion) | data formatting | bytes 18874368
  328.5 0.6 reduce-scatter.11.cloned.1.call-update
  329.5 39.1 %all-reduce = (f32[3,768]{1,0:T(4,128)S(1)}, f32[32,12]{0,1:T(8,128)S(1)}) all-reduce(f32[3,768]{1,0:T(4,128)S(1)} %pad_maximum_fusion.5, f32[32,12]{0,1:T(8,128)S(1)} %fusion.8), channel_id=1, replica_groups=mesh['batch'=8,'head'=4] {'batch','head'}, use_global_device_ids=true, to_apply=%region_4.5 | all-reduce | flops 2688 | bytes 21504 | tf_op jit(solution)/shard_map/psum | solution.py:587
  368.5 0.6 constant_dynamic-slice_fusion
  369.1 0.6 slice_reduce_fusion
  369.7 1.9 convert_element_type.188
  371.7 1.3 fusion.3
  373.0 2.1 fusion.7
  375.1 99.3 %reduce-scatter.13.cloned.1.call-done = bf16[96,1536]{1,0:T(8,128)(2,1)} async-done(((bf16[3072,1536]{1,0:T(8,128)(2,1)}), bf16[96,1536]{1,0:T(8,128)(2,1)}) %reduce-scatter.13.cloned.1.call-update) | async-done | bytes 294928
  474.4 1.2 copy.66
  475.6 140.3 %reduce-scatter.11.cloned.1.call-done = bf16[96,1536]{1,0:T(8,128)(2,1)} async-done(((bf16[3072,1536]{1,0:T(8,128)(2,1)}), bf16[96,1536]{1,0:T(8,128)(2,1)}) %reduce-scatter.11.cloned.1.call-update) | async-done | bytes 294928 | tf_op jit(solution)/shard_map/reduce_scatter | solution.py:569
  616.0 1.0 convert_element_type.190
  617.0 0.7 slice_bitcast_fusion
  617.7 0.7 slice_bitcast_fusion.3
  618.5 0.8 copy.64
  619.3 0.8 copy.62
  620.1 0.7 copy.61
  620.8 0.7 copy.63
  621.5 0.8 pad_maximum_fusion.1
  (68 shorter events, 3.3 us)
Async XLA Ops:
  7.2 18.8 %copy-start.3 = (bf16[2,768,192]{1,2,0:T(8,128)(2,1)S(1)}, bf16[2,768,192]{1,2,0:T(8,128)(2,1)}, u32[]{:S(2)}) copy-start(bf16[2,768,192]{1,2,0:T(8,128)(2,1)} %param.23) | copy-start | bytes 1769476
  7.2 19.2 %copy-start.4 = (bf16[2,768,192]{1,2,0:T(8,128)(2,1)S(1)}, bf16[2,768,192]{1,2,0:T(8,128)(2,1)}, u32[]{:S(2)}) copy-start(bf16[2,768,192]{1,2,0:T(8,128)(2,1)} %param.28) | copy-start | bytes 1769476
  7.2 49.8 %all-gather.10.cloned.1.call-start = ((), (), s32[]{:S(2)}) async-start(), calls=%async_computation.6 | async-start | bytes 2654208 | tf_op jit(solution)/shard_map/all_gather | solution.py:545
  25.9 3.0 copy-start.5
  25.9 3.1 copy-start
  25.9 107.1 %all-gather.8.cloned.1.call-start = ((), (), s32[]{:S(2)}) async-start(), calls=%async_computation.5 | async-start | bytes 7299072 | tf_op jit(solution)/shard_map/all_gather | solution.py:539
  26.4 4.4 copy-start.11
  26.4 16.9 %copy-start.9 = (bf16[768]{0:T(1024)(128)(2,1)S(1)}, bf16[768]{0:T(1024)(128)(2,1)}, u32[]{:S(2)}) copy-start(bf16[768]{0:T(1024)(128)(2,1)} %param.26) | copy-start | bytes 4612
  26.4 17.4 %copy-start.10 = (bf16[768]{0:T(1024)(128)(2,1)S(1)}, bf16[768]{0:T(1024)(128)(2,1)}, u32[]{:S(2)}) copy-start(bf16[768]{0:T(1024)(128)(2,1)} %param.30) | copy-start | bytes 4612
  28.9 142.0 %all-gather.6.cloned.1.call-start = ((), (), s32[]{:S(2)}) async-start(), calls=%async_computation.4 | async-start | bytes 1966080 | tf_op jit(solution)/shard_map/all_gather | solution.py:528
  30.1 178.2 %all-gather.12.cloned.1.call-start = ((), (), s32[]{:S(2)}) async-start(), calls=%async_computation.7 | async-start | bytes 1966080 | tf_op jit(solution)/shard_map/all_gather | solution.py:551
  30.7 339.1 %reduce-scatter.9.cloned.1.call-start = ((), (), s32[]{:S(2)}) async-start(), calls=%async_computation.9 | async-start | bytes 1966080 | tf_op jit(solution)/shard_map/reduce_scatter | solution.py:572
  263.2 108.4 %reduce-scatter.7.cloned.1.call-start = ((), (), s32[]{:S(2)}) async-start(), calls=%async_computation.8 | async-start | bytes 1966080 | tf_op jit(solution)/shard_map/reduce_scatter | solution.py:575
  292.9 181.4 %reduce-scatter.13.cloned.1.call-start = ((), (), s32[]{:S(2)}) async-start(), calls=%async_computation.11 | async-start | bytes 9732096
  328.4 287.6 %reduce-scatter.11.cloned.1.call-start = ((), (), s32[]{:S(2)}) async-start(), calls=%async_computation.10 | async-start | bytes 9732096 | tf_op jit(solution)/shard_map/reduce_scatter | solution.py:569
  328.5 0.7 copy-start.6
  328.5 0.7 copy-start.7
  328.5 0.7 copy-start.8
  328.5 0.7 copy-start.12
  328.5 43.2 %copy-start.1 = (bf16[2,128,768]{2,1,0:T(8,128)(2,1)S(1)}, bf16[2,128,768]{2,1,0:T(8,128)(2,1)}, u32[]{:S(2)}) copy-start(bf16[2,128,768]{2,1,0:T(8,128)(2,1)} %param.17) | copy-start | bytes 1179652
  329.2 43.8 %copy-start.2 = (f32[256,768]{1,0:T(8,128)S(1)}, f32[256,768]{1,0:T(8,128)}, u32[]{:S(2)}) copy-start(f32[256,768]{1,0:T(8,128)} %get-tuple-element.52.dy_ref) | copy-start | bytes 2359300
Sparse Core Ops, SparseCore 0:
  26.0 30.9 all-gather.9
  60.5 72.4 all-gather.7
  135.2 35.6 all-gather.5
  172.3 35.9 all-gather.11
  263.4 34.1 reduce-scatter.8
  299.7 34.2 reduce-scatter.6
  339.9 134.4 reduce-scatter.12
  481.3 134.6 reduce-scatter.10

commit v2 on v1

--- a/solution.py
+++ b/solution.py
@@ -83,6 +83,12 @@
     return jnp.concatenate([v, jnp.zeros((v.shape[0], extra), v.dtype)], axis=1)
 
 
+def put_rows(ref, value, order):
+    step = value.shape[0] // len(order)
+    for source, slot in enumerate(order):
+        ref[slot * step : (slot + 1) * step, :] = value[source * step : (source + 1) * step, :]
+
+
 def vmem():
     return pl.BlockSpec(memory_space=pltpu.VMEM)
 
@@ -99,8 +105,10 @@
     return jax.ShapeDtypeStruct(shape, dtype)
 
 
-def bias_kernel(me_ref, w_ref, b_ref, ext_ref):
+def bias_kernel(me_ref, table_ref, onehot_ref, b_ref, ext_ref, line_ref):
     heads, block, full = b_ref.shape
+    shards = table_ref.shape[0]
+    group = heads // shards
     me = me_ref[0]
     start = pl.multiple_of(me * block, block)
     width = 2 * block
@@ -109,30 +117,35 @@
     masked = (col_i - row_i) > block
     far = lax.broadcasted_iota(jnp.int32, ext_ref.shape, 1) < start
 
-    def body(head, carry):
-        row = w_ref[pl.ds(head, 1), :]
-        tile = pltpu.roll(
-            jnp.broadcast_to(row, (block, width)), 0, 1, stride=1, stride_axis=0
-        )
-        ext_ref[...] = jnp.where(far, row[:, width - 1 : width], NEG)
-        ext_ref[:, pl.ds(start, width)] = jnp.where(masked, NEG, tile)
-        b_ref[head] = ext_ref[:, block:]
+    def body(h, carry):
+        line_ref[...] = tn(table_ref[h], onehot_ref[...])
+        for a in range(group):
+            row = line_ref[a : a + 1, :]
+            tile = pltpu.roll(
+                jnp.broadcast_to(row, (block, width)), 0, 1, stride=1, stride_axis=0
+            )
+            ext_ref[...] = jnp.where(far, row[:, width - 1 : width], NEG)
+            ext_ref[:, pl.ds(start, width)] = jnp.where(masked, NEG, tile)
+            b_ref[h * group + a] = ext_ref[:, block:]
         return carry
 
-    lax.fori_loop(0, heads, body, 0)
-
-
-def bias_tiles(me, table, block, full):
-    heads = table.shape[0]
+    lax.fori_loop(0, shards, body, 0)
+
+
+def bias_tiles(me, tables, onehot, group, block, full):
+    shards, buckets, lanes = tables.shape
     return pl.pallas_call(
         bias_kernel,
-        out_shape=sds((heads, block, full), F32),
-        in_specs=[smem(), vmem()],
+        out_shape=sds((shards * group, block, full), F32),
+        in_specs=[smem(), vmem(), vmem()],
         out_specs=vmem(),
-        scratch_shapes=[pltpu.VMEM((block, full + block), F32)],
+        scratch_shapes=[
+            pltpu.VMEM((block, full + block), F32),
+            pltpu.VMEM((lanes, 2 * block), F32),
+        ],
         compiler_params=params(),
         name="bias_tiles",
-    )(me, table)
+    )(me, tables, onehot)
 
 
 def lane_groups(width, group, size):
@@ -167,10 +180,9 @@
     key = lax.broadcasted_iota(jnp.int32, (1, full), 1)
 
     def body(h, carry):
-        q_ref[h] = padded(nn(nq_ref[...], wq_ref[h]).astype(BF16), pw)
-        kv = nn(nk_ref[...], wkv_ref[h]).astype(BF16)
-        k_ref[h] = padded(kv[:, :win], pw)
-        v_ref[h] = padded(kv[:, win:], pw)
+        q_ref[h] = padded(nt(nq_ref[...], wq_ref[h]).astype(BF16), pw)
+        k_ref[h] = padded(nt(nk_ref[...], wkv_ref[h, 0]).astype(BF16), pw)
+        v_ref[h] = padded(nt(nk_ref[...], wkv_ref[h, 1]).astype(BF16), pw)
         for s in range(seqs):
             kw = k_ref[h, s * full : (s + 1) * full, :]
             vw = v_ref[h, s * full : (s + 1) * full, :]
@@ -232,6 +244,7 @@
     biased,
     group,
     size,
+    order,
     len_ref,
     me_ref,
     nq_ref,
@@ -262,9 +275,9 @@
     me = me_ref[0]
 
     da = dy_ref[...].astype(BF16)
-    nqt_ref[...] = nq_ref[...].T
-    nkt_ref[...] = nk_ref[...].T
-    dat_ref[...] = da.T
+    put_rows(nqt_ref, nq_ref[...].T, order)
+    put_rows(nkt_ref, nk_ref[...].T, order)
+    put_rows(dat_ref, da.T, order)
     if biased:
         ext_ref[:, :block] = jnp.zeros((block, block), F32)
         start = pl.multiple_of(me * block, block)
@@ -321,8 +334,8 @@
                 diag_ref[pl.ds(h * group + a, 1), :] = line
         dkv = dkv_ref[...]
         dq_h = dq_ref[...][:, :win]
-        kv_term = nt(dkv, wkv_ref[h])
-        q_term = nt(dq_h, wq_ref[h])
+        kv_term = nn(dkv[:, :win], wkv_ref[h, 0]) + nn(dkv[:, win:], wkv_ref[h, 1])
+        q_term = nn(dq_h, wq_ref[h])
         w_ref[h] = jnp.concatenate(
             [
                 nn(nkt_ref[...], dkv).astype(BF16),
@@ -361,7 +374,9 @@
         gg_ref[...] = gg
 
 
-def attend_backward(lens, me, nq, nk, saved, wq, wkv, wo, dy, gain, extra, biased, group, size):
+def attend_backward(
+    lens, me, nq, nk, saved, wq, wkv, wo, dy, gain, extra, biased, group, size, order
+):
     q, k, v, c, lse = saved
     rows, width = nq.shape
     shards, keys, pw = k.shape
@@ -391,7 +406,7 @@
         ]
     flops = 4 * (rows + 2 * keys + rows) * width * width + 10 * rows * full * width
     return pl.pallas_call(
-        functools.partial(backward_kernel, biased, group, size),
+        functools.partial(backward_kernel, biased, group, size, order),
         out_shape=out_shape,
         in_specs=[smem(), smem()] + [vmem()] * (len(args) - 2),
         out_specs=[vmem()] * 4,
@@ -405,7 +420,7 @@
 
 
 def feed_kernel(
-    y_ref, n_ref, cot_ref, win_ref, wout_ref, gain_ref, out_ref, dy_ref, gg_ref, w_ref,
+    order, y_ref, n_ref, cot_ref, win_ref, wout_ref, gain_ref, out_ref, dy_ref, gg_ref, w_ref,
     acc_ref, dn_ref, nt_ref, ct_ref,
 ):
     step = pl.program_id(0)
@@ -413,8 +428,8 @@
 
     @pl.when(step == 0)
     def _():
-        nt_ref[...] = n_ref[...].T
-        ct_ref[...] = cot_ref[...].T
+        put_rows(nt_ref, n_ref[...].T, order)
+        put_rows(ct_ref, cot_ref[...].T, order)
         acc_ref[...] = y_ref[...]
         dn_ref[...] = jnp.zeros_like(dn_ref)
 
@@ -446,13 +461,13 @@
         gg_ref[...] = gg
 
 
-def feed(y, n, cot, w_in, w_out, gain, shards):
+def feed(y, n, cot, w_in, w_out, gain, shards, order):
     rows, width = y.shape
     hidden = w_out.shape[0]
     part = hidden // shards
     fixed = lambda shape: pl.BlockSpec(shape, lambda j: (0,) * len(shape))
     return pl.pallas_call(
-        feed_kernel,
+        functools.partial(feed_kernel, order),
         grid=(shards,),
         out_shape=[
             sds((rows, width), BF16),
@@ -488,6 +503,301 @@
     )(y, n, cot, w_in, w_out, gain)
 
 
+MESH = pl.DeviceIdType.MESH
+
+
+def place():
+    b = lax.axis_index("batch")
+    me = lax.axis_index("head")
+    core = lax.rem(b, 2)
+    x = lax.rem(lax.div(b, 2), 2)
+    y = lax.div(b, 4)
+    return b, me, core, x, y
+
+
+def near_devices(b, me, core, x, y, shards):
+    over_core = (b + 1 - 2 * core, me)
+    over_x = (b + 2 - 4 * x, me)
+    over_y = (b + 4 - 8 * y, me)
+    across = (b + 2 - 4 * x + 4 - 8 * y, me)
+    ahead = [(b, lax.rem(me + k, shards)) for k in range(1, shards)]
+    return over_core, over_x, over_y, across, ahead
+
+
+def greet(devices):
+    barrier = pltpu.get_barrier_semaphore()
+    for device in devices:
+        pl.semaphore_signal(barrier, inc=1, device_id=device, device_id_type=MESH)
+    pl.semaphore_wait(barrier, len(devices))
+
+
+def remote(src, dst, send, recv, device):
+    return pltpu.make_async_remote_copy(
+        src_ref=src,
+        dst_ref=dst,
+        send_sem=send,
+        recv_sem=recv,
+        device_id=device,
+        device_id_type=MESH,
+    )
+
+
+def gather_kernel(n, *refs):
+    shard_refs, table_ref = refs[:n], refs[n]
+    full_refs, tables_ref = refs[n + 1 : 2 * n + 1], refs[2 * n + 1]
+    (zs, zr, ps, pr, cs, cr, ts, tr, local) = refs[2 * n + 2 :]
+    shards = tables_ref.shape[0]
+    b, me, core, x, y = place()
+    over_core, over_x, over_y, across, ahead = near_devices(b, me, core, x, y, shards)
+    greet([over_core, over_x, over_y, across] + ahead)
+    slot = core * 4 + lax.div(b, 2)
+
+    def window(ref, first, count):
+        step = ref.shape[-2] // 8
+        rows = pl.ds(pl.multiple_of(first * step, step), count * step)
+        return ref.at[:, rows, :]
+
+    started = []
+
+    def start(copy):
+        copy.start()
+        started.append(copy)
+        return copy
+
+    from_z, from_plane, from_core = {}, {}, {}
+    for k in range(1, shards):
+        start(remote(table_ref, tables_ref.at[me], ts.at[k - 1], tr.at[k - 1], ahead[k - 1]))
+    for i in range(n):
+        for k in range(1, shards):
+            from_z[i, k] = start(
+                remote(
+                    window(shard_refs[i], slot, 1),
+                    window(full_refs[i].at[me], slot, 1),
+                    zs.at[i, k - 1],
+                    zr.at[i, k - 1],
+                    ahead[k - 1],
+                )
+            )
+    copies = [pltpu.make_async_copy(table_ref, tables_ref.at[me], local.at[n])]
+    copies += [
+        pltpu.make_async_copy(shard_refs[i], full_refs[i].at[me], local.at[i]) for i in range(n)
+    ]
+    for copy in copies:
+        copy.start()
+    for i in range(n):
+        for k in range(1, shards):
+            from_z[i, k].wait_recv()
+            piece = window(full_refs[i].at[lax.rem(me + shards - k, shards)], slot, 1)
+            for d, device in enumerate((over_x, over_y, across)):
+                from_plane[i, k, d] = start(
+                    remote(piece, piece, ps.at[i, k - 1, d], pr.at[i, k - 1, d], device)
+                )
+    for i in range(n):
+        for k in range(1, shards):
+            for d in range(3):
+                from_plane[i, k, d].wait_recv()
+            half = window(full_refs[i].at[lax.rem(me + shards - k, shards)], core * 4, 4)
+            from_core[i, k] = start(
+                remote(half, half, cs.at[i, k - 1], cr.at[i, k - 1], over_core)
+            )
+    for copy in from_core.values():
+        copy.wait_recv()
+    for k in range(1, shards):
+        started[k - 1].wait_recv()
+    for copy in started:
+        copy.wait_send()
+    for copy in copies:
+        copy.wait()
+
+
+def gather_weights(weights, table, shards):
+    n = len(weights)
+    anywhere = pl.BlockSpec(memory_space=pl.ANY)
+    dma = pltpu.SemaphoreType.DMA
+    return pl.pallas_call(
+        functools.partial(gather_kernel, n),
+        out_shape=[sds((shards, *w.shape), w.dtype) for w in weights]
+        + [sds((shards, *table.shape), table.dtype)],
+        in_specs=[anywhere] * (n + 1),
+        out_specs=[anywhere] * (n + 1),
+        scratch_shapes=[
+            dma((n, shards - 1)),
+            dma((n, shards - 1)),
+            dma((n, shards - 1, 3)),
+            dma((n, shards - 1, 3)),
+            dma((n, shards - 1)),
+            dma((n, shards - 1)),
+            dma((shards - 1,)),
+            dma((shards - 1,)),
+            dma((n + 1,)),
+        ],
+        compiler_params=pltpu.CompilerParams(
+            collective_id=0, has_side_effects=True, vmem_limit_bytes=VMEM_LIMIT
+        ),
+        name="gather_weights",
+    )(*weights, table)
+
+
+def reduce_kernel(items, w_count, *refs):
+    w_refs, small_ref = refs[:w_count], refs[w_count]
+    out_refs, small_out = refs[w_count + 1 : 2 * w_count + 1], refs[2 * w_count + 1]
+    (own, rc, r1a, r1b, r2a, r2b, tot, rz, sr, lsem, cs, cr, s1, q1, s2, q2, zs, zr, ms, mr) = refs[
+        2 * w_count + 2 :
+    ]
+    shards = w_refs[0].shape[0]
+    cols = own.shape[-1]
+    half = cols // 2
+    b, me, core, x, y = place()
+    over_core, over_x, over_y, across, ahead = near_devices(b, me, core, x, y, shards)
+    greet([over_core, over_x, over_y] + ahead)
+    chunks = [(i, k) for i in range(len(items)) for k in range(shards)]
+    owner = [lax.rem(me + 1 + k, shards) for k in range(shards)]
+    started = []
+
+    def start(copy):
+        copy.start()
+        started.append(copy)
+        return copy
+
+    small = [start(remote(small_ref, sr.at[0], ms.at[0], mr.at[0], over_core))]
+    load, first, second, third, last = {}, {}, {}, {}, {}
+
+    def stage_load(c):
+        i, k = chunks[c]
+        w, col = items[i]
+        piece = lambda side: w_refs[w].at[owner[k], side, :, :, :, pl.ds(col, cols)]
+        load[c] = pltpu.make_async_copy(piece(core), own.at[c], lsem.at[c])
+        load[c].start()
+        first[c] = start(remote(piece(1 - core), rc.at[c], cs.at[c], cr.at[c], over_core))
+
+    def stage_core(c):
+        load[c].wait()
+        first[c].wait_recv()
+        own[c] = own[c] + rc[c]
+        second[c] = [
+            start(
+                remote(
+                    own.at[c, :, 1 - x, :, pl.ds(0, half)],
+                    r1a.at[c],
+                    s1.at[c, 0],
+                    q1.at[c, 0],
+                    over_x,
+                )
+            ),
+            start(
+                remote(
+                    own.at[c, 1 - y, :, :, pl.ds(half, half)],
+                    r1b.at[c],
+                    s1.at[c, 1],
+                    q1.at[c, 1],
+                    over_y,
+                )
+            ),
+        ]
+
+    def stage_first(c):
+        for copy in second[c]:
+            copy.wait_recv()
+        for other in range(2):
+            r1a[c, other] = r1a[c, other] + own[c, other, x, :, :half]
+            r1b[c, other] = r1b[c, other] + own[c, y, other, :, half:]
+        third[c] = [
+            start(remote(r1a.at[c, 1 - y], r2a.at[c], s2.at[c, 0], q2.at[c, 0], over_y)),
+            start(remote(r1b.at[c, 1 - x], r2b.at[c], s2.at[c, 1], q2.at[c, 1], over_x)),
+        ]
+
+    def stage_second(c):
+        i, k = chunks[c]
+        for copy in third[c]:
+            copy.wait_recv()
+        tot[c, :, :half] = r1a[c, y] + r2a[c]
+        tot[c, :, half:] = r1b[c, x] + r2b[c]
+        if k < shards - 1:
+            last[i, k] = start(
+                remote(tot.at[c], rz.at[i, k], zs.at[i, k], zr.at[i, k], (b, owner[k]))
+            )
+
+    for c in range(len(chunks)):
+        stage_load(c)
+    for t in range(len(chunks) + 3):
+        if t < len(chunks):
+            stage_core(t)
+        if t == 0:
+            small[0].wait_recv()
+            sr[6] = small_ref[...] + sr[0]
+            small.append(start(remote(sr.at[6], sr.at[1], ms.at[1], mr.at[1], over_x)))
+        if t == 2:
+            small[1].wait_recv()
+            sr[7] = sr[6] + sr[1]
+            small.append(start(remote(sr.at[7], sr.at[2], ms.at[2], mr.at[2], over_y)))
+        if t == 4:
+            small[2].wait_recv()
+            sr[8] = sr[7] + sr[2]
+            for k in range(shards - 1):
+                small.append(
+                    start(remote(sr.at[8], sr.at[3 + k], ms.at[3 + k], mr.at[3 + k], ahead[k]))
+                )
+        if 0 <= t - 1 < len(chunks):
+            stage_first(t - 1)
+        if 0 <= t - 3 < len(chunks):
+            stage_second(t - 3)
+    total = sr[8]
+    for k in range(shards - 1):
+        small[3 + k].wait_recv()
+        total = total + sr[3 + k]
+    small_out[...] = total
+    for i, (w, col) in enumerate(items):
+        total = tot[i * shards + shards - 1].astype(F32)
+        for k in range(shards - 1):
+            last[i, k].wait_recv()
+            total = total + rz[i, k].astype(F32)
+        out_refs[w][:, col : col + cols] = total
+    for copy in started:
+        copy.wait_send()
+
+
+def reduce_blocks(arrays, small, cols):
+    shards, tall = arrays[0].shape[:2]
+    rows = tall // 8
+    items = [(w, col) for w, a in enumerate(arrays) for col in range(0, a.shape[2], cols)]
+    n = len(items) * shards
+    half = cols // 2
+    anywhere = pl.BlockSpec(memory_space=pl.ANY)
+    dma = pltpu.SemaphoreType.DMA
+    return pl.pallas_call(
+        functools.partial(reduce_kernel, items, len(arrays)),
+        out_shape=[sds((rows, a.shape[2]), F32) for a in arrays] + [sds(small.shape, F32)],
+        in_specs=[anywhere] * len(arrays) + [vmem()],
+        out_specs=[vmem()] * (len(arrays) + 1),
+        scratch_shapes=[
+            pltpu.VMEM((n, 2, 2, rows, cols), BF16),
+            pltpu.VMEM((n, 2, 2, rows, cols), BF16),
+            pltpu.VMEM((n, 2, rows, half), BF16),
+            pltpu.VMEM((n, 2, rows, half), BF16),
+            pltpu.VMEM((n, rows, half), BF16),
+            pltpu.VMEM((n, rows, half), BF16),
+            pltpu.VMEM((n, rows, cols), BF16),
+            pltpu.VMEM((len(items), shards - 1, rows, cols), BF16),
+            pltpu.VMEM((9, *small.shape), F32),
+            dma((n,)),
+            dma((n,)),
+            dma((n,)),
+            dma((n, 2)),
+            dma((n, 2)),
+            dma((n, 2)),
+            dma((n, 2)),
+            dma((len(items), shards - 1)),
+            dma((len(items), shards - 1)),
+            dma((6,)),
+            dma((6,)),
+        ],
+        compiler_params=pltpu.CompilerParams(
+            collective_id=1, has_side_effects=True, vmem_limit_bytes=VMEM_LIMIT
+        ),
+        name="reduce_blocks",
+    )(*[a.reshape(shards, 2, 2, 2, rows, a.shape[2]) for a in arrays], small)
+
+
 def per_device(
     layer_input,
     memory,
@@ -510,7 +820,6 @@
     shards = lax.axis_size("head")
     me = lax.axis_index("head").astype(jnp.int32).reshape(1)
     batch_count = lax.axis_size("batch")
-    batch_index = lax.axis_index("batch")
     seqs, block, width = layer_input.shape
     group = rel_bias.shape[1]
     size = self_query.shape[1] // group
@@ -518,7 +827,6 @@
     full = block * shards
     enc_full = memory.shape[1] * shards
     rows = seqs * block
-    slice_width = width // batch_count
     part = feed_in.shape[2] // shards
     sg, cg, fg = (g.astype(F32).reshape(1, width) for g in (self_gain, cross_gain, feed_gain))
 
@@ -528,26 +836,22 @@
     n1_all = lax.all_gather(n1.reshape(seqs, block, width), "head", axis=1, tiled=True)
     n1_all = n1_all.reshape(seqs * full, width)
 
-    def take(weight, axis):
-        length = weight.shape[axis] // batch_count
-        return lax.dynamic_slice_in_dim(weight, batch_index * length, length, axis)
-
-    projections = jnp.concatenate(
-        [take(self_query, 0), take(self_key_value[0], 0), take(self_key_value[1], 0),
-         take(cross_query, 0), take(cross_key_value[0], 0), take(cross_key_value[1], 0)], axis=1
-    )
-    projections = lax.all_gather(projections, ("head", "batch"), axis=0, tiled=True)
-    projections = projections.reshape(shards, width, 6 * win)
-    wq1, wkv1 = projections[:, :, :win], projections[:, :, win : 3 * win]
-    wq2, wkv2 = projections[:, :, 3 * win : 4 * win], projections[:, :, 4 * win :]
-    outs = jnp.concatenate([take(self_out, 1), take(cross_out, 1)], axis=1)
-    outs = lax.all_gather(outs, "head", axis=0, tiled=True)
-    outs = lax.all_gather(outs.reshape(width, 2, slice_width), "batch", axis=2, tiled=True)
-    wo1, wo2 = outs[:, 0], outs[:, 1]
-    table = lax.all_gather(rel_bias.T, "head", axis=0, tiled=True).astype(F32)
+    tight = batch_count == 8 and shards == 4
+    order = tuple((i % 2) * 4 + i // 2 for i in range(8)) if tight else (0,)
+    table = jnp.pad(rel_bias, ((0, 0), (0, 128 - group)))
+    flip = lambda w: jnp.swapaxes(w, -1, -2)
+    weights = [flip(self_query)[None], flip(self_key_value), self_out[None]]
+    weights += [flip(cross_query)[None], flip(cross_key_value), cross_out[None]]
+    if tight:
+        *weights, tables = gather_weights(weights, table, shards)
+    else:
+        weights = [lax.all_gather(w, "head", axis=0) for w in weights]
+        tables = lax.all_gather(table, "head", axis=0)
+    wq1, wkv1, wo1, wq2, wkv2, wo2 = weights
+    wq1, wq2 = wq1[:, 0], wq2[:, 0]
+    wo1, wo2 = wo1.reshape(width, width), wo2.reshape(width, width)
     onehot = near_onehot(block)
-    near = jnp.einsum("hb,tb->ht", table, onehot, precision=highest)
-    bias = bias_tiles(me, near, block, full)
+    bias = bias_tiles(me, tables, onehot.T.astype(BF16), group, block, full)
     memory_all = lax.all_gather(memory, "head", axis=1, tiled=True).reshape(seqs * enc_full, width)
 
     *saved1, y1, n2 = attend_forward(
@@ -557,44 +861,49 @@
         enc_lengths, n2, memory_all, y1, wq2, wkv2, wo2, fg, None, group, size
     )
     result, dy2, gain3, feed_w = feed(
-        y2, n3, out_cotangent.reshape(rows, width), feed_in, feed_out, fg, shards
+        y2, n3, out_cotangent.reshape(rows, width), feed_in, feed_out, fg, shards, order
     )
     memory_part, gain2, cross_w, dy1 = attend_backward(
-        enc_lengths, me, n2, memory_all, saved2, wq2, wkv2, wo2, dy2, cg, y1, False, group, size
+        enc_lengths, me, n2, memory_all, saved2, wq2, wkv2, wo2, dy2, cg, y1, False, group, size, order
     )
     input_part, gain1, self_w, diag = attend_backward(
-        dec_lengths, me, n1, n1_all, saved1, wq1, wkv1, wo1, dy1, sg, bias, True, group, size
+        dec_lengths, me, n1, n1_all, saved1, wq1, wkv1, wo1, dy1, sg, bias, True, group, size, order
     )
 
-    feed_w = lax.psum_scatter(
-        feed_w.reshape(shards * width, 3 * part), ("head", "batch"), scatter_dimension=0, tiled=True
-    ).astype(F32)
     memory_grad = lax.psum_scatter(
         memory_part.reshape(seqs, enc_full, width), "head", scatter_dimension=1, tiled=True
     ).astype(F32)
     dn1 = lax.psum_scatter(
         input_part.reshape(seqs, full, width), "head", scatter_dimension=1, tiled=True
     ).astype(F32)
-    pair_w = jnp.concatenate(
-        [self_w.reshape(shards * width, 4 * win), cross_w.reshape(shards * width, 4 * win)], axis=1
-    )
-    pair_w = lax.psum_scatter(
-        pair_w, ("head", "batch"), scatter_dimension=0, tiled=True
-    ).astype(F32)
+    lines = jnp.concatenate([gain1, gain2, gain3], axis=0).reshape(-1, 2 * block)
+    spare = -(lines.shape[0] + diag.shape[0]) % 8
+    small = jnp.concatenate([lines, diag, jnp.zeros((spare, 2 * block), F32)], axis=0)
+    if tight:
+        feed_w, cross_w, self_w, small = reduce_blocks([feed_w, cross_w, self_w], small, 4 * win)
+    else:
+        feed_w, cross_w, self_w = (
+            lax.psum_scatter(
+                w.reshape(shards * width, w.shape[2]).astype(F32),
+                ("head", "batch"),
+                scatter_dimension=0,
+                tiled=True,
+            )
+            for w in (feed_w, cross_w, self_w)
+        )
+        small = lax.psum(small, ("batch", "head"))
+    gains = small[: lines.shape[0]].reshape(3, width)
+    diag = lax.dynamic_slice_in_dim(small, lines.shape[0] + me[0] * group, group, 0)
+    table_grad = jnp.einsum("tb,ht->bh", onehot, diag, precision=highest)
     dx, _ = norm_grads(x32, sg, dn1.reshape(rows, width))
     input_grad = (dy1 + dx).reshape(seqs, block, width)
-    table_grad = jnp.einsum("tb,ht->bh", onehot, diag, precision=highest)
-    gains, table_grad = lax.psum(
-        (jnp.concatenate([gain1, gain2, gain3], axis=0), table_grad), ("batch", "head")
-    )
-    table_grad = lax.dynamic_slice_in_dim(table_grad, me[0] * group, group, 1)
 
     def split(w):
         kv = jnp.stack([w[:, :win], w[:, win : 2 * win]])
         return w[:, 2 * win : 3 * win], kv, w[:, 3 * win :].T
 
-    self_q, self_kv, self_o = split(pair_w[:, : 4 * win])
-    cross_q, cross_kv, cross_o = split(pair_w[:, 4 * win :])
+    self_q, self_kv, self_o = split(self_w)
+    cross_q, cross_kv, cross_o = split(cross_w)
     return (
         result.reshape(seqs, block, width),
         input_grad,

time: 631 us -> 338 us (0.54)
  waiting for transfers between devices: 355 us -> 1.04 us
  Pallas kernels: 103 us -> 291 us
  blocking collectives: 67 us -> 0 us
  local copies, waits for them, and re-layouts: 69.6 us -> 12.2 us
    pallas_call x4 -> x6, Pallas kernels: 74.2 us -> 262 us  [the longest x1 107 us: reduce_blocks(): pl.pallas_call(functools.partial(reduce_kernel, items, len(arrays)), out_...]
    reduce_scatter x1 -> x0, waiting for transfers between devices: 140 us -> none  [per_device(): lax.psum_scatter(feed_w.reshape(shards * width, 3 * part), ('head', 'batc...]
    unnamed x9 -> x4, waiting for transfers between devices: 101 us -> 1.03 us
    all_gather x2 -> x0, waiting for transfers between devices: 64.8 us -> none  [the longest x1 57.3 us: per_device(): lax.all_gather(projections, ('head', 'batch'), axis=0, tiled=True)]
    psum x1 -> x0, blocking collectives: 39.1 us -> none  [per_device(): lax.psum((jnp.concatenate([gain1, gain2, gain3], axis=0), table_grad), ('...]
    all_gather x2 -> x0, blocking collectives: 27.9 us -> none  [the longest x1 16.2 us: per_device(): outs = lax.all_gather(outs, 'head', axis=0, tiled=True)]
    all_gather x1, waiting for transfers between devices: 26.9 us -> 0.01 us  [per_device(): lax.all_gather(n1.reshape(seqs, block, width), 'head', axis=1, tiled=True)]
    unnamed x37 -> x19, local copies, waits for them, and re-layouts: 28 us -> 2.29 us
  transfers between devices with their start and end apart: 8 -> 4, of which waited for: 6 -> 0; matrix products, arithmetic and copies ran while one was open for 13% -> 6% of each run, Pallas kernels for 8% -> 62%
where the time goes in v2:
time: 338 us; the launch traced here: 333 us
  Pallas kernels  291 us (86%)
  between operations  13.9 us (4%)
  other arithmetic  13.5 us (4%)
  local copies, waits for them, and re-layouts  12.2 us (4%)
    pallas_call x1, Pallas kernels, reduce_blocks(): pl.pallas_call(functools.partial(reduce_kernel, items, len(arrays)), out_...  107 us
    pallas_call x1, Pallas kernels, gather_weights(): pl.pallas_call(functools.partial(gather_kernel, n), out_shape=[sds((shard...  79.7 us
    pallas_call x2, Pallas kernels, attend_backward(): pl.pallas_call(functools.partial(backward_kernel, biased, group, size, or...  57.9 us
    pallas_call x2, Pallas kernels, attend_forward(): pl.pallas_call(functools.partial(forward_kernel, bias is not None, group,...  28.4 us
    pallas_call x1, Pallas kernels, feed(): pl.pallas_call(functools.partial(feed_kernel, order), grid=(shards,), out...  13.6 us
  transfers between devices with their start and end apart: 4, of which 0 were waited for; matrix products, arithmetic and copies ran while one was open for 6% of the time, Pallas kernels for 62%

profile of v2, /device:TPU:0, one launch (start us, length us, event | category | flops | bytes accessed | tf_op | source)
XLA Modules:
  0.0 333.2 jit_solution(10693611096489466142)
XLA Ops:
  7.2 0.0 all-gather.3.cloned.1.call-start
  7.2 0.7 convert_element_type.170
  7.9 1.2 fusion.4
  9.1 1.9 fusion.2
  11.0 0.0 all-gather.3.cloned.1.call-update
  11.0 0.0 all-gather.5.cloned.1.call-start
  11.1 0.7 all-gather.5.cloned.1.call-update
  11.8 0.0 reduce-scatter.3.cloned.1.call-start
  11.8 1.3 reshape.210.gain_ref
  13.1 0.8 copy.32
  13.8 1.3 reshape.220.gain_ref
  15.1 1.3 reshape.222.gain_ref
  16.4 0.6 pad.4.refs_6_
  17.0 79.7 %gather_weights.1 = (bf16[4,1,192,768]{3,2,1,0:T(8,128)(2,1)}, bf16[4,2,192,768]{3,2,1,0:T(8,128)(2,1)}, bf16[4,1,192,768]{3,2,1,0:T(8,128)(2,1)}, bf16[4,1,192,...) custom-call(bf16[1,192,768]{2,1,0:T(8,128)(2,1)} %bitcast.67, ...), custom_call_target="tpu_custom_call" | custom-call | tf_op jit(solution)/shard_map/gather_weights/pallas_call | solution.py:617
  96.7 0.0 copy-start
  96.7 0.6 convert_convert_fusion.onehot_ref
  97.3 4.2 %bias_tiles.1.rest_0_ = f32[12,128,512]{2,1,0:T(8,128)} custom-call(s32[1]{0:T(128)} %bitcast.13.me_ref, bf16[4,32,128]{2,1,0:T(8,128)(2,1)} %get-tuple-element.55.table_ref, bf16[32,256]{1,0:T(8,128)(2,1)} %convert_convert_fusion.onehot_ref), custom_call_target="tpu_custom_call" | custom-call | tf_op jit(solution)/shard_map/bias_tiles/pallas_call | solution.py:137
  101.6 0.9 multiply_convert_fusion.nq_ref
  102.5 14.5 %attend_forward.2 = (bf16[4,256,256]{2,1,0:T(8,128)(2,1)}, bf16[4,1024,256]{2,1,0:T(8,128)(2,1)}, bf16[4,1024,256]{2,1,0:T(8,128)(2,1)}, bf16[4,256,256]{2,1,0:T...) custom-call(s32[2]{0:T(128)} %len_ref.7, ...), custom_call_target="tpu_custom_call" | custom-call | flops 3825205248 | bytes 16777216 | tf_op jit(solution)/shard_map/attend_forward/pallas_call | solution.py:222
  117.0 13.8 %attend_forward.3 = (bf16[4,256,256]{2,1,0:T(8,128)(2,1)}, bf16[4,1024,256]{2,1,0:T(8,128)(2,1)}, bf16[4,1024,256]{2,1,0:T(8,128)(2,1)}, bf16[4,256,256]{2,1,0:T...) custom-call(s32[2]{0:T(128)} %len_ref.6, ...), custom_call_target="tpu_custom_call" | custom-call | flops 3825205248 | bytes 16777216 | tf_op jit(solution)/shard_map/attend_forward/pallas_call | solution.py:222
  130.8 13.6 %feed.1 = (bf16[256,768]{1,0:T(8,128)(2,1)}, f32[256,768]{1,0:T(8,128)}, f32[1,768]{1,0:T(1,128)}, bf16[4,768,1536]{2,1,0:T(8,128)(2,1)}) custom-call(f32[256,768]{1,0:T(8,128)} %get-tuple-element.61.y_ref, bf16[256,768]{1,0:T(8,128)(2,1)} %get-tuple-element.62.n_ref, bf16[256,768]{1,0:T(8,128)(2,1)} %bitcast.83, bf16[2,768,2048]{2,1,0:T(8,128)(2,1)} %win_ref.1, ...), custom_call_target="tpu_custom_call" | custom-call | flops 7247757312 | bytes 25165824 | tf_op jit(solution)/shard_map/feed/pallas_call | solution.py:469
  144.5 28.3 %attend_backward.2 = (bf16[1024,768]{1,0:T(8,128)(2,1)}, f32[1,768]{1,0:T(1,128)}, bf16[4,768,768]{2,1,0:T(8,128)(2,1)}, f32[256,768]{1,0:T(8,128)}) custom-call(s32[2]{0:T(128)} %len_ref.6, s32[1]{0:T(128)} %bitcast.13.me_ref, bf16[256,768]{1,0:T(8,128)(2,1)} %get-tuple-element.56.nq_ref, bf16[1024,768]{1,0:T(8,128)(2,1)} %bitcast.74, ...), custom_call_target="tpu_custom_call" | custom-call | flops 7046430720 | bytes 25165824 | tf_op jit(solution)/shard_map/attend_backward/pallas_call | solution.py:408
  172.8 29.5 %attend_backward.3 = (bf16[1024,768]{1,0:T(8,128)(2,1)}, f32[1,768]{1,0:T(1,128)}, bf16[4,768,768]{2,1,0:T(8,128)(2,1)}, f32[12,256]{1,0:T(8,128)}) custom-call(s32[2]{0:T(128)} %len_ref.7, s32[1]{0:T(128)} %bitcast.13.me_ref, bf16[256,768]{1,0:T(8,128)(2,1)} %multiply_convert_fusion.nq_ref, bf16[1024,768]{1,0:T(8,128)(2,1)} %bitcast.72, ...), custom_call_target="tpu_custom_call" | custom-call | flops 7046430720 | bytes 25165824 | tf_op jit(solution)/shard_map/attend_backward/pallas_call | solution.py:408
  202.4 0.0 copy-start.6
  202.4 0.0 copy-start.7
  202.4 0.0 copy-start.4
  202.4 0.0 reduce-scatter.3.cloned.1.call-update
  202.4 0.3 reduce-scatter.5.cloned.1.call-start
  202.7 0.3 reduce-scatter.5.cloned.1.call-update
  203.0 0.1 pad.13.clone
  203.1 0.7 maximum_maximum_fusion.refs_3_
  203.8 106.8 %reduce_blocks.1 = (f32[96,1536]{1,0:T(8,128)}, f32[96,768]{1,0:T(8,128)}, f32[96,768]{1,0:T(8,128)}, f32[24,256]{1,0:T(8,128)}) custom-call(bf16[4,2,2,2,96,1536]{5,4,3,2,1,0:T(8,128)(2,1)} %bitcast.59, bf16[4,2,2,2,96,768]{5,4,3,2,1,0:T(8,128)(2,1)} %bitcast.60, bf16[4,2,2,2,96,768]{5,4,3,2,1,0:T(8,128)(2,1)} %bitcast.61, ...), custom_call_target="tpu_custom_call" | custom-call | tf_op jit(solution)/shard_map/reduce_blocks/pallas_call | solution.py:767
  310.7 0.0 copy-start.1
  310.7 2.1 slice_bitcast_fusion.3
  312.8 0.7 copy.33
  313.5 0.7 copy.34
  314.3 0.8 fusion.28
  315.1 0.6 squeeze.17
  315.7 0.6 squeeze.18
  316.3 0.6 squeeze.19
  316.9 0.7 pad_maximum_fusion.2
  317.6 0.7 pad_maximum_fusion.1
  318.3 0.7 slice_bitcast_fusion
  319.0 0.8 pad_maximum_fusion
  319.8 1.5 fusion.8
  321.3 1.3 fusion.3
  322.6 2.1 fusion.7
  324.7 1.9 convert_element_type.191
  (21 shorter events, 0.1 us)
Async XLA Ops:
  7.2 95.3 %all-gather.3.cloned.1.call-start = ((), (), s32[]{:S(2)}) async-start(), calls=%async_computation.2 | async-start | bytes 1966080 | tf_op jit(solution)/shard_map/all_gather | solution.py:836
  11.0 106.0 %all-gather.5.cloned.1.call-start = ((), (), s32[]{:S(2)}) async-start(), calls=%async_computation.3 | async-start | bytes 1966080 | tf_op jit(solution)/shard_map/all_gather | solution.py:855
  11.8 309.5 %reduce-scatter.3.cloned.1.call-start = ((), (), s32[]{:S(2)}) async-start(), calls=%async_computation.4 | async-start | bytes 1966080 | tf_op jit(solution)/shard_map/reduce_scatter | solution.py:876
  96.7 4.9 %copy-start = (bf16[2,128,768]{2,1,0:T(8,128)(2,1)S(1)}, bf16[2,128,768]{2,1,0:T(8,128)(2,1)}, u32[]{:S(2)}) copy-start(bf16[2,128,768]{2,1,0:T(8,128)(2,1)} %param.17) | copy-start | bytes 1179652
  202.3 0.7 copy-start.5
  202.4 0.7 copy-start.6
  202.4 0.7 copy-start.7
  202.4 0.8 copy-start.4
  202.4 122.3 %reduce-scatter.5.cloned.1.call-start = ((), (), s32[]{:S(2)}) async-start(), calls=%async_computation.5 | async-start | bytes 1966080 | tf_op jit(solution)/shard_map/reduce_scatter | solution.py:873
  310.7 7.6 %copy-start.3 = (f32[96,1536]{1,0:T(8,128)S(1)}, f32[96,1536]{1,0:T(8,128)}, u32[]{:S(2)}) copy-start(f32[96,1536]{1,0:T(8,128)} %get-tuple-element.88) | copy-start | bytes 1769476
  310.7 10.6 %copy-start.1 = (bf16[2,128,768]{2,1,0:T(8,128)(2,1)S(1)}, bf16[2,128,768]{2,1,0:T(8,128)(2,1)}, u32[]{:S(2)}) copy-start(bf16[2,128,768]{2,1,0:T(8,128)(2,1)} %param.17) | copy-start | bytes 1179652
  312.8 9.8 %copy-start.2 = (f32[256,768]{1,0:T(8,128)S(1)}, f32[256,768]{1,0:T(8,128)}, u32[]{:S(2)}) copy-start(f32[256,768]{1,0:T(8,128)} %get-tuple-element.70.dy_ref) | copy-start | bytes 2359300
Sparse Core Ops, SparseCore 0:
  11.1 64.3 all-gather.2
  77.1 36.2 all-gather.4
  202.5 43.1 reduce-scatter.2
  247.9 61.1 reduce-scatter.4

commit v3 on v2

--- a/solution.py
+++ b/solution.py
@@ -638,164 +638,536 @@
     )(*weights, table)
 
 
-def reduce_kernel(items, w_count, *refs):
-    w_refs, small_ref = refs[:w_count], refs[w_count]
-    out_refs, small_out = refs[w_count + 1 : 2 * w_count + 1], refs[2 * w_count + 1]
-    (own, rc, r1a, r1b, r2a, r2b, tot, rz, sr, lsem, cs, cr, s1, q1, s2, q2, zs, zr, ms, mr) = refs[
-        2 * w_count + 2 :
+def flipped(bit, by):
+    return bit + by - 2 * bit * by
+
+
+class Links:
+    def __init__(self):
+        b, me, core, x, y = place()
+        self.me, self.core, self.x, self.y = me, core, x, y
+        self.high, self.low = lax.div(me, 2), lax.rem(me, 2)
+        self.pair, self.far, self.cross = self.owner(1), self.owner(2), self.owner(0)
+        self.over_core = (b + 1 - 2 * core, me)
+        self.over_x = (b + 2 - 4 * x, me)
+        self.over_y = (b + 4 - 8 * y, me)
+        self.to_pair, self.to_far, self.to_cross = (b, self.pair), (b, self.far), (b, self.cross)
+
+    def owner(self, k):
+        by_low, by_high = 1 - k // 2, 1 - k % 2
+        return 2 * flipped(self.high, by_high) + flipped(self.low, by_low)
+
+    def greet(self):
+        greet(
+            [self.over_core, self.over_x, self.over_y, self.to_pair, self.to_far, self.to_cross]
+        )
+
+
+class Sums:
+    @staticmethod
+    def scratch(chunks, rows, cols):
+        items, half = chunks // 4, cols // 2
+        dma = pltpu.SemaphoreType.DMA
+        return [
+            pltpu.VMEM((chunks, 2, 2, rows, cols), BF16),
+            pltpu.VMEM((chunks, 2, 2, rows, cols), BF16),
+            pltpu.VMEM((chunks, 2, rows, half), BF16),
+            pltpu.VMEM((chunks, 2, rows, half), BF16),
+            pltpu.VMEM((chunks, rows, half), BF16),
+            pltpu.VMEM((chunks, rows, half), BF16),
+            pltpu.VMEM((chunks, rows, cols), BF16),
+            pltpu.VMEM((items, 3, rows, cols), BF16),
+            dma((chunks,)),
+            dma((chunks,)),
+            dma((chunks,)),
+            dma((chunks, 2)),
+            dma((chunks, 2)),
+            dma((chunks, 2)),
+            dma((chunks, 2)),
+            dma((items, 3)),
+            dma((items, 3)),
+        ]
+
+    count = 17
+
+    def __init__(self, links, refs):
+        (self.own, self.rc, self.r1a, self.r1b, self.r2a, self.r2b, self.tot, self.rz) = refs[:8]
+        (self.ls, self.cs, self.cr, self.s1, self.q1, self.s2, self.q2, self.zs, self.zr) = refs[8:]
+        self.links = links
+        self.chunks, self.cols = self.own.shape[0], self.own.shape[-1]
+        self.half = self.cols // 2
+
+    def piece(self, w_ref, c, side, base):
+        start = pl.multiple_of(((c - base) // 4) * self.cols, self.cols)
+        return w_ref.at[self.links.owner((c - base) % 4), side, :, :, :, pl.ds(start, self.cols)]
+
+    def local(self, w_ref, c, base):
+        return pltpu.make_async_copy(
+            self.piece(w_ref, c, self.links.core, base), self.own.at[c], self.ls.at[c]
+        )
+
+    def over_core(self, c, source):
+        return remote(
+            source, self.rc.at[c], self.cs.at[c], self.cr.at[c], self.links.over_core
+        )
+
+    def load(self, w_ref, c, base=0):
+        self.local(w_ref, c, base).start()
+        self.over_core(c, self.piece(w_ref, c, 1 - self.links.core, base)).start()
+
+    def firsts(self, c):
+        links, half = self.links, self.half
+        return (
+            remote(
+                self.own.at[c, :, 1 - links.x, :, pl.ds(0, half)],
+                self.r1a.at[c],
+                self.s1.at[c, 0],
+                self.q1.at[c, 0],
+                links.over_x,
+            ),
+            remote(
+                self.own.at[c, 1 - links.y, :, :, pl.ds(half, half)],
+                self.r1b.at[c],
+                self.s1.at[c, 1],
+                self.q1.at[c, 1],
+                links.over_y,
+            ),
+        )
+
+    def seconds(self, c):
+        links = self.links
+        return (
+            remote(
+                self.r1a.at[c, 1 - links.y],
+                self.r2a.at[c],
+                self.s2.at[c, 0],
+                self.q2.at[c, 0],
+                links.over_y,
+            ),
+            remote(
+                self.r1b.at[c, 1 - links.x],
+                self.r2b.at[c],
+                self.s2.at[c, 1],
+                self.q2.at[c, 1],
+                links.over_x,
+            ),
+        )
+
+    def along(self, item, slot, c):
+        device = self.links.to_far if slot == 2 else self.links.to_pair
+        return remote(
+            self.tot.at[c],
+            self.rz.at[item, slot],
+            self.zs.at[item, slot],
+            self.zr.at[item, slot],
+            device,
+        )
+
+    def core(self, c, base=0, w_ref=None, mine=None):
+        if mine is None:
+            self.local(w_ref, c, base).wait()
+            mine = self.own[c]
+        self.over_core(c, self.rc.at[c]).wait_recv()
+        self.own[c] = mine + self.rc[c]
+        for copy in self.firsts(c):
+            copy.start()
+
+    def first(self, c):
+        for copy in self.firsts(c):
+            copy.wait_recv()
+        links, half = self.links, self.half
+        for other in range(2):
+            self.r1a[c, other] = self.r1a[c, other] + self.own[c, other, links.x, :, :half]
+            self.r1b[c, other] = self.r1b[c, other] + self.own[c, links.y, other, :, half:]
+        for copy in self.seconds(c):
+            copy.start()
+
+    def second(self, c):
+        for copy in self.seconds(c):
+            copy.wait_recv()
+        links, half = self.links, self.half
+        self.tot[c, :, :half] = self.r1a[c, links.y] + self.r2a[c]
+        self.tot[c, :, half:] = self.r1b[c, links.x] + self.r2b[c]
+        item, k = c // 4, c % 4
+        for slot in range(2):
+
+            @pl.when(k == slot)
+            def _(slot=slot):
+                self.along(item, slot, c).start()
+
+        @pl.when(k == 2)
+        def _():
+            self.along(item, 0, c).wait_recv()
+            self.tot[c] = self.tot[c] + self.rz[item, 0]
+            self.along(item, 2, c).start()
+
+    def finish(self, item):
+        c = 4 * item
+        for slot in (1, 2):
+            self.along(item, slot, c).wait_recv()
+        total = self.tot[c + 3].astype(F32)
+        return total + self.rz[item, 1].astype(F32) + self.rz[item, 2].astype(F32)
+
+    def drain(self):
+        def body(c, carry):
+            self.over_core(c, self.rc.at[c]).wait_send()
+            for copy in self.firsts(c) + self.seconds(c):
+                copy.wait_send()
+            return carry
+
+        lax.fori_loop(0, self.chunks, body, 0)
+        for item in range(self.chunks // 4):
+            for slot in range(3):
+                self.along(item, slot, 4 * item).wait_send()
+
+
+class Rows:
+    @staticmethod
+    def scratch(rows, width):
+        dma = pltpu.SemaphoreType.DMA
+        return [
+            pltpu.VMEM((4, rows, width), BF16),
+            pltpu.VMEM((3, rows, width), BF16),
+            dma((3,)),
+            dma((3,)),
+        ]
+
+    count = 4
+
+    def __init__(self, links, refs):
+        self.links = links
+        self.buf, self.rx, self.ss, self.rs = refs
+
+    def copy(self, slot):
+        links = self.links
+        block = (links.cross, links.pair, links.far)[slot]
+        device = links.to_far if slot == 2 else links.to_pair
+        return remote(
+            self.buf.at[block], self.rx.at[slot], self.ss.at[slot], self.rs.at[slot], device
+        )
+
+    def start(self):
+        self.copy(0).start()
+        self.copy(1).start()
+
+    def middle(self):
+        self.copy(0).wait_recv()
+        far = self.links.far
+        self.buf[far] = self.buf[far] + self.rx[0]
+        self.copy(2).start()
+
+    def finish(self):
+        for slot in (1, 2):
+            self.copy(slot).wait_recv()
+        return self.rx[1].astype(F32) + self.rx[2].astype(F32)
+
+    def drain(self):
+        for slot in range(3):
+            self.copy(slot).wait_send()
+
+
+def head_grads(qw, kw, vw, dcw, lse_tile, bias, keep, lanes):
+    block, group = qw.shape[0], len(lanes)
+    qcat, dcat = stack_heads(qw, lanes), stack_heads(dcw, lanes)
+    sc = nt(qcat, kw)
+    if bias is not None:
+        sc = sc + bias
+    sc = jnp.where(keep, sc, NEG)
+    lse = jnp.concatenate([lse_tile[:, a : a + 1] for a in range(group)], axis=0)
+    p = jnp.exp(sc - lse)
+    dp = nt(dcat, vw)
+    ds = (p * (dp - jnp.sum(p * dp, axis=-1, keepdims=True))).astype(BF16)
+    dq = join_heads(nn(ds, kw), lanes, block).astype(BF16)
+    dk = tn(ds, qcat).astype(BF16)
+    dv = tn(p.astype(BF16), dcat).astype(BF16)
+    return ds, dq, dk, dv
+
+
+def diagonal_line(near, far_sum):
+    block, width = near.shape
+    half = block // 2
+    while half >= 8:
+        near = near[:half] + pltpu.roll(near[half:], width - half, 1)
+        half //= 2
+    row8 = lax.broadcasted_iota(jnp.int32, (8, width), 0)
+    for bit in (4, 2, 1):
+        near = jnp.where((row8 & bit) != 0, pltpu.roll(near, width - bit, 1), near)
+    line = jnp.sum(near, axis=0, keepdims=True)
+    lane = lax.broadcasted_iota(jnp.int32, (1, width), 1)
+    return line + jnp.where(lane == width - 1, far_sum, 0.0)
+
+
+def linked_kernel(biased, group, size, order, *refs):
+    (len_ref, nq_ref, nk_ref, q_ref, k_ref, v_ref, c_ref, lse_ref, wq_ref, wkv_ref, wo_ref) = refs[:11]
+    dy_ref, gain_ref, given_ref, refs = refs[11], refs[12], refs[13], refs[14:]
+    if biased:
+        bias_ref, x_ref, rows_ref, lines_ref, grad_ref, mem_ref, given_out, own_out, small_out, *refs = refs
+    else:
+        y_ref, dprev_ref, gg_ref, w_ref, later_ref, mem_ref, given_out, *refs = refs
+    dq_ref, dkv_ref, acck_ref, accq_ref, nqt_ref, nkt_ref, dat_ref, *refs = refs
+    links = Links()
+    sums = Sums(links, refs[: Sums.count])
+    refs = refs[Sums.count :]
+    exchanges = []
+    for _ in range(3 if biased else 1):
+        exchanges.append(Rows(links, refs[: Rows.count]))
+        refs = refs[Rows.count :]
+    if biased:
+        ds_ref, ext_ref, wtmp_ref, diag_ref, sr, ms, mr = refs
+    shards, rows, pw = q_ref.shape
+    seqs = len_ref.shape[0]
+    block = rows // seqs
+    full = k_ref.shape[1] // seqs
+    win = group * size
+    lanes = lane_groups(pw, group, size)
+    key = lax.broadcasted_iota(jnp.int32, (1, full), 1)
+    me = links.me
+    start = pl.multiple_of(me * block, block)
+    ready = 4 if biased else 8
+    lag = 1 if biased else 0
+
+    links.greet()
+    for c in range(ready):
+        sums.load(given_ref, c)
+    if biased:
+        exchanges[0].buf[...] = rows_ref[...]
+        exchanges[0].start()
+
+    def core(c):
+        if biased:
+
+            @pl.when(c < ready)
+            def _():
+                sums.core(c, w_ref=given_ref)
+
+            @pl.when(c >= ready)
+            def _():
+                sums.core(c, mine=wtmp_ref[c - ready, links.core])
+
+        else:
+            sums.core(c, w_ref=given_ref)
+
+    def tick(t):
+        for stage, late in ((core, 0), (sums.first, 1), (sums.second, 3)):
+            c = t - lag - late
+
+            @pl.when((c >= 0) & (c < sums.chunks))
+            def _(stage=stage, c=c):
+                stage(c)
+
+    da = dy_ref[...].astype(BF16)
+    put_rows(nqt_ref, nq_ref[...].T, order)
+    put_rows(nkt_ref, nk_ref[...].T, order)
+    put_rows(dat_ref, da.T, order)
+    if biased:
+        ext_ref[:, :block] = jnp.zeros((block, block), F32)
+        far = lax.broadcasted_iota(jnp.int32, ext_ref.shape, 1) < start
+
+    for s in range(seqs):
+        mine = slice(s * block, (s + 1) * block)
+        theirs = slice(s * full, (s + 1) * full)
+
+        def body(k, carry):
+            h = links.owner(k)
+            wo_h = wo_ref[pl.ds(pl.multiple_of(h * win, size), win), :]
+            dcw = padded(nt(da[mine], wo_h).astype(BF16), pw)
+            bias = None
+            if biased:
+                bias = bias_ref[pl.ds(h * group, group)].reshape(group * block, full)
+            ds, dq, dk, dv = head_grads(
+                q_ref[h, mine, :],
+                k_ref[h, theirs, :],
+                v_ref[h, theirs, :],
+                dcw,
+                lse_ref[h, s],
+                bias,
+                key < len_ref[s],
+                lanes,
+            )
+            dkv = jnp.concatenate([dk[:, :win], dv[:, :win]], axis=1)
+            dkv_ref[h, theirs, :] = dkv
+            dq_ref[h, mine, :] = dq
+            kv_term = nn(dkv[:, :win], wkv_ref[h, 0]) + nn(dkv[:, win:], wkv_ref[h, 1])
+            q_term = nn(dq[:, :win], wq_ref[h])
+
+            @pl.when(k == 0)
+            def _():
+                acck_ref[...] = kv_term
+                accq_ref[mine, :] = q_term
+
+            @pl.when(k != 0)
+            def _():
+                acck_ref[...] += kv_term
+                accq_ref[mine, :] += q_term
+
+            if biased and s < seqs - 1:
+                ds_ref[h] = ds if s == 0 else ds_ref[h] + ds
+            if biased and s == seqs - 1:
+                whole = ds_ref[h].astype(F32) + ds.astype(F32)
+                for a in range(group):
+                    ext_ref[:, block:] = whole[a * block : (a + 1) * block, :]
+                    far_sum = jnp.sum(jnp.where(far, ext_ref[...], 0.0))
+                    near = ext_ref[:, pl.ds(start, 2 * block)]
+                    diag_ref[pl.ds(h * group + a, 1), :] = diagonal_line(near, far_sum)
+            if s == seqs - 1:
+                dkv = dkv_ref[h]
+                w = jnp.concatenate(
+                    [
+                        nn(nkt_ref[...], dkv).astype(BF16),
+                        nn(nqt_ref[...], dq_ref[h][:, :win]).astype(BF16),
+                        nn(dat_ref[...], c_ref[h][:, :win]).astype(BF16),
+                    ],
+                    axis=1,
+                ).reshape(2, 2, 2, w_rows, 4 * win)
+                if biased:
+                    wtmp_ref[k] = w
+                    sums.over_core(ready + k, wtmp_ref.at[k, 1 - links.core]).start()
+                else:
+                    w_ref[h] = w
+            tick(4 * s + k)
+            return carry
+
+        w_rows = nqt_ref.shape[0] // 8
+        lax.fori_loop(0, shards, body, 0)
+        if biased:
+            acck_ref[pl.ds(start, block), :] += accq_ref[mine, :]
+            total = acck_ref[...]
+            part = jnp.sum(total * nk_ref[theirs, :].astype(F32), axis=0, keepdims=True)
+            gain1 = part if s == 0 else gain1 + part
+            mover = exchanges[1 + s]
+            mover.buf[...] = total.astype(BF16).reshape(shards, block, -1)
+            mover.start()
+            grad_ref[mine, :] = acck_ref[pl.ds(start, block), :]
+            if s == 0:
+                exchanges[0].middle()
+        elif s == 0:
+            exchanges[0].buf[...] = acck_ref[...].astype(BF16).reshape(shards, block, -1)
+            exchanges[0].start()
+            mem_ref[...] = acck_ref[pl.ds(start, block), :]
+        else:
+            later_ref[...] = acck_ref[...].astype(BF16).reshape(shards, block, -1)
+
+    steps = range(4 * seqs, lag + sums.chunks + 3)
+    if not biased:
+        exchanges[0].middle()
+        dy, gg = norm_grads(y_ref[...], gain_ref[...], accq_ref[...])
+        dprev_ref[...] = dy_ref[...] + dy
+        gg_ref[...] = gg
+        for t in steps:
+            tick(t)
+        mem_ref[...] += exchanges[0].finish()
+        for item in range(sums.chunks // 4):
+            cols = slice(item * sums.cols, (item + 1) * sums.cols)
+            given_out[:, cols] = sums.finish(item)
+    else:
+        gain1 = gain1 / gain_ref[...]
+        width = gain1.shape[1]
+        exchanges[1].middle()
+        diag_ref[shards * group :, :] = jnp.zeros_like(diag_ref[shards * group :, :])
+        lines = lines_ref.shape[0]
+        sr[0, : diag_ref.shape[0], :] = diag_ref[...]
+        sr[0, diag_ref.shape[0] :, :] = lines_ref[...]
+        for j in range(width // (2 * block)):
+            row = diag_ref.shape[0] + j
+            sr[0, row : row + 1, :] = gain1[:, j * 2 * block : (j + 1) * 2 * block]
+        hops = [links.over_core, links.over_x, links.over_y, links.to_pair, links.to_far]
+
+        def hop(i):
+            return remote(sr.at[i], sr.at[len(hops) + 1 + i], ms.at[i], mr.at[i], hops[i])
+
+        hop(0).start()
+        for i in range(max(len(steps), len(hops))):
+            if i < len(steps):
+                tick(steps[i])
+            if i < len(hops):
+                hop(i).wait_recv()
+                sr[i + 1] = sr[i] + sr[len(hops) + 1 + i]
+                if i + 1 < len(hops):
+                    hop(i + 1).start()
+            if i == 1:
+                exchanges[2].middle()
+        small_out[...] = sr[len(hops)]
+        mem_ref[...] = exchanges[0].buf[me].astype(F32) + exchanges[0].finish()
+        given_out[...] = sums.finish(0)
+        for s in range(seqs):
+            mine = slice(s * block, (s + 1) * block)
+            dn = grad_ref[mine, :] + exchanges[1 + s].finish()
+            dx, _ = norm_grads(x_ref[mine, :].astype(F32), gain_ref[...], dn)
+            grad_ref[mine, :] = dy_ref[mine, :] + dx
+        own_out[...] = sums.finish(1)
+        for i in range(len(hops)):
+            hop(i).wait_send()
+    for mover in exchanges:
+        mover.drain()
+    sums.drain()
+
+
+def linked_backward(lens, nq, nk, saved, wq, wkv, wo, dy, gain, given, extras, biased, group, size, order):
+    q, k, v, c, lse = saved
+    rows, width = nq.shape
+    shards, keys, pw = k.shape
+    seqs = lens.shape[0]
+    block, full, win = rows // seqs, keys // seqs, group * size
+    cols = 4 * win
+    share = width // 8
+    given = given.reshape(shards, 2, 2, 2, share, -1)
+    args = [lens, nq, nk, q, k, v, c, lse, wq, wkv, wo, dy, gain, given, *extras]
+    chunks = 8
+    if biased:
+        lines = extras[3].shape[0]
+        diag_rows = -(-shards * group // 8) * 8
+        out_shape = [
+            sds((rows, width), F32),
+            sds((block, width), F32),
+            sds((share, cols), F32),
+            sds((share, cols), F32),
+            sds((diag_rows + lines, 2 * block), F32),
+        ]
+    else:
+        out_shape = [
+            sds((rows, width), F32),
+            sds((1, width), F32),
+            sds((shards, 2, 2, 2, share, cols), BF16),
+            sds((shards, block, width), BF16),
+            sds((block, width), F32),
+            sds((share, given.shape[-1]), F32),
+        ]
+    scratch = [
+        pltpu.VMEM((shards, rows, pw), BF16),
+        pltpu.VMEM((shards, keys, 2 * win), BF16),
+        pltpu.VMEM((full, width), F32),
+        pltpu.VMEM((rows, width), F32),
+        pltpu.VMEM((width, rows), BF16),
+        pltpu.VMEM((width, keys), BF16),
+        pltpu.VMEM((width, rows), BF16),
     ]
-    shards = w_refs[0].shape[0]
-    cols = own.shape[-1]
-    half = cols // 2
-    b, me, core, x, y = place()
-    over_core, over_x, over_y, across, ahead = near_devices(b, me, core, x, y, shards)
-    greet([over_core, over_x, over_y] + ahead)
-    chunks = [(i, k) for i in range(len(items)) for k in range(shards)]
-    owner = [lax.rem(me + 1 + k, shards) for k in range(shards)]
-    started = []
-
-    def start(copy):
-        copy.start()
-        started.append(copy)
-        return copy
-
-    small = [start(remote(small_ref, sr.at[0], ms.at[0], mr.at[0], over_core))]
-    load, first, second, third, last = {}, {}, {}, {}, {}
-
-    def stage_load(c):
-        i, k = chunks[c]
-        w, col = items[i]
-        piece = lambda side: w_refs[w].at[owner[k], side, :, :, :, pl.ds(col, cols)]
-        load[c] = pltpu.make_async_copy(piece(core), own.at[c], lsem.at[c])
-        load[c].start()
-        first[c] = start(remote(piece(1 - core), rc.at[c], cs.at[c], cr.at[c], over_core))
-
-    def stage_core(c):
-        load[c].wait()
-        first[c].wait_recv()
-        own[c] = own[c] + rc[c]
-        second[c] = [
-            start(
-                remote(
-                    own.at[c, :, 1 - x, :, pl.ds(0, half)],
-                    r1a.at[c],
-                    s1.at[c, 0],
-                    q1.at[c, 0],
-                    over_x,
-                )
-            ),
-            start(
-                remote(
-                    own.at[c, 1 - y, :, :, pl.ds(half, half)],
-                    r1b.at[c],
-                    s1.at[c, 1],
-                    q1.at[c, 1],
-                    over_y,
-                )
-            ),
+    scratch += Sums.scratch(chunks, share, cols)
+    for _ in range(3 if biased else 1):
+        scratch += Rows.scratch(block, width)
+    if biased:
+        dma = pltpu.SemaphoreType.DMA
+        scratch += [
+            pltpu.VMEM((shards, group * block, full), BF16),
+            pltpu.VMEM((block, full + block), F32),
+            pltpu.VMEM((shards, 2, 2, 2, share, cols), BF16),
+            pltpu.VMEM((diag_rows, 2 * block), F32),
+            pltpu.VMEM((11, diag_rows + lines, 2 * block), F32),
+            dma((5,)),
+            dma((5,)),
         ]
-
-    def stage_first(c):
-        for copy in second[c]:
-            copy.wait_recv()
-        for other in range(2):
-            r1a[c, other] = r1a[c, other] + own[c, other, x, :, :half]
-            r1b[c, other] = r1b[c, other] + own[c, y, other, :, half:]
-        third[c] = [
-            start(remote(r1a.at[c, 1 - y], r2a.at[c], s2.at[c, 0], q2.at[c, 0], over_y)),
-            start(remote(r1b.at[c, 1 - x], r2b.at[c], s2.at[c, 1], q2.at[c, 1], over_x)),
-        ]
-
-    def stage_second(c):
-        i, k = chunks[c]
-        for copy in third[c]:
-            copy.wait_recv()
-        tot[c, :, :half] = r1a[c, y] + r2a[c]
-        tot[c, :, half:] = r1b[c, x] + r2b[c]
-        if k < shards - 1:
-            last[i, k] = start(
-                remote(tot.at[c], rz.at[i, k], zs.at[i, k], zr.at[i, k], (b, owner[k]))
-            )
-
-    for c in range(len(chunks)):
-        stage_load(c)
-    for t in range(len(chunks) + 3):
-        if t < len(chunks):
-            stage_core(t)
-        if t == 0:
-            small[0].wait_recv()
-            sr[6] = small_ref[...] + sr[0]
-            small.append(start(remote(sr.at[6], sr.at[1], ms.at[1], mr.at[1], over_x)))
-        if t == 2:
-            small[1].wait_recv()
-            sr[7] = sr[6] + sr[1]
-            small.append(start(remote(sr.at[7], sr.at[2], ms.at[2], mr.at[2], over_y)))
-        if t == 4:
-            small[2].wait_recv()
-            sr[8] = sr[7] + sr[2]
-            for k in range(shards - 1):
-                small.append(
-                    start(remote(sr.at[8], sr.at[3 + k], ms.at[3 + k], mr.at[3 + k], ahead[k]))
-                )
-        if 0 <= t - 1 < len(chunks):
-            stage_first(t - 1)
-        if 0 <= t - 3 < len(chunks):
-            stage_second(t - 3)
-    total = sr[8]
-    for k in range(shards - 1):
-        small[3 + k].wait_recv()
-        total = total + sr[3 + k]
-    small_out[...] = total
-    for i, (w, col) in enumerate(items):
-        total = tot[i * shards + shards - 1].astype(F32)
-        for k in range(shards - 1):
-            last[i, k].wait_recv()
-            total = total + rz[i, k].astype(F32)
-        out_refs[w][:, col : col + cols] = total
-    for copy in started:
-        copy.wait_send()
-
-
-def reduce_blocks(arrays, small, cols):
-    shards, tall = arrays[0].shape[:2]
-    rows = tall // 8
-    items = [(w, col) for w, a in enumerate(arrays) for col in range(0, a.shape[2], cols)]
-    n = len(items) * shards
-    half = cols // 2
-    anywhere = pl.BlockSpec(memory_space=pl.ANY)
-    dma = pltpu.SemaphoreType.DMA
+    in_specs = [smem()] + [vmem()] * (len(args) - 1)
+    in_specs[13] = pl.BlockSpec(memory_space=pl.ANY)
     return pl.pallas_call(
-        functools.partial(reduce_kernel, items, len(arrays)),
-        out_shape=[sds((rows, a.shape[2]), F32) for a in arrays] + [sds(small.shape, F32)],
-        in_specs=[anywhere] * len(arrays) + [vmem()],
-        out_specs=[vmem()] * (len(arrays) + 1),
-        scratch_shapes=[
-            pltpu.VMEM((n, 2, 2, rows, cols), BF16),
-            pltpu.VMEM((n, 2, 2, rows, cols), BF16),
-            pltpu.VMEM((n, 2, rows, half), BF16),
-            pltpu.VMEM((n, 2, rows, half), BF16),
-            pltpu.VMEM((n, rows, half), BF16),
-            pltpu.VMEM((n, rows, half), BF16),
-            pltpu.VMEM((n, rows, cols), BF16),
-            pltpu.VMEM((len(items), shards - 1, rows, cols), BF16),
-            pltpu.VMEM((9, *small.shape), F32),
-            dma((n,)),
-            dma((n,)),
-            dma((n,)),
-            dma((n, 2)),
-            dma((n, 2)),
-            dma((n, 2)),
-            dma((n, 2)),
-            dma((len(items), shards - 1)),
-            dma((len(items), shards - 1)),
-            dma((6,)),
-            dma((6,)),
-        ],
+        functools.partial(linked_kernel, biased, group, size, order),
+        out_shape=out_shape,
+        in_specs=in_specs,
+        out_specs=[vmem()] * len(out_shape),
+        scratch_shapes=scratch,
         compiler_params=pltpu.CompilerParams(
-            collective_id=1, has_side_effects=True, vmem_limit_bytes=VMEM_LIMIT
+            collective_id=2 if biased else 1, has_side_effects=True, vmem_limit_bytes=VMEM_LIMIT
         ),
-        name="reduce_blocks",
-    )(*[a.reshape(shards, 2, 2, 2, rows, a.shape[2]) for a in arrays], small)
+        name="self_backward" if biased else "cross_backward",
+    )(*args)
 
 
 def per_device(
@@ -836,7 +1208,7 @@
     n1_all = lax.all_gather(n1.reshape(seqs, block, width), "head", axis=1, tiled=True)
     n1_all = n1_all.reshape(seqs * full, width)
 
-    tight = batch_count == 8 and shards == 4
+    tight = batch_count == 8 and shards == 4 and seqs == 2
     order = tuple((i % 2) * 4 + i // 2 for i in range(8)) if tight else (0,)
     table = jnp.pad(rel_bias, ((0, 0), (0, 128 - group)))
     flip = lambda w: jnp.swapaxes(w, -1, -2)
@@ -863,25 +1235,36 @@
     result, dy2, gain3, feed_w = feed(
         y2, n3, out_cotangent.reshape(rows, width), feed_in, feed_out, fg, shards, order
     )
-    memory_part, gain2, cross_w, dy1 = attend_backward(
-        enc_lengths, me, n2, memory_all, saved2, wq2, wkv2, wo2, dy2, cg, y1, False, group, size, order
-    )
-    input_part, gain1, self_w, diag = attend_backward(
-        dec_lengths, me, n1, n1_all, saved1, wq1, wkv1, wo1, dy1, sg, bias, True, group, size, order
-    )
-
-    memory_grad = lax.psum_scatter(
-        memory_part.reshape(seqs, enc_full, width), "head", scatter_dimension=1, tiled=True
-    ).astype(F32)
-    dn1 = lax.psum_scatter(
-        input_part.reshape(seqs, full, width), "head", scatter_dimension=1, tiled=True
-    ).astype(F32)
-    lines = jnp.concatenate([gain1, gain2, gain3], axis=0).reshape(-1, 2 * block)
-    spare = -(lines.shape[0] + diag.shape[0]) % 8
-    small = jnp.concatenate([lines, diag, jnp.zeros((spare, 2 * block), F32)], axis=0)
+    gain_rows = width // (2 * block)
     if tight:
-        feed_w, cross_w, self_w, small = reduce_blocks([feed_w, cross_w, self_w], small, 4 * win)
+        dy1, gain2, cross_w, memory_later, memory_first, feed_w = linked_backward(
+            enc_lengths, n2, memory_all, saved2, wq2, wkv2, wo2, dy2, cg, feed_w, [y1],
+            False, group, size, order,
+        )
+        lines = jnp.concatenate([jnp.zeros((1, width), F32), gain2, gain3], axis=0)
+        lines = lines.reshape(-1, 2 * block)
+        lines = jnp.pad(lines, ((0, -lines.shape[0] % 8), (0, 0)))
+        input_grad, memory_last, cross_w, self_w, small = linked_backward(
+            dec_lengths, n1, n1_all, saved1, wq1, wkv1, wo1, dy1, sg, cross_w,
+            [bias, x, memory_later, lines], True, group, size, order,
+        )
+        memory_grad = jnp.stack([memory_first, memory_last])
+        diag, lines = small[: -lines.shape[0]], small[-lines.shape[0] :]
     else:
+        memory_part, gain2, cross_w, dy1 = attend_backward(
+            enc_lengths, me, n2, memory_all, saved2, wq2, wkv2, wo2, dy2, cg, y1,
+            False, group, size, order,
+        )
+        input_part, gain1, self_w, diag = attend_backward(
+            dec_lengths, me, n1, n1_all, saved1, wq1, wkv1, wo1, dy1, sg, bias,
+            True, group, size, order,
+        )
+        memory_grad = lax.psum_scatter(
+            memory_part.reshape(seqs, enc_full, width), "head", scatter_dimension=1, tiled=True
+        ).astype(F32)
+        dn1 = lax.psum_scatter(
+            input_part.reshape(seqs, full, width), "head", scatter_dimension=1, tiled=True
+        ).astype(F32)
         feed_w, cross_w, self_w = (
             lax.psum_scatter(
                 w.reshape(shards * width, w.shape[2]).astype(F32),
@@ -891,12 +1274,13 @@
             )
             for w in (feed_w, cross_w, self_w)
         )
-        small = lax.psum(small, ("batch", "head"))
-    gains = small[: lines.shape[0]].reshape(3, width)
-    diag = lax.dynamic_slice_in_dim(small, lines.shape[0] + me[0] * group, group, 0)
+        lines = jnp.concatenate([gain1, gain2, gain3], axis=0).reshape(-1, 2 * block)
+        diag, lines = lax.psum((diag, lines), ("batch", "head"))
+        dx, _ = norm_grads(x32, sg, dn1.reshape(rows, width))
+        input_grad = dy1 + dx
+    gains = lines[: 3 * gain_rows].reshape(3, width)
+    diag = lax.dynamic_slice_in_dim(diag, me[0] * group, group, 0)
     table_grad = jnp.einsum("tb,ht->bh", onehot, diag, precision=highest)
-    dx, _ = norm_grads(x32, sg, dn1.reshape(rows, width))
-    input_grad = (dy1 + dx).reshape(seqs, block, width)
 
     def split(w):
         kv = jnp.stack([w[:, :win], w[:, win : 2 * win]])
@@ -906,7 +1290,7 @@
     cross_q, cross_kv, cross_o = split(cross_w)
     return (
         result.reshape(seqs, block, width),
-        input_grad,
+        input_grad.reshape(seqs, block, width),
         memory_grad,
         gains[0],
         self_q,

time: 338 us -> 305 us (0.902); the launches traced: 333 us -> 304 us
  Pallas kernels: 291 us -> 265 us
  other arithmetic: 13.5 us -> 9.13 us
    pallas_call x3 -> x2, Pallas kernels: 165 us -> 139 us  [linked_backward(): pl.pallas_call(functools.partial(linked_kernel, biased, group, size, orde...]
  transfers between devices with their start and end apart: 4 -> 2, of which waited for: 0 -> 0; matrix products, arithmetic and copies ran while one was open for 6% -> 2% of each run, Pallas kernels for 62% -> 32%
where the time goes in v3:
time: 305 us; the launch traced here: 304 us
  Pallas kernels  265 us (87%)
  local copies, waits for them, and re-layouts  14.3 us (5%)
  between operations  14.1 us (5%)
  other arithmetic  9.13 us (3%)
    pallas_call x2, Pallas kernels, linked_backward(): pl.pallas_call(functools.partial(linked_kernel, biased, group, size, orde...  139 us
    pallas_call x1, Pallas kernels, gather_weights(): pl.pallas_call(functools.partial(gather_kernel, n), out_shape=[sds((shard...  79.7 us
    pallas_call x2, Pallas kernels, attend_forward(): pl.pallas_call(functools.partial(forward_kernel, bias is not None, group,...  28.4 us
    pallas_call x1, Pallas kernels, feed(): pl.pallas_call(functools.partial(feed_kernel, order), grid=(shards,), out...  13.7 us
  transfers between devices with their start and end apart: 2, of which 0 were waited for; matrix products, arithmetic and copies ran while one was open for 2% of the time, Pallas kernels for 32%

profile of v3, /device:TPU:0, one launch (start us, length us, event | category | flops | bytes accessed | tf_op | source)
XLA Modules:
  0.0 304.4 jit_solution(16484965236923235956)
XLA Ops:
  7.2 0.0 all-gather.3.cloned.1.call-start
  7.2 0.7 convert_element_type.165
  7.9 1.2 fusion
  9.1 1.9 fusion.2
  11.0 0.0 all-gather.3.cloned.1.call-update
  11.0 0.0 all-gather.5.cloned.1.call-start
  11.1 0.7 all-gather.5.cloned.1.call-update
  11.8 1.3 reshape.177.refs_12_
  13.0 0.8 copy.32
  13.8 1.3 reshape.181.gain_ref.refs_12_
  15.1 1.3 reshape.183.gain_ref
  16.3 0.6 pad.8.refs_6_
  16.9 79.7 %gather_weights.1 = (bf16[4,1,192,768]{3,2,1,0:T(8,128)(2,1)}, bf16[4,2,192,768]{3,2,1,0:T(8,128)(2,1)}, bf16[4,1,192,768]{3,2,1,0:T(8,128)(2,1)}, bf16[4,1,192,...) custom-call(bf16[1,192,768]{2,1,0:T(8,128)(2,1)} %bitcast.66, ...), custom_call_target="tpu_custom_call" | custom-call | tf_op jit(solution)/shard_map/gather_weights/pallas_call | solution.py:617
  96.6 0.0 copy-start
  96.7 0.6 convert_convert_fusion.onehot_ref
  97.3 4.1 %bias_tiles.1.rest_0_.refs_14_ = f32[12,128,512]{2,1,0:T(8,128)} custom-call(s32[1]{0:T(128)} %bitcast.13.me_ref, bf16[4,32,128]{2,1,0:T(8,128)(2,1)} %get-tuple-element.54.table_ref, bf16[32,256]{1,0:T(8,128)(2,1)} %convert_convert_fusion.onehot_ref), custom_call_target="tpu_custom_call" | custom-call | tf_op jit(solution)/shard_map/bias_tiles/pallas_call | solution.py:137
  101.4 0.0 copy-done
  101.4 0.9 multiply_convert_fusion.nq_ref.refs_1_
  102.3 14.6 %attend_forward.2 = (bf16[4,256,256]{2,1,0:T(8,128)(2,1)}, bf16[4,1024,256]{2,1,0:T(8,128)(2,1)}, bf16[4,1024,256]{2,1,0:T(8,128)(2,1)}, bf16[4,256,256]{2,1,0:T...) custom-call(s32[2]{0:T(128)} %refs_0_.3, ...), custom_call_target="tpu_custom_call" | custom-call | flops 3825205248 | bytes 16777216 | tf_op jit(solution)/shard_map/attend_forward/pallas_call | solution.py:222
  116.9 0.0 all-gather.5.cloned.1.call-done
  116.9 13.8 %attend_forward.3 = (bf16[4,256,256]{2,1,0:T(8,128)(2,1)}, bf16[4,1024,256]{2,1,0:T(8,128)(2,1)}, bf16[4,1024,256]{2,1,0:T(8,128)(2,1)}, bf16[4,256,256]{2,1,0:T...) custom-call(s32[2]{0:T(128)} %refs_0_.2, ...), custom_call_target="tpu_custom_call" | custom-call | flops 3825205248 | bytes 16777216 | tf_op jit(solution)/shard_map/attend_forward/pallas_call | solution.py:222
  130.8 13.7 %feed.1 = (bf16[256,768]{1,0:T(8,128)(2,1)}, f32[256,768]{1,0:T(8,128)}, f32[1,768]{1,0:T(1,128)}, bf16[4,768,1536]{2,1,0:T(8,128)(2,1)}) custom-call(f32[256,768]{1,0:T(8,128)} %get-tuple-element.60.y_ref, bf16[256,768]{1,0:T(8,128)(2,1)} %get-tuple-element.61.n_ref, bf16[256,768]{1,0:T(8,128)(2,1)} %bitcast.70, bf16[2,768,2048]{2,1,0:T(8,128)(2,1)} %win_ref.1, ...), custom_call_target="tpu_custom_call" | custom-call | flops 7247757312 | bytes 25165824 | tf_op jit(solution)/shard_map/feed/pallas_call | solution.py:469
  144.4 61.5 %cross_backward.1 = (f32[256,768]{1,0:T(8,128)}, f32[1,768]{1,0:T(1,128)}, bf16[4,2,2,2,96,768]{5,4,3,2,1,0:T(8,128)(2,1)}, bf16[4,128,768]{2,1,0:T(8,128)(2,1)}...) custom-call(s32[2]{0:T(128)} %refs_0_.2, bf16[256,768]{1,0:T(8,128)(2,1)} %get-tuple-element.55.nq_ref.refs_1_, ...), custom_call_target="tpu_custom_call" | custom-call | tf_op jit(solution)/shard_map/cross_backward/pallas_call | solution.py:1160
  205.9 0.0 copy-done.5
  205.9 0.8 pad_maximum_fusion.4
  206.7 0.6 pad.9.refs_17_
  207.3 77.9 %self_backward.1 = (f32[256,768]{1,0:T(8,128)}, f32[128,768]{1,0:T(8,128)}, f32[96,768]{1,0:T(8,128)}, f32[96,768]{1,0:T(8,128)}, f32[32,256]{1,0:T(8,128)}) custom-call(s32[2]{0:T(128)} %refs_0_.3, bf16[256,768]{1,0:T(8,128)(2,1)} %multiply_convert_fusion.nq_ref.refs_1_, bf16[1024,768]{1,0:T(8,128)(2,1)} %bitcast.50, ...), custom_call_target="tpu_custom_call" | custom-call | tf_op jit(solution)/shard_map/self_backward/pallas_call | solution.py:1160
  285.2 0.0 copy-start.2
  285.2 0.0 copy-start.3
  285.2 0.0 copy-start.4
  285.2 0.8 fusion.23
  286.1 0.7 slice.59
  286.8 0.6 squeeze.17
  287.4 2.0 slice_bitcast_fusion.3
  289.4 0.7 copy.33
  290.1 0.6 squeeze.18
  290.7 0.7 copy.34
  291.5 0.6 squeeze.19
  292.1 0.0 copy-done.2
  292.1 0.7 slice_bitcast_fusion
  292.8 0.0 copy-done.3
  292.8 0.0 copy-done.4
  292.8 0.9 pad_maximum_fusion
  293.7 0.7 pad_maximum_fusion.2
  294.4 0.8 fusion.3
  295.2 0.7 pad_maximum_fusion.3
  295.9 0.8 pad_maximum_fusion.1
  296.7 0.9 copy.36
  (8 shorter events, 0.1 us)
Async XLA Ops:
  7.2 95.2 %all-gather.3.cloned.1.call-start = ((), (), s32[]{:S(2)}) async-start(), calls=%async_computation | async-start | bytes 1966080 | tf_op jit(solution)/shard_map/all_gather | solution.py:1208
  11.0 105.9 %all-gather.5.cloned.1.call-start = ((), (), s32[]{:S(2)}) async-start(), calls=%async_computation.1 | async-start | bytes 1966080 | tf_op jit(solution)/shard_map/all_gather | solution.py:1227
  96.6 4.8 %copy-start = (bf16[2,128,768]{2,1,0:T(8,128)(2,1)S(1)}, bf16[2,128,768]{2,1,0:T(8,128)(2,1)}, u32[]{:S(2)}) copy-start(bf16[2,128,768]{2,1,0:T(8,128)(2,1)} %param.17) | copy-start | bytes 1179652
  144.4 61.5 %copy-start.5 = (f32[1,768]{1,0:T(1,128)S(1)}, f32[1,768]{1,0:T(1,128)}, u32[]{:S(2)}) copy-start(f32[1,768]{1,0:T(1,128)} %get-tuple-element.79) | copy-start | bytes 9220
  285.2 6.9 %copy-start.2 = (f32[96,1536]{1,0:T(8,128)S(1)}, f32[96,1536]{1,0:T(8,128)}, u32[]{:S(2)}) copy-start(f32[96,1536]{1,0:T(8,128)} %get-tuple-element.86) | copy-start | bytes 1769476
  285.2 7.6 %copy-start.3 = (f32[128,768]{1,0:T(8,128)S(1)}, f32[128,768]{1,0:T(8,128)}, u32[]{:S(2)}) copy-start(f32[128,768]{1,0:T(8,128)} %get-tuple-element.81) | copy-start | bytes 1179652
  285.2 7.6 %copy-start.4 = (f32[128,768]{1,0:T(8,128)S(1)}, f32[128,768]{1,0:T(8,128)}, u32[]{:S(2)}) copy-start(f32[128,768]{1,0:T(8,128)} %get-tuple-element.82) | copy-start | bytes 1179652
  292.1 4.6 %copy-start.1 = (f32[256,768]{1,0:T(8,128)S(1)}, f32[256,768]{1,0:T(8,128)}, u32[]{:S(2)}) copy-start(f32[256,768]{1,0:T(8,128)} %get-tuple-element.80) | copy-start | bytes 2359300
Sparse Core Ops, SparseCore 0:
  11.1 64.3 all-gather.2
  77.0 36.2 all-gather.4

commit v4 on v3

--- a/solution.py
+++ b/solution.py
@@ -11,7 +11,7 @@
 NB = 32
 MAX_DIST = 128
 NEG = -1e30
-VMEM_LIMIT = 56 * 1024 * 1024
+VMEM_LIMIT = 60 * 1024 * 1024
 F32 = jnp.float32
 BF16 = jnp.bfloat16
 
@@ -65,7 +65,9 @@
 
 
 def rms(v):
-    return lax.rsqrt(jnp.mean(v * v, axis=-1, keepdims=True) + 1e-06)
+    mean = jnp.mean(v * v, axis=-1, keepdims=True) + 1e-06
+    r = lax.rsqrt(mean)
+    return r * (1.5 - 0.5 * mean * r * r)
 
 
 def norm_grads(y, gain, e):
@@ -105,11 +107,10 @@
     return jax.ShapeDtypeStruct(shape, dtype)
 
 
-def bias_kernel(me_ref, table_ref, onehot_ref, b_ref, ext_ref, line_ref):
+def build_bias(me, table_ref, onehot_ref, b_ref, ext_ref, line_ref):
     heads, block, full = b_ref.shape
     shards = table_ref.shape[0]
     group = heads // shards
-    me = me_ref[0]
     start = pl.multiple_of(me * block, block)
     width = 2 * block
     row_i = lax.broadcasted_iota(jnp.int32, (block, width), 0)
@@ -126,17 +127,21 @@
             )
             ext_ref[...] = jnp.where(far, row[:, width - 1 : width], NEG)
             ext_ref[:, pl.ds(start, width)] = jnp.where(masked, NEG, tile)
-            b_ref[h * group + a] = ext_ref[:, block:]
+            b_ref[h * group + a] = ext_ref[:, block:].astype(BF16)
         return carry
 
     lax.fori_loop(0, shards, body, 0)
+
+
+def bias_kernel(me_ref, *refs):
+    build_bias(me_ref[0], *refs)
 
 
 def bias_tiles(me, tables, onehot, group, block, full):
     shards, buckets, lanes = tables.shape
     return pl.pallas_call(
         bias_kernel,
-        out_shape=sds((shards * group, block, full), F32),
+        out_shape=sds((shards * group, block, full), BF16),
         in_specs=[smem(), vmem(), vmem()],
         out_specs=vmem(),
         scratch_shapes=[
@@ -162,6 +167,25 @@
     for a in range(1, len(lanes)):
         total = total + jnp.where(lanes[a], tall[a * rows : (a + 1) * rows], 0.0)
     return total
+
+
+def head_context(qw, kw, vw, bias, keep, lanes):
+    block, group = qw.shape[0], len(lanes)
+    sc = nt(stack_heads(qw, lanes), kw)
+    if bias is not None:
+        sc = sc + bias
+    sc = jnp.where(keep, sc, NEG)
+    top = jnp.max(sc, axis=-1, keepdims=True)
+    e = jnp.exp(sc - top)
+    total = jnp.sum(e, axis=-1, keepdims=True)
+    p = (e * (1.0 / total)).astype(BF16)
+    c = join_heads(nn(p, vw), lanes, block).astype(BF16)
+    lse = top + jnp.log(total)
+    lane = lax.broadcasted_iota(jnp.int32, (block, 128), 1)
+    tile = jnp.zeros((block, 128), F32)
+    for a in range(group):
+        tile = jnp.where(lane == a, lse[a * block : (a + 1) * block], tile)
+    return c, tile
 
 
 def forward_kernel(
@@ -176,7 +200,6 @@
     full = k_ref.shape[1] // seqs
     win = group * size
     lanes = lane_groups(pw, group, size)
-    lane128 = lax.broadcasted_iota(jnp.int32, (block, 128), 1)
     key = lax.broadcasted_iota(jnp.int32, (1, full), 1)
 
     def body(h, carry):
@@ -184,24 +207,18 @@
         k_ref[h] = padded(nt(nk_ref[...], wkv_ref[h, 0]).astype(BF16), pw)
         v_ref[h] = padded(nt(nk_ref[...], wkv_ref[h, 1]).astype(BF16), pw)
         for s in range(seqs):
-            kw = k_ref[h, s * full : (s + 1) * full, :]
-            vw = v_ref[h, s * full : (s + 1) * full, :]
-            qcat = stack_heads(q_ref[h, s * block : (s + 1) * block, :], lanes)
-            sc = nt(qcat, kw)
+            bias = None
             if biased:
-                sc = sc + b_ref[pl.ds(h * group, group)].reshape(group * block, full)
-            sc = jnp.where(key < len_ref[s], sc, NEG)
-            top = jnp.max(sc, axis=-1, keepdims=True)
-            e = jnp.exp(sc - top)
-            total = jnp.sum(e, axis=-1, keepdims=True)
-            p = (e * (1.0 / total)).astype(BF16)
-            c = join_heads(nn(p, vw), lanes, block)
-            c_ref[h, s * block : (s + 1) * block, :] = c.astype(BF16)
-            lse = top + jnp.log(total)
-            tile = jnp.zeros((block, 128), F32)
-            for a in range(group):
-                tile = jnp.where(lane128 == a, lse[a * block : (a + 1) * block], tile)
-            lse_ref[h, s] = tile
+                bias = b_ref[pl.ds(h * group, group)].reshape(group * block, full).astype(F32)
+            c, lse_ref[h, s] = head_context(
+                q_ref[h, s * block : (s + 1) * block, :],
+                k_ref[h, s * full : (s + 1) * full, :],
+                v_ref[h, s * full : (s + 1) * full, :],
+                bias,
+                key < len_ref[s],
+                lanes,
+            )
+            c_ref[h, s * block : (s + 1) * block, :] = c
         return carry
 
     lax.fori_loop(0, shards, body, 0)
@@ -295,7 +312,7 @@
             dcat = stack_heads(dc_ref[s * block : (s + 1) * block, :], lanes)
             sc = nt(qcat, kw)
             if biased:
-                sc = sc + b_ref[pl.ds(h * group, group)].reshape(group * block, full)
+                sc = sc + b_ref[pl.ds(h * group, group)].reshape(group * block, full).astype(F32)
             sc = jnp.where(key < len_ref[s], sc, NEG)
             lse_tile = lse_ref[h, s]
             lse = jnp.concatenate([lse_tile[:, a : a + 1] for a in range(group)], axis=0)
@@ -515,15 +532,6 @@
     return b, me, core, x, y
 
 
-def near_devices(b, me, core, x, y, shards):
-    over_core = (b + 1 - 2 * core, me)
-    over_x = (b + 2 - 4 * x, me)
-    over_y = (b + 4 - 8 * y, me)
-    across = (b + 2 - 4 * x + 4 - 8 * y, me)
-    ahead = [(b, lax.rem(me + k, shards)) for k in range(1, shards)]
-    return over_core, over_x, over_y, across, ahead
-
-
 def greet(devices):
     barrier = pltpu.get_barrier_semaphore()
     for device in devices:
@@ -542,104 +550,11 @@
     )
 
 
-def gather_kernel(n, *refs):
-    shard_refs, table_ref = refs[:n], refs[n]
-    full_refs, tables_ref = refs[n + 1 : 2 * n + 1], refs[2 * n + 1]
-    (zs, zr, ps, pr, cs, cr, ts, tr, local) = refs[2 * n + 2 :]
-    shards = tables_ref.shape[0]
-    b, me, core, x, y = place()
-    over_core, over_x, over_y, across, ahead = near_devices(b, me, core, x, y, shards)
-    greet([over_core, over_x, over_y, across] + ahead)
-    slot = core * 4 + lax.div(b, 2)
-
-    def window(ref, first, count):
-        step = ref.shape[-2] // 8
-        rows = pl.ds(pl.multiple_of(first * step, step), count * step)
-        return ref.at[:, rows, :]
-
-    started = []
-
-    def start(copy):
-        copy.start()
-        started.append(copy)
-        return copy
-
-    from_z, from_plane, from_core = {}, {}, {}
-    for k in range(1, shards):
-        start(remote(table_ref, tables_ref.at[me], ts.at[k - 1], tr.at[k - 1], ahead[k - 1]))
-    for i in range(n):
-        for k in range(1, shards):
-            from_z[i, k] = start(
-                remote(
-                    window(shard_refs[i], slot, 1),
-                    window(full_refs[i].at[me], slot, 1),
-                    zs.at[i, k - 1],
-                    zr.at[i, k - 1],
-                    ahead[k - 1],
-                )
-            )
-    copies = [pltpu.make_async_copy(table_ref, tables_ref.at[me], local.at[n])]
-    copies += [
-        pltpu.make_async_copy(shard_refs[i], full_refs[i].at[me], local.at[i]) for i in range(n)
-    ]
-    for copy in copies:
-        copy.start()
-    for i in range(n):
-        for k in range(1, shards):
-            from_z[i, k].wait_recv()
-            piece = window(full_refs[i].at[lax.rem(me + shards - k, shards)], slot, 1)
-            for d, device in enumerate((over_x, over_y, across)):
-                from_plane[i, k, d] = start(
-                    remote(piece, piece, ps.at[i, k - 1, d], pr.at[i, k - 1, d], device)
-                )
-    for i in range(n):
-        for k in range(1, shards):
-            for d in range(3):
-                from_plane[i, k, d].wait_recv()
-            half = window(full_refs[i].at[lax.rem(me + shards - k, shards)], core * 4, 4)
-            from_core[i, k] = start(
-                remote(half, half, cs.at[i, k - 1], cr.at[i, k - 1], over_core)
-            )
-    for copy in from_core.values():
-        copy.wait_recv()
-    for k in range(1, shards):
-        started[k - 1].wait_recv()
-    for copy in started:
-        copy.wait_send()
-    for copy in copies:
-        copy.wait()
-
-
-def gather_weights(weights, table, shards):
-    n = len(weights)
-    anywhere = pl.BlockSpec(memory_space=pl.ANY)
-    dma = pltpu.SemaphoreType.DMA
-    return pl.pallas_call(
-        functools.partial(gather_kernel, n),
-        out_shape=[sds((shards, *w.shape), w.dtype) for w in weights]
-        + [sds((shards, *table.shape), table.dtype)],
-        in_specs=[anywhere] * (n + 1),
-        out_specs=[anywhere] * (n + 1),
-        scratch_shapes=[
-            dma((n, shards - 1)),
-            dma((n, shards - 1)),
-            dma((n, shards - 1, 3)),
-            dma((n, shards - 1, 3)),
-            dma((n, shards - 1)),
-            dma((n, shards - 1)),
-            dma((shards - 1,)),
-            dma((shards - 1,)),
-            dma((n + 1,)),
-        ],
-        compiler_params=pltpu.CompilerParams(
-            collective_id=0, has_side_effects=True, vmem_limit_bytes=VMEM_LIMIT
-        ),
-        name="gather_weights",
-    )(*weights, table)
-
-
 def flipped(bit, by):
     return bit + by - 2 * bit * by
+
+
+AHEAD = 2
 
 
 class Links:
@@ -651,6 +566,7 @@
         self.over_core = (b + 1 - 2 * core, me)
         self.over_x = (b + 2 - 4 * x, me)
         self.over_y = (b + 4 - 8 * y, me)
+        self.over_plane = (b + 2 - 4 * x + 4 - 8 * y, me)
         self.to_pair, self.to_far, self.to_cross = (b, self.pair), (b, self.far), (b, self.cross)
 
     def owner(self, k):
@@ -659,7 +575,8 @@
 
     def greet(self):
         greet(
-            [self.over_core, self.over_x, self.over_y, self.to_pair, self.to_far, self.to_cross]
+            [self.over_core, self.over_x, self.over_y, self.over_plane]
+            + [self.to_pair, self.to_far, self.to_cross]
         )
 
 
@@ -697,13 +614,13 @@
         self.chunks, self.cols = self.own.shape[0], self.own.shape[-1]
         self.half = self.cols // 2
 
-    def piece(self, w_ref, c, side, base):
-        start = pl.multiple_of(((c - base) // 4) * self.cols, self.cols)
-        return w_ref.at[self.links.owner((c - base) % 4), side, :, :, :, pl.ds(start, self.cols)]
-
-    def local(self, w_ref, c, base):
+    def piece(self, w_ref, c, side, left):
+        start = pl.multiple_of((c // 4) * self.cols + left, 128)
+        return w_ref.at[self.links.owner(c % 4), side, :, :, :, pl.ds(start, self.cols)]
+
+    def local(self, w_ref, c, left):
         return pltpu.make_async_copy(
-            self.piece(w_ref, c, self.links.core, base), self.own.at[c], self.ls.at[c]
+            self.piece(w_ref, c, self.links.core, left), self.own.at[c], self.ls.at[c]
         )
 
     def over_core(self, c, source):
@@ -711,9 +628,9 @@
             source, self.rc.at[c], self.cs.at[c], self.cr.at[c], self.links.over_core
         )
 
-    def load(self, w_ref, c, base=0):
-        self.local(w_ref, c, base).start()
-        self.over_core(c, self.piece(w_ref, c, 1 - self.links.core, base)).start()
+    def load(self, w_ref, c, left=0):
+        self.local(w_ref, c, left).start()
+        self.over_core(c, self.piece(w_ref, c, 1 - self.links.core, left)).start()
 
     def firsts(self, c):
         links, half = self.links, self.half
@@ -763,50 +680,62 @@
             device,
         )
 
-    def core(self, c, base=0, w_ref=None, mine=None):
-        if mine is None:
-            self.local(w_ref, c, base).wait()
-            mine = self.own[c]
+    def core(self, c, w_ref=None, left=0):
+        if w_ref is not None:
+            self.local(w_ref, c, left).wait()
         self.over_core(c, self.rc.at[c]).wait_recv()
-        self.own[c] = mine + self.rc[c]
+        x, y, half = 1 - self.links.x, 1 - self.links.y, self.half
+        self.own[c, :, x, :, :half] = self.own[c, :, x, :, :half] + self.rc[c, :, x, :, :half]
+        self.own[c, y, :, :, half:] = self.own[c, y, :, :, half:] + self.rc[c, y, :, :, half:]
         for copy in self.firsts(c):
             copy.start()
+
+    def left(self, c, y):
+        x, half = self.links.x, self.half
+        total = self.own[c, y, x, :, :half].astype(F32) + self.rc[c, y, x, :, :half].astype(F32)
+        return total + self.r1a[c, y].astype(F32)
+
+    def right(self, c, x):
+        y, half = self.links.y, self.half
+        total = self.own[c, y, x, :, half:].astype(F32) + self.rc[c, y, x, :, half:].astype(F32)
+        return total + self.r1b[c, x].astype(F32)
 
     def first(self, c):
         for copy in self.firsts(c):
             copy.wait_recv()
-        links, half = self.links, self.half
-        for other in range(2):
-            self.r1a[c, other] = self.r1a[c, other] + self.own[c, other, links.x, :, :half]
-            self.r1b[c, other] = self.r1b[c, other] + self.own[c, links.y, other, :, half:]
+        x, y = 1 - self.links.x, 1 - self.links.y
+        self.r1a[c, y] = self.left(c, y).astype(BF16)
+        self.r1b[c, x] = self.right(c, x).astype(BF16)
         for copy in self.seconds(c):
             copy.start()
+
+    def whole(self, c):
+        left = self.left(c, self.links.y) + self.r2a[c].astype(F32)
+        right = self.right(c, self.links.x) + self.r2b[c].astype(F32)
+        return jnp.concatenate([left, right], axis=1)
 
     def second(self, c):
         for copy in self.seconds(c):
             copy.wait_recv()
-        links, half = self.links, self.half
-        self.tot[c, :, :half] = self.r1a[c, links.y] + self.r2a[c]
-        self.tot[c, :, half:] = self.r1b[c, links.x] + self.r2b[c]
         item, k = c // 4, c % 4
         for slot in range(2):
 
             @pl.when(k == slot)
             def _(slot=slot):
+                self.tot[c] = self.whole(c).astype(BF16)
                 self.along(item, slot, c).start()
 
         @pl.when(k == 2)
         def _():
             self.along(item, 0, c).wait_recv()
-            self.tot[c] = self.tot[c] + self.rz[item, 0]
+            self.tot[c] = (self.whole(c) + self.rz[item, 0].astype(F32)).astype(BF16)
             self.along(item, 2, c).start()
 
     def finish(self, item):
         c = 4 * item
         for slot in (1, 2):
             self.along(item, slot, c).wait_recv()
-        total = self.tot[c + 3].astype(F32)
-        return total + self.rz[item, 1].astype(F32) + self.rz[item, 2].astype(F32)
+        return self.whole(c + 3) + self.rz[item, 1].astype(F32) + self.rz[item, 2].astype(F32)
 
     def drain(self):
         def body(c, carry):
@@ -819,6 +748,317 @@
         for item in range(self.chunks // 4):
             for slot in range(3):
                 self.along(item, slot, 4 * item).wait_send()
+
+
+class Weights:
+    @staticmethod
+    def scratch(n):
+        dma = pltpu.SemaphoreType.DMA
+        return [dma((n, 3)), dma((n, 3)), dma((n, 3, 3)), dma((n, 3, 3)), dma((n, 3)), dma((n, 3))]
+
+    def __init__(self, links, shards, fulls, sems):
+        self.links, self.shards, self.fulls = links, shards, fulls
+        self.zs, self.zr, self.ps, self.pr, self.cs, self.cr = sems
+        self.n = len(shards)
+        self.planes = (links.pair, links.far, links.cross)
+        self.slot = links.core * 4 + links.y * 2 + links.x
+
+    def window(self, ref, first, count):
+        step = ref.shape[-2] // 8
+        return ref.at[:, pl.ds(pl.multiple_of(first * step, step), count * step), :]
+
+    def along(self, i, slot):
+        links = self.links
+        source = self.planes[1] if slot == 2 else links.me
+        into = self.window(self.fulls[i].at[source], self.slot, 1)
+        mine = into if slot == 2 else self.window(self.shards[i], self.slot, 1)
+        device = links.to_far if slot == 1 else links.to_pair
+        return remote(mine, into, self.zs.at[i, slot], self.zr.at[i, slot], device)
+
+    def across(self, i, j, d):
+        links = self.links
+        piece = self.window(self.fulls[i].at[self.planes[j]], self.slot, 1)
+        device = (links.over_x, links.over_y, links.over_plane)[d]
+        return remote(piece, piece, self.ps.at[i, j, d], self.pr.at[i, j, d], device)
+
+    def core(self, i, j):
+        half = self.window(self.fulls[i].at[self.planes[j]], self.links.core * 4, 4)
+        return remote(half, half, self.cs.at[i, j], self.cr.at[i, j], self.links.over_core)
+
+    def start(self):
+        for i in range(self.n):
+            for slot in (0, 1):
+                self.along(i, slot).start()
+
+    def arrive(self, j):
+        for i in range(self.n):
+            self.along(i, j).wait_recv()
+            if j == 1:
+                self.along(i, 2).start()
+            for d in range(3):
+                self.across(i, j, d).start()
+
+    def share(self, j):
+        for i in range(self.n):
+            for d in range(3):
+                self.across(i, j, d).wait_recv()
+            self.core(i, j).start()
+
+    def finish(self, j):
+        for i in range(self.n):
+            self.core(i, j).wait_recv()
+
+    def drain(self):
+        for i in range(self.n):
+            for j in range(3):
+                self.along(i, j).wait_send()
+                self.core(i, j).wait_send()
+                for d in range(3):
+                    self.across(i, j, d).wait_send()
+
+
+class Gathered:
+    def __init__(self, links, source, into, sems):
+        self.links, self.source, self.into = links, source, into
+        self.ss, self.rs = sems
+        self.seqs, self.block = into.shape[0], into.shape[1] // 4
+
+    def window(self, s, plane):
+        rows = pl.ds(pl.multiple_of(plane * self.block, self.block), self.block)
+        return self.into.at[s, rows, :]
+
+    def copy(self, s, slot):
+        links = self.links
+        into = self.window(s, links.far if slot == 2 else links.me)
+        mine = into if slot == 2 else self.source(s)
+        device = links.to_far if slot == 1 else links.to_pair
+        return remote(mine, into, self.ss.at[s, slot], self.rs.at[s, slot], device)
+
+    def start(self):
+        for s in range(self.seqs):
+            for slot in (1, 0):
+                self.copy(s, slot).start()
+
+    def forward(self):
+        for s in range(self.seqs):
+            self.copy(s, 1).wait_recv()
+            self.copy(s, 2).start()
+
+    def finish(self):
+        for s in range(self.seqs):
+            for slot in (0, 2):
+                self.copy(s, slot).wait_recv()
+
+    def drain(self):
+        for s in range(self.seqs):
+            for slot in range(3):
+                self.copy(s, slot).wait_send()
+
+
+def front_kernel(group, size, *refs):
+    len_ref, x_ref, self_gain_ref, cross_gain_ref, table_ref, onehot_ref, *refs = refs
+    memory_ref, own_weights, refs = refs[0], refs[1:7], refs[7:]
+    n_ref, y_ref, n2_ref, memory_out, *refs = refs
+    self_out, cross_out, refs = refs[:3], refs[3:6], refs[6:]
+    outs, kept, refs = refs[:7], refs[7:14], refs[14:]
+    nall_ref, bias_ref, q_ref, k_ref, v_ref, c_ref, lse_ref = kept
+    self_full, refs = refs[:3], refs[3:]
+    tables_ref, ext_ref, line_ref, held_memory, *refs = refs
+    held_cross, refs = refs[:3], refs[3:]
+    (table_s, table_r, rows_s, rows_r, memory_s, memory_r, local, placed, held, done, *refs) = refs
+    links = Links()
+    me = links.me
+    w1 = Weights(links, own_weights[:3], self_out, refs[:6])
+    w2 = Weights(links, own_weights[3:], cross_out, refs[6:])
+    shards, rows, pw = q_ref.shape
+    seqs = len_ref.shape[0]
+    block = rows // seqs
+    full = block * shards
+    win = group * size
+    lanes = lane_groups(pw, group, size)
+    key = lax.broadcasted_iota(jnp.int32, (1, full), 1)
+    start = pl.multiple_of(me * block, block)
+    rows_one = Gathered(
+        links, lambda s: nall_ref.at[s, pl.ds(start, block), :], nall_ref, (rows_s, rows_r)
+    )
+    rows_memory = Gathered(links, lambda s: held_memory.at[s], memory_out, (memory_s, memory_r))
+
+    links.greet()
+    w1.start()
+    heard = [
+        remote(table_ref, tables_ref.at[me], table_s.at[i], table_r.at[i], to)
+        for i, to in enumerate((links.to_pair, links.to_far, links.to_cross))
+    ]
+    for copy in heard:
+        copy.start()
+    taken = [
+        pltpu.make_async_copy(own_weights[i], self_full[i].at[me], local.at[i]) for i in range(3)
+    ]
+    taken += [
+        pltpu.make_async_copy(own_weights[3 + i], held_cross[i], local.at[3 + i]) for i in range(3)
+    ]
+    taken.append(pltpu.make_async_copy(memory_ref, held_memory, local.at[6]))
+    for copy in taken:
+        copy.start()
+    x = x_ref[...].astype(F32)
+    n_ref[...] = (x * rms(x) * self_gain_ref[...]).astype(BF16)
+    for s in range(seqs):
+        nall_ref[s, pl.ds(start, block), :] = n_ref[s * block : (s + 1) * block, :]
+    tables_ref[me] = table_ref[...]
+    w1.arrive(0)
+    w1.arrive(1)
+    rows_one.start()
+    w1.arrive(2)
+    for copy in heard:
+        copy.wait_recv()
+    build_bias(me, tables_ref, onehot_ref, bias_ref, ext_ref, line_ref)
+    for copy in taken:
+        copy.wait()
+    put = [pltpu.make_async_copy(held_cross[i], cross_out[i].at[me], placed.at[i]) for i in range(3)]
+    put += [
+        pltpu.make_async_copy(self_full[i].at[me], self_out[i].at[me], placed.at[3 + i])
+        for i in range(3)
+    ]
+    put += [
+        pltpu.make_async_copy(held_memory.at[s], rows_memory.window(s, me), placed.at[6 + s])
+        for s in range(seqs)
+    ]
+    for copy in put:
+        copy.start()
+    rows_one.forward()
+    for j in range(3):
+        w1.share(j)
+    def hold(i, j):
+        plane = w1.planes[j]
+        return pltpu.make_async_copy(self_out[i].at[plane], self_full[i].at[plane], held.at[i, j])
+
+    for j in range(3):
+        w1.finish(j)
+        for i in range(3):
+            hold(i, j).start()
+    rows_one.finish()
+    w2.start()
+
+    def keep(i, h=None):
+        if h is None:
+            return pltpu.make_async_copy(kept[i], outs[i], done.at[i, 0])
+        return pltpu.make_async_copy(kept[i].at[h], outs[i].at[h], done.at[i, h])
+
+    for i in range(2):
+        keep(i).start()
+    for j in range(3):
+        for i in range(3):
+            hold(i, j).wait()
+
+    def body(k, carry):
+        h = links.owner(lax.rem(k + 3, shards))
+        nk = nall_ref[...].reshape(seqs * full, -1)
+        q_ref[h] = padded(nt(n_ref[...], self_full[0][h, 0]).astype(BF16), pw)
+        k_ref[h] = padded(nt(nk, self_full[1][h, 0]).astype(BF16), pw)
+        v_ref[h] = padded(nt(nk, self_full[1][h, 1]).astype(BF16), pw)
+        for s in range(seqs):
+            c, lse_ref[h, s] = head_context(
+                q_ref[h, s * block : (s + 1) * block, :],
+                k_ref[h, s * full : (s + 1) * full, :],
+                v_ref[h, s * full : (s + 1) * full, :],
+                bias_ref[pl.ds(h * group, group)].reshape(group * block, full).astype(F32),
+                key < len_ref[s],
+                lanes,
+            )
+            c_ref[h, s * block : (s + 1) * block, :] = c
+        for i in range(2, 7):
+            keep(i, h).start()
+
+        @pl.when(k == 0)
+        def _():
+            w2.arrive(0)
+            w2.arrive(1)
+            rows_memory.start()
+
+        @pl.when(k == 1)
+        def _():
+            w2.arrive(2)
+
+        return carry
+
+    lax.fori_loop(0, shards, body, 0)
+    joined = jnp.concatenate([c_ref[h][:, :win] for h in range(shards)], axis=1)
+    out_weight = self_full[2][...].reshape(shards * win, -1)
+    y = x_ref[...].astype(F32) + nn(joined, out_weight)
+    y_ref[...] = y
+    n2_ref[...] = (y * rms(y) * cross_gain_ref[...]).astype(BF16)
+    for j in range(3):
+        w2.share(j)
+    rows_memory.forward()
+    for j in range(3):
+        w2.finish(j)
+    rows_memory.finish()
+    w1.drain()
+    w2.drain()
+    rows_one.drain()
+    rows_memory.drain()
+    for copy in heard:
+        copy.wait_send()
+    for copy in put:
+        copy.wait()
+    for i in range(2):
+        keep(i).wait()
+    for h in range(shards):
+        for i in range(2, 7):
+            keep(i, h).wait()
+
+
+def front(lens, x, self_gain, cross_gain, table, onehot, memory, weights, shards, group, size):
+    rows, width = x.shape
+    seqs = lens.shape[0]
+    block = rows // seqs
+    full, keys = block * shards, rows * shards
+    win = group * size
+    pw = -(-win // 128) * 128
+    fulls = [((shards, *w.shape), BF16) for w in weights]
+    kept = [((seqs, full, width), BF16), ((shards * group, block, full), BF16)]
+    kept += [((shards, n, pw), BF16) for n in (rows, keys, keys, rows)]
+    kept.append(((shards, seqs, block, 128), F32))
+    dma = pltpu.SemaphoreType.DMA
+    anywhere = pl.BlockSpec(memory_space=pl.ANY)
+    return pl.pallas_call(
+        functools.partial(front_kernel, group, size),
+        out_shape=[
+            sds((rows, width), BF16),
+            sds((rows, width), F32),
+            sds((rows, width), BF16),
+            sds((seqs, full, width), BF16),
+        ]
+        + [sds(*a) for a in fulls + kept],
+        in_specs=[smem()] + [vmem()] * 5 + [anywhere] * 7,
+        out_specs=[vmem()] * 3 + [anywhere] * 14,
+        scratch_shapes=[pltpu.VMEM(*a) for a in kept + fulls[:3]]
+        + [
+            pltpu.VMEM((shards, *table.shape), BF16),
+            pltpu.VMEM((block, full + block), F32),
+            pltpu.VMEM((table.shape[1], 2 * block), F32),
+            pltpu.VMEM(memory.shape, BF16),
+        ]
+        + [pltpu.VMEM(w.shape, BF16) for w in weights[3:]]
+        + [
+            dma((3,)),
+            dma((3,)),
+            dma((seqs, 3)),
+            dma((seqs, 3)),
+            dma((seqs, 3)),
+            dma((seqs, 3)),
+            dma((7,)),
+            dma((6 + seqs,)),
+            dma((3, 3)),
+            dma((len(kept), shards)),
+        ]
+        + Weights.scratch(3)
+        + Weights.scratch(3),
+        compiler_params=pltpu.CompilerParams(
+            collective_id=0, has_side_effects=True, vmem_limit_bytes=VMEM_LIMIT
+        ),
+        name="front",
+    )(lens, x, self_gain, cross_gain, table, onehot, memory, *weights)
 
 
 class Rows:
@@ -840,26 +1080,20 @@
 
     def copy(self, slot):
         links = self.links
-        block = (links.cross, links.pair, links.far)[slot]
-        device = links.to_far if slot == 2 else links.to_pair
+        block = (links.cross, links.far, links.pair)[slot]
+        device = (links.to_cross, links.to_far, links.to_pair)[slot]
         return remote(
             self.buf.at[block], self.rx.at[slot], self.ss.at[slot], self.rs.at[slot], device
         )
 
     def start(self):
-        self.copy(0).start()
-        self.copy(1).start()
-
-    def middle(self):
-        self.copy(0).wait_recv()
-        far = self.links.far
-        self.buf[far] = self.buf[far] + self.rx[0]
-        self.copy(2).start()
+        for slot in range(3):
+            self.copy(slot).start()
 
     def finish(self):
-        for slot in (1, 2):
+        for slot in range(3):
             self.copy(slot).wait_recv()
-        return self.rx[1].astype(F32) + self.rx[2].astype(F32)
+        return sum(self.rx[slot].astype(F32) for slot in range(3))
 
     def drain(self):
         for slot in range(3):
@@ -898,22 +1132,32 @@
 
 
 def linked_kernel(biased, group, size, order, *refs):
-    (len_ref, nq_ref, nk_ref, q_ref, k_ref, v_ref, c_ref, lse_ref, wq_ref, wkv_ref, wo_ref) = refs[:11]
-    dy_ref, gain_ref, given_ref, refs = refs[11], refs[12], refs[13], refs[14:]
+    len_ref, dy_ref, gain_ref, given_ref, *refs = refs
+    held_count = 11 if biased else 10
+    held, refs = refs[:held_count], refs[held_count:]
     if biased:
-        bias_ref, x_ref, rows_ref, lines_ref, grad_ref, mem_ref, given_out, own_out, small_out, *refs = refs
+        feed_ref, x_ref, rows_ref, lines_ref, *refs = refs
+        grad_ref, mem_ref, feed_out, given_out, own_out, small_out, *refs = refs
     else:
         y_ref, dprev_ref, gg_ref, w_ref, later_ref, mem_ref, given_out, *refs = refs
-    dq_ref, dkv_ref, acck_ref, accq_ref, nqt_ref, nkt_ref, dat_ref, *refs = refs
+    buffers, held_sem, refs = refs[:held_count], refs[held_count], refs[held_count + 1 :]
+    nq_ref, nk_ref, c_ref, wo_ref, q_ref, k_ref, v_ref, lse_ref, wq_ref, wkv_ref = buffers[:10]
+    bias_ref = buffers[-1]
+    dq_ref, dkv_ref, acck_ref, accq_ref, nqt_ref, nkt_ref, dat_ref, wtmp_ref, *refs = refs
     links = Links()
     sums = Sums(links, refs[: Sums.count])
     refs = refs[Sums.count :]
+    if biased:
+        feed_sums = Sums(links, refs[: Sums.count])
+        refs = refs[Sums.count :]
     exchanges = []
     for _ in range(3 if biased else 1):
         exchanges.append(Rows(links, refs[: Rows.count]))
         refs = refs[Rows.count :]
     if biased:
-        ds_ref, ext_ref, wtmp_ref, diag_ref, sr, ms, mr = refs
+        ds_ref, ext_ref, diag_ref, sr, ms, mr = refs
+    else:
+        (w_sem,) = refs
     shards, rows, pw = q_ref.shape
     seqs = len_ref.shape[0]
     block = rows // seqs
@@ -923,57 +1167,98 @@
     key = lax.broadcasted_iota(jnp.int32, (1, full), 1)
     me = links.me
     start = pl.multiple_of(me * block, block)
-    ready = 4 if biased else 8
-    lag = 1 if biased else 0
+    def fetch(j, h=None):
+        if h is None:
+            return pltpu.make_async_copy(held[j], buffers[j], held_sem.at[j, 0])
+        part = pl.ds(h * group, group) if j == 10 else h
+        return pltpu.make_async_copy(held[j].at[part], buffers[j].at[part], held_sem.at[j, h])
 
     links.greet()
-    for c in range(ready):
-        sums.load(given_ref, c)
     if biased:
         exchanges[0].buf[...] = rows_ref[...]
         exchanges[0].start()
-
-    def core(c):
-        if biased:
-
-            @pl.when(c < ready)
+    for place in range(AHEAD):
+        sums.load(given_ref, place)
+    fetch(3).start()
+    for k in range(shards):
+        for j in range(4, held_count):
+            fetch(j, links.owner(k)).start()
+    for j in range(3):
+        fetch(j).start()
+
+    def stage(name, place):
+        if name == "load":
+            if not biased:
+                sums.load(given_ref, place)
+                return
+
+            @pl.when(place < 4)
             def _():
-                sums.core(c, w_ref=given_ref)
-
-            @pl.when(c >= ready)
+                sums.load(given_ref, place)
+
+            @pl.when(place >= 4)
             def _():
-                sums.core(c, mine=wtmp_ref[c - ready, links.core])
-
-        else:
-            sums.core(c, w_ref=given_ref)
+                feed_sums.load(feed_ref, place - 4, 2 * feed_sums.cols)
+
+            return
+        if not biased:
+            run = getattr(sums, name)
+            run(place, given_ref) if name == "core" else run(place)
+            return
+
+        @pl.when(place < 4)
+        def _():
+            sums.core(place, given_ref) if name == "core" else getattr(sums, name)(place)
+
+        @pl.when((place >= 4) & (place < 8))
+        def _():
+            c = place - 4
+            if name == "core":
+                feed_sums.core(c, feed_ref, 2 * feed_sums.cols)
+            else:
+                getattr(feed_sums, name)(c)
+
+        @pl.when(place >= 8)
+        def _():
+            getattr(sums, name)(place - 4)
+
+    places = 12 if biased else sums.chunks
+    late = (("load", -AHEAD), ("core", 0), ("first", 1), ("second", 3))
 
     def tick(t):
-        for stage, late in ((core, 0), (sums.first, 1), (sums.second, 3)):
-            c = t - lag - late
-
-            @pl.when((c >= 0) & (c < sums.chunks))
-            def _(stage=stage, c=c):
-                stage(c)
+        for name, behind in late:
+            place = t - behind
+
+            @pl.when((place >= 0) & (place < (8 if name == "load" else places)))
+            def _(name=name, place=place):
+                stage(name, place)
 
     da = dy_ref[...].astype(BF16)
-    put_rows(nqt_ref, nq_ref[...].T, order)
-    put_rows(nkt_ref, nk_ref[...].T, order)
-    put_rows(dat_ref, da.T, order)
     if biased:
         ext_ref[:, :block] = jnp.zeros((block, block), F32)
         far = lax.broadcasted_iota(jnp.int32, ext_ref.shape, 1) < start
+    fetch(3).wait()
 
     for s in range(seqs):
         mine = slice(s * block, (s + 1) * block)
         theirs = slice(s * full, (s + 1) * full)
+        if s == seqs - 1:
+            for j in (0, 2) if biased else range(3):
+                fetch(j).wait()
+            put_rows(nqt_ref, nq_ref[...].T, order)
+            put_rows(nkt_ref, nk_ref[...].T, order)
+            put_rows(dat_ref, da.T, order)
 
         def body(k, carry):
             h = links.owner(k)
+            if s == 0:
+                for j in range(4, held_count):
+                    fetch(j, h).wait()
             wo_h = wo_ref[pl.ds(pl.multiple_of(h * win, size), win), :]
             dcw = padded(nt(da[mine], wo_h).astype(BF16), pw)
             bias = None
             if biased:
-                bias = bias_ref[pl.ds(h * group, group)].reshape(group * block, full)
+                bias = bias_ref[pl.ds(h * group, group)].reshape(group * block, full).astype(F32)
             ds, dq, dk, dv = head_grads(
                 q_ref[h, mine, :],
                 k_ref[h, theirs, :],
@@ -1011,19 +1296,26 @@
                     diag_ref[pl.ds(h * group + a, 1), :] = diagonal_line(near, far_sum)
             if s == seqs - 1:
                 dkv = dkv_ref[h]
-                w = jnp.concatenate(
-                    [
-                        nn(nkt_ref[...], dkv).astype(BF16),
-                        nn(nqt_ref[...], dq_ref[h][:, :win]).astype(BF16),
-                        nn(dat_ref[...], c_ref[h][:, :win]).astype(BF16),
-                    ],
-                    axis=1,
-                ).reshape(2, 2, 2, w_rows, 4 * win)
+
+                def weight_rows(side):
+                    rows = pl.ds(pl.multiple_of(side * 4 * w_rows, 4 * w_rows), 4 * w_rows)
+                    return jnp.concatenate(
+                        [
+                            nn(nkt_ref[rows, :], dkv).astype(BF16),
+                            nn(nqt_ref[rows, :], dq_ref[h][:, :win]).astype(BF16),
+                            nn(dat_ref[rows, :], c_ref[h][:, :win]).astype(BF16),
+                        ],
+                        axis=1,
+                    ).reshape(2, 2, w_rows, 4 * win)
+
                 if biased:
-                    wtmp_ref[k] = w
-                    sums.over_core(ready + k, wtmp_ref.at[k, 1 - links.core]).start()
+                    wtmp_ref[k] = weight_rows(1 - links.core)
+                    sums.over_core(4 + k, wtmp_ref.at[k]).start()
+                    sums.own[4 + k] = weight_rows(links.core)
                 else:
-                    w_ref[h] = w
+                    for side in range(2):
+                        wtmp_ref[h, side] = weight_rows(side)
+                    pltpu.make_async_copy(wtmp_ref.at[h], w_ref.at[h], w_sem.at[h]).start()
             tick(4 * s + k)
             return carry
 
@@ -1032,14 +1324,14 @@
         if biased:
             acck_ref[pl.ds(start, block), :] += accq_ref[mine, :]
             total = acck_ref[...]
+            if s == 0:
+                fetch(1).wait()
             part = jnp.sum(total * nk_ref[theirs, :].astype(F32), axis=0, keepdims=True)
             gain1 = part if s == 0 else gain1 + part
             mover = exchanges[1 + s]
             mover.buf[...] = total.astype(BF16).reshape(shards, block, -1)
             mover.start()
             grad_ref[mine, :] = acck_ref[pl.ds(start, block), :]
-            if s == 0:
-                exchanges[0].middle()
         elif s == 0:
             exchanges[0].buf[...] = acck_ref[...].astype(BF16).reshape(shards, block, -1)
             exchanges[0].start()
@@ -1047,22 +1339,21 @@
         else:
             later_ref[...] = acck_ref[...].astype(BF16).reshape(shards, block, -1)
 
-    steps = range(4 * seqs, lag + sums.chunks + 3)
+    steps = range(4 * seqs, places + late[-1][1])
     if not biased:
-        exchanges[0].middle()
         dy, gg = norm_grads(y_ref[...], gain_ref[...], accq_ref[...])
         dprev_ref[...] = dy_ref[...] + dy
         gg_ref[...] = gg
         for t in steps:
             tick(t)
         mem_ref[...] += exchanges[0].finish()
-        for item in range(sums.chunks // 4):
-            cols = slice(item * sums.cols, (item + 1) * sums.cols)
-            given_out[:, cols] = sums.finish(item)
+        for item in range(2):
+            given_out[item] = sums.finish(item)
+        for h in range(shards):
+            pltpu.make_async_copy(wtmp_ref.at[h], w_ref.at[h], w_sem.at[h]).wait()
     else:
         gain1 = gain1 / gain_ref[...]
         width = gain1.shape[1]
-        exchanges[1].middle()
         diag_ref[shards * group :, :] = jnp.zeros_like(diag_ref[shards * group :, :])
         lines = lines_ref.shape[0]
         sr[0, : diag_ref.shape[0], :] = diag_ref[...]
@@ -1070,24 +1361,34 @@
         for j in range(width // (2 * block)):
             row = diag_ref.shape[0] + j
             sr[0, row : row + 1, :] = gain1[:, j * 2 * block : (j + 1) * 2 * block]
-        hops = [links.over_core, links.over_x, links.over_y, links.to_pair, links.to_far]
+        plane = 2 + 2 * links.y + links.x
+        hops = [(1, 0, links.over_core)]
+        hops += [(plane, plane, to) for to in (links.over_x, links.over_y, links.over_plane)]
+        hops += [(6 + me, 6 + me, to) for to in (links.to_pair, links.to_far, links.to_cross)]
 
         def hop(i):
-            return remote(sr.at[i], sr.at[len(hops) + 1 + i], ms.at[i], mr.at[i], hops[i])
+            into, source, to = hops[i]
+            return remote(sr.at[source], sr.at[into], ms.at[i], mr.at[i], to)
 
         hop(0).start()
-        for i in range(max(len(steps), len(hops))):
-            if i < len(steps):
-                tick(steps[i])
-            if i < len(hops):
-                hop(i).wait_recv()
-                sr[i + 1] = sr[i] + sr[len(hops) + 1 + i]
-                if i + 1 < len(hops):
-                    hop(i + 1).start()
+        for i, t in enumerate(steps):
+            tick(t)
             if i == 1:
-                exchanges[2].middle()
-        small_out[...] = sr[len(hops)]
+                hop(0).wait_recv()
+                sr[plane] = sr[0] + sr[1]
+                for j in (1, 2, 3):
+                    hop(j).start()
+            if i == 3:
+                for j in (1, 2, 3):
+                    hop(j).wait_recv()
+                sr[6 + me] = (sr[2] + sr[3]) + (sr[4] + sr[5])
+                for j in (4, 5, 6):
+                    hop(j).start()
+        for j in (4, 5, 6):
+            hop(j).wait_recv()
+        small_out[...] = (sr[6] + sr[7]) + (sr[8] + sr[9])
         mem_ref[...] = exchanges[0].buf[me].astype(F32) + exchanges[0].finish()
+        feed_out[...] = feed_sums.finish(0)
         given_out[...] = sums.finish(0)
         for s in range(seqs):
             mine = slice(s * block, (s + 1) * block)
@@ -1100,6 +1401,8 @@
     for mover in exchanges:
         mover.drain()
     sums.drain()
+    if biased:
+        feed_sums.drain()
 
 
 def linked_backward(lens, nq, nk, saved, wq, wkv, wo, dy, gain, given, extras, biased, group, size, order):
@@ -1110,15 +1413,20 @@
     block, full, win = rows // seqs, keys // seqs, group * size
     cols = 4 * win
     share = width // 8
-    given = given.reshape(shards, 2, 2, 2, share, -1)
-    args = [lens, nq, nk, q, k, v, c, lse, wq, wkv, wo, dy, gain, given, *extras]
-    chunks = 8
+    split = lambda w: w.reshape(shards, 2, 2, 2, share, -1)
+    held = [nq, nk, c, wo, q, k, v, lse, wq, wkv]
+    if biased:
+        held.append(extras[1])
+        extras = [split(extras[0]), *extras[2:]]
+    args = [lens, dy, gain, split(given), *held, *extras]
+    part = split(extras[0] if biased else given).shape[-1] // 3
     if biased:
         lines = extras[3].shape[0]
         diag_rows = -(-shards * group // 8) * 8
         out_shape = [
             sds((rows, width), F32),
             sds((block, width), F32),
+            sds((share, part), F32),
             sds((share, cols), F32),
             sds((share, cols), F32),
             sds((diag_rows + lines, 2 * block), F32),
@@ -1130,9 +1438,11 @@
             sds((shards, 2, 2, 2, share, cols), BF16),
             sds((shards, block, width), BF16),
             sds((block, width), F32),
-            sds((share, given.shape[-1]), F32),
+            sds((2, share, part), F32),
         ]
-    scratch = [
+    scratch = [pltpu.VMEM(a.shape, a.dtype) for a in held]
+    scratch += [
+        pltpu.SemaphoreType.DMA((len(held), shards)),
         pltpu.VMEM((shards, rows, pw), BF16),
         pltpu.VMEM((shards, keys, 2 * win), BF16),
         pltpu.VMEM((full, width), F32),
@@ -1141,7 +1451,10 @@
         pltpu.VMEM((width, keys), BF16),
         pltpu.VMEM((width, rows), BF16),
     ]
-    scratch += Sums.scratch(chunks, share, cols)
+    scratch.append(pltpu.VMEM((shards, *(() if biased else (2,)), 2, 2, share, cols), BF16))
+    scratch += Sums.scratch(8, share, cols if biased else part)
+    if biased:
+        scratch += Sums.scratch(4, share, part)
     for _ in range(3 if biased else 1):
         scratch += Rows.scratch(block, width)
     if biased:
@@ -1149,19 +1462,24 @@
         scratch += [
             pltpu.VMEM((shards, group * block, full), BF16),
             pltpu.VMEM((block, full + block), F32),
-            pltpu.VMEM((shards, 2, 2, 2, share, cols), BF16),
             pltpu.VMEM((diag_rows, 2 * block), F32),
-            pltpu.VMEM((11, diag_rows + lines, 2 * block), F32),
-            dma((5,)),
-            dma((5,)),
+            pltpu.VMEM((10, diag_rows + lines, 2 * block), F32),
+            dma((7,)),
+            dma((7,)),
         ]
-    in_specs = [smem()] + [vmem()] * (len(args) - 1)
-    in_specs[13] = pl.BlockSpec(memory_space=pl.ANY)
+    else:
+        scratch.append(pltpu.SemaphoreType.DMA((shards,)))
+    anywhere = pl.BlockSpec(memory_space=pl.ANY)
+    in_specs = [smem(), vmem(), vmem(), anywhere] + [anywhere] * len(held)
+    in_specs += [anywhere if biased else vmem()] + [vmem()] * (len(extras) - 1)
+    out_specs = [vmem()] * len(out_shape)
+    if not biased:
+        out_specs[2] = anywhere
     return pl.pallas_call(
         functools.partial(linked_kernel, biased, group, size, order),
         out_shape=out_shape,
         in_specs=in_specs,
-        out_specs=[vmem()] * len(out_shape),
+        out_specs=out_specs,
         scratch_shapes=scratch,
         compiler_params=pltpu.CompilerParams(
             collective_id=2 if biased else 1, has_side_effects=True, vmem_limit_bytes=VMEM_LIMIT
@@ -1204,31 +1522,34 @@
 
     x = layer_input.reshape(rows, width)
     x32 = x.astype(F32)
-    n1 = (x32 * rms(x32) * sg).astype(BF16)
-    n1_all = lax.all_gather(n1.reshape(seqs, block, width), "head", axis=1, tiled=True)
-    n1_all = n1_all.reshape(seqs * full, width)
-
     tight = batch_count == 8 and shards == 4 and seqs == 2
     order = tuple((i % 2) * 4 + i // 2 for i in range(8)) if tight else (0,)
     table = jnp.pad(rel_bias, ((0, 0), (0, 128 - group)))
     flip = lambda w: jnp.swapaxes(w, -1, -2)
     weights = [flip(self_query)[None], flip(self_key_value), self_out[None]]
     weights += [flip(cross_query)[None], flip(cross_key_value), cross_out[None]]
+    onehot = near_onehot(block)
+    lines_of = onehot.T.astype(BF16)
     if tight:
-        *weights, tables = gather_weights(weights, table, shards)
+        n1, y1, n2, memory_all, wq1, wkv1, wo1, wq2, wkv2, wo2, n1_all, bias, *saved1 = front(
+            dec_lengths, x, sg, cg, table, lines_of, memory, weights, shards, group, size
+        )
+        n1_all = n1_all.reshape(seqs * full, width)
     else:
-        weights = [lax.all_gather(w, "head", axis=0) for w in weights]
+        n1 = (x32 * rms(x32) * sg).astype(BF16)
+        n1_all = lax.all_gather(n1.reshape(seqs, block, width), "head", axis=1, tiled=True)
+        n1_all = n1_all.reshape(seqs * full, width)
+        wq1, wkv1, wo1, wq2, wkv2, wo2 = [lax.all_gather(w, "head", axis=0) for w in weights]
         tables = lax.all_gather(table, "head", axis=0)
-    wq1, wkv1, wo1, wq2, wkv2, wo2 = weights
+        bias = bias_tiles(me, tables, lines_of, group, block, full)
+        memory_all = lax.all_gather(memory, "head", axis=1, tiled=True)
+    memory_all = memory_all.reshape(seqs * enc_full, width)
     wq1, wq2 = wq1[:, 0], wq2[:, 0]
     wo1, wo2 = wo1.reshape(width, width), wo2.reshape(width, width)
-    onehot = near_onehot(block)
-    bias = bias_tiles(me, tables, onehot.T.astype(BF16), group, block, full)
-    memory_all = lax.all_gather(memory, "head", axis=1, tiled=True).reshape(seqs * enc_full, width)
-
-    *saved1, y1, n2 = attend_forward(
-        dec_lengths, n1, n1_all, x, wq1, wkv1, wo1, cg, bias, group, size
-    )
+    if not tight:
+        *saved1, y1, n2 = attend_forward(
+            dec_lengths, n1, n1_all, x, wq1, wkv1, wo1, cg, bias, group, size
+        )
     *saved2, y2, n3 = attend_forward(
         enc_lengths, n2, memory_all, y1, wq2, wkv2, wo2, fg, None, group, size
     )
@@ -1237,16 +1558,16 @@
     )
     gain_rows = width // (2 * block)
     if tight:
-        dy1, gain2, cross_w, memory_later, memory_first, feed_w = linked_backward(
+        dy1, gain2, cross_w, memory_later, memory_first, feed_in_grad = linked_backward(
             enc_lengths, n2, memory_all, saved2, wq2, wkv2, wo2, dy2, cg, feed_w, [y1],
             False, group, size, order,
         )
         lines = jnp.concatenate([jnp.zeros((1, width), F32), gain2, gain3], axis=0)
         lines = lines.reshape(-1, 2 * block)
         lines = jnp.pad(lines, ((0, -lines.shape[0] % 8), (0, 0)))
-        input_grad, memory_last, cross_w, self_w, small = linked_backward(
+        input_grad, memory_last, feed_out_grad, cross_w, self_w, small = linked_backward(
             dec_lengths, n1, n1_all, saved1, wq1, wkv1, wo1, dy1, sg, cross_w,
-            [bias, x, memory_later, lines], True, group, size, order,
+            [feed_w, bias, x, memory_later, lines], True, group, size, order,
         )
         memory_grad = jnp.stack([memory_first, memory_last])
         diag, lines = small[: -lines.shape[0]], small[-lines.shape[0] :]
@@ -1278,6 +1599,8 @@
         diag, lines = lax.psum((diag, lines), ("batch", "head"))
         dx, _ = norm_grads(x32, sg, dn1.reshape(rows, width))
         input_grad = dy1 + dx
+        feed_in_grad = jnp.stack([feed_w[:, :part], feed_w[:, part : 2 * part]])
+        feed_out_grad = feed_w[:, 2 * part :]
     gains = lines[: 3 * gain_rows].reshape(3, width)
     diag = lax.dynamic_slice_in_dim(diag, me[0] * group, group, 0)
     table_grad = jnp.einsum("tb,ht->bh", onehot, diag, precision=highest)
@@ -1302,8 +1625,8 @@
         cross_kv,
         cross_o,
         gains[2],
-        jnp.stack([feed_w[:, :part], feed_w[:, part : 2 * part]]),
-        feed_w[:, 2 * part :].T,
+        feed_in_grad,
+        feed_out_grad.T,
     )
 
 

time: 305 us -> 255 us (0.84)
  Pallas kernels: 265 us -> 237 us
  between operations: 14.1 us -> 0.75 us
  other arithmetic: 9.13 us -> 3.69 us
    pallas_call x2 -> x1, Pallas kernels: 28.4 us -> 13.8 us  [attend_forward(): pl.pallas_call(functools.partial(forward_kernel, bias is not None, group,...]
    pallas_call x2, Pallas kernels: 139 us -> 126 us  [linked_backward(): pl.pallas_call(functools.partial(linked_kernel, biased, group, size, orde...]
    convert_element_type x4 -> x1, other arithmetic: 4.11 us -> 0.62 us  [per_device(): lines_of = onehot.T.astype(BF16)]
    pallas_call x2 -> x1, Pallas kernels: 83.8 us -> 83.6 us  [front(): pl.pallas_call(functools.partial(front_kernel, group, size), out_shape=[s...]
  transfers between devices with their start and end apart: 2 -> 0, of which waited for: 0 -> 0; matrix products, arithmetic and copies ran while one was open for 2% -> 0% of each run, Pallas kernels for 32% -> 0%
where the time goes in v4:
time: 255 us
  Pallas kernels  237 us (93%)
  local copies, waits for them, and re-layouts  12.9 us (5%)
  other arithmetic  3.69 us (1%)
    pallas_call x2, Pallas kernels, linked_backward(): pl.pallas_call(functools.partial(linked_kernel, biased, group, size, orde...  126 us
    pallas_call x1, Pallas kernels, front(): pl.pallas_call(functools.partial(front_kernel, group, size), out_shape=[s...  83.6 us
    pallas_call x1, Pallas kernels, attend_forward(): pl.pallas_call(functools.partial(forward_kernel, bias is not None, group,...  13.8 us
    pallas_call x1, Pallas kernels, feed(): pl.pallas_call(functools.partial(feed_kernel, order), grid=(shards,), out...  13.7 us

profile of v4, /device:TPU:0, one launch (start us, length us, event | category | flops | bytes accessed | tf_op | source)
XLA Modules:
  0.0 255.0 jit_solution(14011052001912540894)
XLA Ops:
  0.6 0.0 copy-start.7
  0.7 0.6 convert_convert_fusion.refs_5_
  1.3 1.3 reshape.153.refs_2_
  2.6 1.3 reshape.155.refs_3_.refs_2_
  3.8 0.8 copy.32
  4.6 0.6 pad.8.refs_4_
  5.2 83.6 %front.1 = (bf16[256,768]{1,0:T(8,128)(2,1)}, f32[256,768]{1,0:T(8,128)}, bf16[256,768]{1,0:T(8,128)(2,1)}, bf16[2,512,768]{2,1,0:T(8,128)(2,1)}, bf16[4,1,192,7...) custom-call(s32[2]{0:T(128)} %refs_0_.5, ...), custom_call_target="tpu_custom_call" | custom-call | tf_op jit(solution)/shard_map/front/pallas_call | solution.py:1024
  88.8 0.0 copy-done.7
  88.8 0.6 reshape.157.gain_ref
  89.4 13.8 %attend_forward.1 = (bf16[4,256,256]{2,1,0:T(8,128)(2,1)}, bf16[4,1024,256]{2,1,0:T(8,128)(2,1)}, bf16[4,1024,256]{2,1,0:T(8,128)(2,1)}, bf16[4,256,256]{2,1,0:T...) custom-call(s32[2]{0:T(128)} %refs_0_.4, ...), custom_call_target="tpu_custom_call" | custom-call | flops 3825205248 | bytes 16777216 | tf_op jit(solution)/shard_map/attend_forward/pallas_call | solution.py:239
  103.2 13.7 %feed.1 = (bf16[256,768]{1,0:T(8,128)(2,1)}, f32[256,768]{1,0:T(8,128)}, f32[1,768]{1,0:T(1,128)}, bf16[4,768,1536]{2,1,0:T(8,128)(2,1)}) custom-call(f32[256,768]{1,0:T(8,128)} %get-tuple-element.61.y_ref, bf16[256,768]{1,0:T(8,128)(2,1)} %get-tuple-element.62.n_ref, bf16[256,768]{1,0:T(8,128)(2,1)} %bitcast.60, bf16[2,768,2048]{2,1,0:T(8,128)(2,1)} %win_ref.1, ...), custom_call_target="tpu_custom_call" | custom-call | flops 7247757312 | bytes 25165824 | tf_op jit(solution)/shard_map/feed/pallas_call | solution.py:486
  117.0 0.0 copy-start.6
  117.0 49.0 %cross_backward.1 = (f32[256,768]{1,0:T(8,128)}, f32[1,768]{1,0:T(1,128)}, bf16[4,2,2,2,96,768]{5,4,3,2,1,0:T(8,128)(2,1)}, bf16[4,128,768]{2,1,0:T(8,128)(2,1)}...) custom-call(s32[2]{0:T(128)} %refs_0_.4, f32[256,768]{1,0:T(8,128)} %get-tuple-element.64.refs_1_, ...), custom_call_target="tpu_custom_call" | custom-call | tf_op jit(solution)/shard_map/cross_backward/pallas_call | solution.py:1478
  166.0 0.0 copy-done.6
  166.0 0.7 pad_maximum_fusion.3
  166.8 0.6 pad.9.refs_18_
  167.4 76.7 %self_backward.1 = (f32[256,768]{1,0:T(8,128)}, f32[128,768]{1,0:T(8,128)}, f32[96,512]{1,0:T(8,128)}, f32[96,768]{1,0:T(8,128)}, f32[96,768]{1,0:T(8,128)}, /*index=5*/f32[32,256]{1,0:T(8,128)}) custom-call(s32[2]{0:T(128)} %refs_0_.5, f32[256,768]{1,0:T(8,128)} %get-tuple-element.71.refs_1_, f32[1,768]{1,0:T(1,128)} %reshape.153.refs_2_, ...), custom_call_target="tpu_custom_call" | custom-call | tf_op jit(solution)/shard_map/self_backward/pallas_call | solution.py:1478
  244.1 0.0 copy-start.2
  244.1 0.0 copy-start.3
  244.1 0.0 copy-start.5
  244.1 0.0 copy-start
  244.1 2.1 slice_bitcast_fusion
  246.3 0.7 pad_maximum_fusion.2
  246.9 0.0 copy-start.1
  246.9 0.7 pad_maximum_fusion.1
  247.6 0.7 copy.33
  248.4 0.7 copy.34
  249.1 0.0 copy-start.4
  249.1 0.0 copy-done.2
  249.1 0.0 copy-done.3
  249.1 0.9 pad_maximum_fusion
  250.1 0.0 copy-done.5
  250.1 0.8 fusion
  250.9 0.6 squeeze.17
  251.5 0.6 squeeze.18
  252.1 0.6 squeeze.19
  252.7 0.0 copy-done
  252.7 0.9 copy.38
  253.6 0.0 copy-done.1
  253.6 0.7 copy.39
  254.3 0.0 copy-done.4
  254.3 0.7 copy.40
  (5 shorter events, 0.0 us)
Async XLA Ops:
  0.6 88.2 %copy-start.7 = (bf16[768]{0:T(1024)(128)(2,1)S(1)}, bf16[768]{0:T(1024)(128)(2,1)}, u32[]{:S(2)}) copy-start(bf16[768]{0:T(1024)(128)(2,1)} %param.30) | copy-start | bytes 4612
  117.0 49.0 %copy-start.6 = (f32[1,768]{1,0:T(1,128)S(1)}, f32[1,768]{1,0:T(1,128)}, u32[]{:S(2)}) copy-start(f32[1,768]{1,0:T(1,128)} %get-tuple-element.86) | copy-start | bytes 9220
  244.1 5.0 %copy-start.2 = (f32[128,768]{1,0:T(8,128)S(1)}, f32[128,768]{1,0:T(8,128)}, u32[]{:S(2)}) copy-start(f32[128,768]{1,0:T(8,128)} %get-tuple-element.88) | copy-start | bytes 1179652
  244.1 5.0 %copy-start.3 = (f32[128,768]{1,0:T(8,128)S(1)}, f32[128,768]{1,0:T(8,128)}, u32[]{:S(2)}) copy-start(f32[128,768]{1,0:T(8,128)} %get-tuple-element.89) | copy-start | bytes 1179652
  244.1 5.9 %copy-start.5 = (f32[32,256]{1,0:T(8,128)S(1)}, f32[32,256]{1,0:T(8,128)}, u32[]{:S(2)}) copy-start(f32[32,256]{1,0:T(8,128)} %get-tuple-element.90) | copy-start | bytes 98308
  244.1 8.6 %copy-start = (f32[256,768]{1,0:T(8,128)S(1)}, f32[256,768]{1,0:T(8,128)}, u32[]{:S(2)}) copy-start(f32[256,768]{1,0:T(8,128)} %get-tuple-element.87) | copy-start | bytes 2359300
  246.9 6.6 %copy-start.1 = (f32[2,96,512]{2,1,0:T(8,128)S(1)}, f32[2,96,512]{2,1,0:T(8,128)}, u32[]{:S(2)}) copy-start(f32[2,96,512]{2,1,0:T(8,128)} %get-tuple-element.153) | copy-start | bytes 1179652
  249.1 5.2 %copy-start.4 = (f32[96,512]{1,0:T(8,128)S(1)}, f32[96,512]{1,0:T(8,128)}, u32[]{:S(2)}) copy-start(f32[96,512]{1,0:T(8,128)} %get-tuple-element.94) | copy-start | bytes 589828

commit v5 on v4

--- a/solution.py
+++ b/solution.py
@@ -78,6 +78,10 @@
     return dy, jnp.sum(e * xhat, axis=0, keepdims=True)
 
 
+def row(ref):
+    return ref[...].astype(F32).reshape(1, -1)
+
+
 def padded(v, width):
     extra = width - v.shape[1]
     if extra == 0:
@@ -107,7 +111,14 @@
     return jax.ShapeDtypeStruct(shape, dtype)
 
 
-def build_bias(me, table_ref, onehot_ref, b_ref, ext_ref, line_ref):
+def bucket_rows(block, count):
+    distance = block - lax.broadcasted_iota(jnp.int32, (1, 2 * block), 1)
+    distance = jnp.where(distance < 0, 2 * MAX_DIST, distance)
+    bucket = bucket_of(distance, NB, MAX_DIST)
+    return bucket == lax.broadcasted_iota(jnp.int32, (count, 2 * block), 0)
+
+
+def build_bias(me, table_ref, b_ref, ext_ref, line_ref):
     heads, block, full = b_ref.shape
     shards = table_ref.shape[0]
     group = heads // shards
@@ -117,9 +128,10 @@
     col_i = lax.broadcasted_iota(jnp.int32, (block, width), 1)
     masked = (col_i - row_i) > block
     far = lax.broadcasted_iota(jnp.int32, ext_ref.shape, 1) < start
+    onehot = bucket_rows(block, table_ref.shape[2]).astype(BF16)
 
     def body(h, carry):
-        line_ref[...] = tn(table_ref[h], onehot_ref[...])
+        line_ref[...] = nn(table_ref[h], onehot)
         for a in range(group):
             row = line_ref[a : a + 1, :]
             tile = pltpu.roll(
@@ -137,12 +149,12 @@
     build_bias(me_ref[0], *refs)
 
 
-def bias_tiles(me, tables, onehot, group, block, full):
-    shards, buckets, lanes = tables.shape
+def bias_tiles(me, tables, group, block, full):
+    shards, lanes = tables.shape[:2]
     return pl.pallas_call(
         bias_kernel,
         out_shape=sds((shards * group, block, full), BF16),
-        in_specs=[smem(), vmem(), vmem()],
+        in_specs=[smem(), vmem()],
         out_specs=vmem(),
         scratch_shapes=[
             pltpu.VMEM((block, full + block), F32),
@@ -150,7 +162,7 @@
         ],
         compiler_params=params(),
         name="bias_tiles",
-    )(me, tables, onehot)
+    )(me, tables)
 
 
 def lane_groups(width, group, size):
@@ -225,7 +237,7 @@
     joined = jnp.concatenate([c_ref[h][:, :win] for h in range(shards)], axis=1)
     y = res_ref[...].astype(F32) + nn(joined, wo_ref[...])
     y_ref[...] = y
-    n_ref[...] = (y * rms(y) * gain_ref[...]).astype(BF16)
+    n_ref[...] = (y * rms(y) * row(gain_ref)).astype(BF16)
 
 
 def attend_forward(lens, nq, nk, res, wq, wkv, wo, gain, bias, group, size):
@@ -382,11 +394,11 @@
         total = acc_ref[: seqs * full, :]
         part_ref[...] = total.astype(BF16)
         gg_ref[...] = (
-            jnp.sum(total * nk_ref[...].astype(F32), axis=0, keepdims=True) / gain_ref[...]
+            jnp.sum(total * nk_ref[...].astype(F32), axis=0, keepdims=True) / row(gain_ref)
         )
     else:
         part_ref[...] = acc_ref[: seqs * full, :].astype(BF16)
-        dy, gg = norm_grads(y_ref[...], gain_ref[...], acc_ref[seqs * full :, :])
+        dy, gg = norm_grads(y_ref[...], row(gain_ref), acc_ref[seqs * full :, :])
         dprev_ref[...] = dy_ref[...] + dy
         gg_ref[...] = gg
 
@@ -473,7 +485,7 @@
     @pl.when(step == pl.num_programs(0) - 1)
     def _():
         out_ref[...] = acc_ref[...].astype(BF16)
-        dy, gg = norm_grads(y_ref[...], gain_ref[...], dn_ref[...])
+        dy, gg = norm_grads(y_ref[...], row(gain_ref), dn_ref[...])
         dy_ref[...] = cot_ref[...].astype(F32) + dy
         gg_ref[...] = gg
 
@@ -498,7 +510,7 @@
             fixed((rows, width)),
             pl.BlockSpec((2, width, part), lambda j: (0, 0, j)),
             pl.BlockSpec((part, width), lambda j: (j, 0)),
-            fixed((1, width)),
+            fixed((width,)),
         ],
         out_specs=[
             fixed((rows, width)),
@@ -844,10 +856,13 @@
             self.copy(s, 1).wait_recv()
             self.copy(s, 2).start()
 
+    def take(self, slot):
+        for s in range(self.seqs):
+            self.copy(s, slot).wait_recv()
+
     def finish(self):
-        for s in range(self.seqs):
-            for slot in (0, 2):
-                self.copy(s, slot).wait_recv()
+        for slot in (0, 2):
+            self.take(slot)
 
     def drain(self):
         for s in range(self.seqs):
@@ -856,15 +871,15 @@
 
 
 def front_kernel(group, size, *refs):
-    len_ref, x_ref, self_gain_ref, cross_gain_ref, table_ref, onehot_ref, *refs = refs
+    len_ref, enc_ref, x_ref, self_gain_ref, cross_gain_ref, feed_gain_ref, table_ref, *refs = refs
     memory_ref, own_weights, refs = refs[0], refs[1:7], refs[7:]
-    n_ref, y_ref, n2_ref, memory_out, *refs = refs
+    n_ref, y_ref, n2_ref, y2_ref, n3_ref, memory_out, *refs = refs
     self_out, cross_out, refs = refs[:3], refs[3:6], refs[6:]
-    outs, kept, refs = refs[:7], refs[7:14], refs[14:]
-    nall_ref, bias_ref, q_ref, k_ref, v_ref, c_ref, lse_ref = kept
-    self_full, refs = refs[:3], refs[3:]
-    tables_ref, ext_ref, line_ref, held_memory, *refs = refs
-    held_cross, refs = refs[:3], refs[3:]
+    outs, kept, refs = refs[:12], refs[12:24], refs[24:]
+    nall_ref, bias_ref, q_ref, k_ref, v_ref, c_ref, lse_ref = kept[:7]
+    q2_ref, k2_ref, v2_ref, c2_ref, lse2_ref = kept[7:]
+    self_full, cross_full, refs = refs[:3], refs[3:6], refs[6:]
+    tables_ref, ext_ref, line_ref, mem_ref, *refs = refs
     (table_s, table_r, rows_s, rows_r, memory_s, memory_r, local, placed, held, done, *refs) = refs
     links = Links()
     me = links.me
@@ -881,12 +896,17 @@
     rows_one = Gathered(
         links, lambda s: nall_ref.at[s, pl.ds(start, block), :], nall_ref, (rows_s, rows_r)
     )
-    rows_memory = Gathered(links, lambda s: held_memory.at[s], memory_out, (memory_s, memory_r))
-
+    rows_memory = Gathered(
+        links, lambda s: mem_ref.at[s, pl.ds(start, block), :], memory_out, (memory_s, memory_r)
+    )
+
+    line_ref[...] = jnp.zeros_like(line_ref)
+    line_ref[:group, :NB] = table_ref[...].astype(F32)
+    tables_ref[me] = line_ref[:, : tables_ref.shape[2]].astype(BF16)
     links.greet()
     w1.start()
     heard = [
-        remote(table_ref, tables_ref.at[me], table_s.at[i], table_r.at[i], to)
+        remote(tables_ref.at[me], tables_ref.at[me], table_s.at[i], table_r.at[i], to)
         for i, to in enumerate((links.to_pair, links.to_far, links.to_cross))
     ]
     for copy in heard:
@@ -895,32 +915,39 @@
         pltpu.make_async_copy(own_weights[i], self_full[i].at[me], local.at[i]) for i in range(3)
     ]
     taken += [
-        pltpu.make_async_copy(own_weights[3 + i], held_cross[i], local.at[3 + i]) for i in range(3)
+        pltpu.make_async_copy(own_weights[3 + i], cross_full[i].at[me], local.at[3 + i])
+        for i in range(3)
     ]
-    taken.append(pltpu.make_async_copy(memory_ref, held_memory, local.at[6]))
+    taken.append(
+        pltpu.make_async_copy(memory_ref, mem_ref.at[:, pl.ds(start, block), :], local.at[6])
+    )
     for copy in taken:
         copy.start()
     x = x_ref[...].astype(F32)
-    n_ref[...] = (x * rms(x) * self_gain_ref[...]).astype(BF16)
+    n_ref[...] = (x * rms(x) * row(self_gain_ref)).astype(BF16)
     for s in range(seqs):
         nall_ref[s, pl.ds(start, block), :] = n_ref[s * block : (s + 1) * block, :]
-    tables_ref[me] = table_ref[...]
     w1.arrive(0)
     w1.arrive(1)
     rows_one.start()
     w1.arrive(2)
     for copy in heard:
         copy.wait_recv()
-    build_bias(me, tables_ref, onehot_ref, bias_ref, ext_ref, line_ref)
+    build_bias(me, tables_ref, bias_ref, ext_ref, line_ref)
     for copy in taken:
         copy.wait()
-    put = [pltpu.make_async_copy(held_cross[i], cross_out[i].at[me], placed.at[i]) for i in range(3)]
+    put = [
+        pltpu.make_async_copy(cross_full[i].at[me], cross_out[i].at[me], placed.at[i])
+        for i in range(3)
+    ]
     put += [
         pltpu.make_async_copy(self_full[i].at[me], self_out[i].at[me], placed.at[3 + i])
         for i in range(3)
     ]
     put += [
-        pltpu.make_async_copy(held_memory.at[s], rows_memory.window(s, me), placed.at[6 + s])
+        pltpu.make_async_copy(
+            rows_memory.source(s), rows_memory.window(s, me), placed.at[6 + s]
+        )
         for s in range(seqs)
     ]
     for copy in put:
@@ -930,7 +957,8 @@
         w1.share(j)
     def hold(i, j):
         plane = w1.planes[j]
-        return pltpu.make_async_copy(self_out[i].at[plane], self_full[i].at[plane], held.at[i, j])
+        into, source = (self_full[i], self_out[i]) if i < 3 else (cross_full[i - 3], cross_out[i - 3])
+        return pltpu.make_async_copy(source.at[plane], into.at[plane], held.at[i, j])
 
     for j in range(3):
         w1.finish(j)
@@ -986,13 +1014,69 @@
     out_weight = self_full[2][...].reshape(shards * win, -1)
     y = x_ref[...].astype(F32) + nn(joined, out_weight)
     y_ref[...] = y
-    n2_ref[...] = (y * rms(y) * cross_gain_ref[...]).astype(BF16)
+    n2_ref[...] = (y * rms(y) * row(cross_gain_ref)).astype(BF16)
     for j in range(3):
         w2.share(j)
     rows_memory.forward()
     for j in range(3):
         w2.finish(j)
-    rows_memory.finish()
+        for i in range(3, 6):
+            hold(i, j).start()
+    for j in range(3):
+        for i in range(3, 6):
+            hold(i, j).wait()
+
+    def ask(h, carry):
+        q2_ref[h] = padded(nt(n2_ref[...], cross_full[0][h, 0]).astype(BF16), pw)
+        return carry
+
+    lax.fori_loop(0, shards, ask, 0)
+
+    def bring(plane, j):
+        rows = pl.ds(pl.multiple_of(plane * block, block), block)
+        return pltpu.make_async_copy(
+            memory_out.at[:, rows, :], mem_ref.at[:, rows, :], local.at[j]
+        )
+
+    for j, (plane, slot) in enumerate(((me, None), (links.far, 1), (links.pair, 0), (links.cross, 2))):
+        if slot is not None:
+            if slot != 1:
+                rows_memory.take(slot)
+            bring(plane, j).start()
+            bring(plane, j).wait()
+        first = pl.multiple_of(plane * block, block)
+        m = mem_ref[:, pl.ds(first, block), :].reshape(rows, -1)
+
+        def answer(h, carry, first=first, m=m):
+            for into, which in ((k2_ref, 0), (v2_ref, 1)):
+                value = padded(nt(m, cross_full[1][h, which]).astype(BF16), pw)
+                for s in range(seqs):
+                    into[h, pl.ds(s * full + first, block), :] = value[s * block : (s + 1) * block]
+            return carry
+
+        lax.fori_loop(0, shards, answer, 0)
+
+    def cross_body(h, carry):
+        for s in range(seqs):
+            c, lse2_ref[h, s] = head_context(
+                q2_ref[h, s * block : (s + 1) * block, :],
+                k2_ref[h, s * full : (s + 1) * full, :],
+                v2_ref[h, s * full : (s + 1) * full, :],
+                None,
+                key < enc_ref[s],
+                lanes,
+            )
+            c2_ref[h, s * block : (s + 1) * block, :] = c
+        for i in range(7, 12):
+            keep(i, h).start()
+        return carry
+
+    lax.fori_loop(0, shards, cross_body, 0)
+    joined = jnp.concatenate([c2_ref[h][:, :win] for h in range(shards)], axis=1)
+    out_weight = cross_full[2][...].reshape(shards * win, -1)
+    y2 = y_ref[...] + nn(joined, out_weight)
+    y2_ref[...] = y2
+    n3_ref[...] = (y2 * rms(y2) * row(feed_gain_ref)).astype(BF16)
     w1.drain()
     w2.drain()
     rows_one.drain()
@@ -1004,11 +1088,11 @@
     for i in range(2):
         keep(i).wait()
     for h in range(shards):
-        for i in range(2, 7):
+        for i in range(2, 12):
             keep(i, h).wait()
 
 
-def front(lens, x, self_gain, cross_gain, table, onehot, memory, weights, shards, group, size):
+def front(lens, encs, x, gains, table, memory, weights, shards, group, size):
     rows, width = x.shape
     seqs = lens.shape[0]
     block = rows // seqs
@@ -1019,6 +1103,7 @@
     kept = [((seqs, full, width), BF16), ((shards * group, block, full), BF16)]
     kept += [((shards, n, pw), BF16) for n in (rows, keys, keys, rows)]
     kept.append(((shards, seqs, block, 128), F32))
+    kept += kept[2:]
     dma = pltpu.SemaphoreType.DMA
     anywhere = pl.BlockSpec(memory_space=pl.ANY)
     return pl.pallas_call(
@@ -1027,20 +1112,19 @@
             sds((rows, width), BF16),
             sds((rows, width), F32),
             sds((rows, width), BF16),
+            sds((rows, width), F32),
+            sds((rows, width), BF16),
             sds((seqs, full, width), BF16),
         ]
         + [sds(*a) for a in fulls + kept],
-        in_specs=[smem()] + [vmem()] * 5 + [anywhere] * 7,
-        out_specs=[vmem()] * 3 + [anywhere] * 14,
-        scratch_shapes=[pltpu.VMEM(*a) for a in kept + fulls[:3]]
+        in_specs=[smem()] * 2 + [vmem()] * 5 + [anywhere] * 7,
+        out_specs=[vmem()] * 5 + [anywhere] * 19,
+        scratch_shapes=[pltpu.VMEM(*a) for a in kept + fulls]
         + [
-            pltpu.VMEM((shards, *table.shape), BF16),
+            pltpu.VMEM((shards, 8, 128), BF16),
             pltpu.VMEM((block, full + block), F32),
-            pltpu.VMEM((table.shape[1], 2 * block), F32),
-            pltpu.VMEM(memory.shape, BF16),
-        ]
-        + [pltpu.VMEM(w.shape, BF16) for w in weights[3:]]
-        + [
+            pltpu.VMEM((8, 2 * block), F32),
+            pltpu.VMEM((seqs, full, width), BF16),
             dma((3,)),
             dma((3,)),
             dma((seqs, 3)),
@@ -1049,7 +1133,7 @@
             dma((seqs, 3)),
             dma((7,)),
             dma((6 + seqs,)),
-            dma((3, 3)),
+            dma((6, 3)),
             dma((len(kept), shards)),
         ]
         + Weights.scratch(3)
@@ -1058,7 +1142,7 @@
             collective_id=0, has_side_effects=True, vmem_limit_bytes=VMEM_LIMIT
         ),
         name="front",
-    )(lens, x, self_gain, cross_gain, table, onehot, memory, *weights)
+    )(lens, encs, x, *gains, table, memory, *weights)
 
 
 class Rows:
@@ -1136,7 +1220,7 @@
     held_count = 11 if biased else 10
     held, refs = refs[:held_count], refs[held_count:]
     if biased:
-        feed_ref, x_ref, rows_ref, lines_ref, *refs = refs
+        feed_ref, x_ref, rows_ref, gain2_ref, gain3_ref, *refs = refs
         grad_ref, mem_ref, feed_out, given_out, own_out, small_out, *refs = refs
     else:
         y_ref, dprev_ref, gg_ref, w_ref, later_ref, mem_ref, given_out, *refs = refs
@@ -1341,7 +1425,7 @@
 
     steps = range(4 * seqs, places + late[-1][1])
     if not biased:
-        dy, gg = norm_grads(y_ref[...], gain_ref[...], accq_ref[...])
+        dy, gg = norm_grads(y_ref[...], row(gain_ref), accq_ref[...])
         dprev_ref[...] = dy_ref[...] + dy
         gg_ref[...] = gg
         for t in steps:
@@ -1352,15 +1436,15 @@
         for h in range(shards):
             pltpu.make_async_copy(wtmp_ref.at[h], w_ref.at[h], w_sem.at[h]).wait()
     else:
-        gain1 = gain1 / gain_ref[...]
+        gain1 = gain1 / row(gain_ref)
         width = gain1.shape[1]
         diag_ref[shards * group :, :] = jnp.zeros_like(diag_ref[shards * group :, :])
-        lines = lines_ref.shape[0]
         sr[0, : diag_ref.shape[0], :] = diag_ref[...]
-        sr[0, diag_ref.shape[0] :, :] = lines_ref[...]
-        for j in range(width // (2 * block)):
-            row = diag_ref.shape[0] + j
-            sr[0, row : row + 1, :] = gain1[:, j * 2 * block : (j + 1) * 2 * block]
+        sr[0, diag_ref.shape[0] :, :] = jnp.zeros_like(sr[0, diag_ref.shape[0] :, :])
+        for i, line in enumerate((gain1, gain2_ref[...], gain3_ref[...])):
+            for j in range(width // (2 * block)):
+                at = diag_ref.shape[0] + i * width // (2 * block) + j
+                sr[0, at : at + 1, :] = line[:, j * 2 * block : (j + 1) * 2 * block]
         plane = 2 + 2 * links.y + links.x
         hops = [(1, 0, links.over_core)]
         hops += [(plane, plane, to) for to in (links.over_x, links.over_y, links.over_plane)]
@@ -1393,7 +1477,7 @@
         for s in range(seqs):
             mine = slice(s * block, (s + 1) * block)
             dn = grad_ref[mine, :] + exchanges[1 + s].finish()
-            dx, _ = norm_grads(x_ref[mine, :].astype(F32), gain_ref[...], dn)
+            dx, _ = norm_grads(x_ref[mine, :].astype(F32), row(gain_ref), dn)
             grad_ref[mine, :] = dy_ref[mine, :] + dx
         own_out[...] = sums.finish(1)
         for i in range(len(hops)):
@@ -1421,7 +1505,7 @@
     args = [lens, dy, gain, split(given), *held, *extras]
     part = split(extras[0] if biased else given).shape[-1] // 3
     if biased:
-        lines = extras[3].shape[0]
+        lines = -(-3 * width // (2 * block) // 8) * 8
         diag_rows = -(-shards * group // 8) * 8
         out_shape = [
             sds((rows, width), F32),
@@ -1488,6 +1572,71 @@
     )(*args)
 
 
+def arrange_kernel(
+    shards, group, win, me_ref, grad_ref, first_ref, last_ref, gates_ref, hid_ref, cross_ref,
+    self_ref, small_ref, grad_out, mem_out, gates_out, hid_out, table_out, *refs,
+):
+    gain_outs, weight_outs = refs[:3], refs[3:]
+    grad_out[...] = grad_ref[...].reshape(grad_out.shape)
+    mem_out[0] = first_ref[...]
+    mem_out[1] = last_ref[...]
+    gates_out[...] = gates_ref[...]
+    hid_out[...] = hid_ref[...]
+    for i, w_ref in enumerate((self_ref, cross_ref)):
+        q_out, kv_out, o_out = weight_outs[3 * i : 3 * i + 3]
+        w = w_ref[...]
+        kv_out[0] = w[:, :win]
+        kv_out[1] = w[:, win : 2 * win]
+        q_out[...] = w[:, 2 * win : 3 * win]
+        o_out[...] = w[:, 3 * win :].T
+    head_rows = -(-shards * group // 8) * 8
+    span = small_ref.shape[1]
+    heads = lax.broadcasted_iota(jnp.int32, (8, head_rows), 0) + me_ref[0] * group
+    pick = (heads == lax.broadcasted_iota(jnp.int32, (8, head_rows), 1)).astype(F32)
+    mine = jnp.dot(pick, small_ref[:head_rows, :], precision=highest)
+    onehot = bucket_rows(span // 2, NB).astype(F32)
+    sums = lax.dot_general(mine, onehot, (((1,), (1,)), ((), ())), precision=highest)
+    table_out[...] = sums[:group, :]
+    for i, gain_out in enumerate(gain_outs):
+        lines = [
+            small_ref[head_rows + i * gain_out.shape[0] // span + j, :]
+            for j in range(gain_out.shape[0] // span)
+        ]
+        gain_out[...] = jnp.concatenate(lines)
+
+
+def arranged(
+    me, result, grad, first, last, gates, hid, cross_w, self_w, small, shards, group, win
+):
+    rows, width = grad.shape
+    block = first.shape[0]
+    share, part = hid.shape
+    weights = [sds((share, win), F32), sds((2, share, win), F32), sds((win, share), F32)]
+    grad, mem, gates, hid, table, gain1, gain2, gain3, *weights = pl.pallas_call(
+        functools.partial(arrange_kernel, shards, group, win),
+        out_shape=[
+            sds((rows // block, block, width), F32),
+            sds((rows // block, block, width), F32),
+            sds(gates.shape, F32),
+            sds((share, part), F32),
+            sds((group, NB), F32),
+            sds((width,), F32),
+            sds((width,), F32),
+            sds((width,), F32),
+            *weights,
+            *weights,
+        ],
+        in_specs=[smem()] + [vmem()] * 8,
+        out_specs=[vmem()] * 14,
+        compiler_params=params(),
+        name="arrange",
+    )(me, grad, first, last, gates, hid, cross_w, self_w, small)
+    result = result.reshape(grad.shape)
+    return (
+        result, grad, mem, gain1, *weights[:3], table.T, gain2, *weights[3:], gain3, gates, hid.T
+    )
+
+
 def per_device(
     layer_input,
     memory,
@@ -1518,66 +1667,67 @@
     enc_full = memory.shape[1] * shards
     rows = seqs * block
     part = feed_in.shape[2] // shards
-    sg, cg, fg = (g.astype(F32).reshape(1, width) for g in (self_gain, cross_gain, feed_gain))
+    sg = self_gain.astype(F32).reshape(1, width)
 
     x = layer_input.reshape(rows, width)
     x32 = x.astype(F32)
     tight = batch_count == 8 and shards == 4 and seqs == 2
     order = tuple((i % 2) * 4 + i // 2 for i in range(8)) if tight else (0,)
-    table = jnp.pad(rel_bias, ((0, 0), (0, 128 - group)))
+    table = rel_bias.T
     flip = lambda w: jnp.swapaxes(w, -1, -2)
     weights = [flip(self_query)[None], flip(self_key_value), self_out[None]]
     weights += [flip(cross_query)[None], flip(cross_key_value), cross_out[None]]
     onehot = near_onehot(block)
-    lines_of = onehot.T.astype(BF16)
     if tight:
-        n1, y1, n2, memory_all, wq1, wkv1, wo1, wq2, wkv2, wo2, n1_all, bias, *saved1 = front(
-            dec_lengths, x, sg, cg, table, lines_of, memory, weights, shards, group, size
-        )
+        n1, y1, n2, y2, n3, memory_all, wq1, wkv1, wo1, wq2, wkv2, wo2, n1_all, bias, *saved = front(
+            dec_lengths, enc_lengths, x, (self_gain, cross_gain, feed_gain), table, memory, weights,
+            shards, group, size,
+        )
+        saved1, saved2 = saved[:5], saved[5:]
         n1_all = n1_all.reshape(seqs * full, width)
     else:
         n1 = (x32 * rms(x32) * sg).astype(BF16)
         n1_all = lax.all_gather(n1.reshape(seqs, block, width), "head", axis=1, tiled=True)
         n1_all = n1_all.reshape(seqs * full, width)
         wq1, wkv1, wo1, wq2, wkv2, wo2 = [lax.all_gather(w, "head", axis=0) for w in weights]
+        table = jnp.pad(table, ((0, 8 - group), (0, 128 - NB)))
         tables = lax.all_gather(table, "head", axis=0)
-        bias = bias_tiles(me, tables, lines_of, group, block, full)
+        bias = bias_tiles(me, tables, group, block, full)
         memory_all = lax.all_gather(memory, "head", axis=1, tiled=True)
     memory_all = memory_all.reshape(seqs * enc_full, width)
     wq1, wq2 = wq1[:, 0], wq2[:, 0]
     wo1, wo2 = wo1.reshape(width, width), wo2.reshape(width, width)
     if not tight:
         *saved1, y1, n2 = attend_forward(
-            dec_lengths, n1, n1_all, x, wq1, wkv1, wo1, cg, bias, group, size
-        )
-    *saved2, y2, n3 = attend_forward(
-        enc_lengths, n2, memory_all, y1, wq2, wkv2, wo2, fg, None, group, size
-    )
+            dec_lengths, n1, n1_all, x, wq1, wkv1, wo1, cross_gain, bias, group, size
+        )
+        *saved2, y2, n3 = attend_forward(
+            enc_lengths, n2, memory_all, y1, wq2, wkv2, wo2, feed_gain, None, group, size
+        )
     result, dy2, gain3, feed_w = feed(
-        y2, n3, out_cotangent.reshape(rows, width), feed_in, feed_out, fg, shards, order
+        y2, n3, out_cotangent.reshape(rows, width), feed_in, feed_out, feed_gain, shards, order
     )
     gain_rows = width // (2 * block)
     if tight:
         dy1, gain2, cross_w, memory_later, memory_first, feed_in_grad = linked_backward(
-            enc_lengths, n2, memory_all, saved2, wq2, wkv2, wo2, dy2, cg, feed_w, [y1],
+            enc_lengths, n2, memory_all, saved2, wq2, wkv2, wo2, dy2, cross_gain, feed_w, [y1],
             False, group, size, order,
         )
-        lines = jnp.concatenate([jnp.zeros((1, width), F32), gain2, gain3], axis=0)
-        lines = lines.reshape(-1, 2 * block)
-        lines = jnp.pad(lines, ((0, -lines.shape[0] % 8), (0, 0)))
         input_grad, memory_last, feed_out_grad, cross_w, self_w, small = linked_backward(
-            dec_lengths, n1, n1_all, saved1, wq1, wkv1, wo1, dy1, sg, cross_w,
-            [feed_w, bias, x, memory_later, lines], True, group, size, order,
-        )
-        memory_grad = jnp.stack([memory_first, memory_last])
-        diag, lines = small[: -lines.shape[0]], small[-lines.shape[0] :]
+            dec_lengths, n1, n1_all, saved1, wq1, wkv1, wo1, dy1, self_gain, cross_w,
+            [feed_w, bias, x, memory_later, gain2, gain3], True, group, size, order,
+        )
+        return arranged(
+            me, result, input_grad, memory_first, memory_last, feed_in_grad, feed_out_grad,
+            cross_w, self_w, small, shards, group, win,
+        )
     else:
         memory_part, gain2, cross_w, dy1 = attend_backward(
-            enc_lengths, me, n2, memory_all, saved2, wq2, wkv2, wo2, dy2, cg, y1,
+            enc_lengths, me, n2, memory_all, saved2, wq2, wkv2, wo2, dy2, cross_gain, y1,
             False, group, size, order,
         )
         input_part, gain1, self_w, diag = attend_backward(
-            dec_lengths, me, n1, n1_all, saved1, wq1, wkv1, wo1, dy1, sg, bias,
+            dec_lengths, me, n1, n1_all, saved1, wq1, wkv1, wo1, dy1, self_gain, bias,
             True, group, size, order,
         )
         memory_grad = lax.psum_scatter(

time: 255 us -> 240 us (0.941)
  local copies, waits for them, and re-layouts: 12.9 us -> 0 us
  other arithmetic: 3.69 us -> 0 us
    pallas_call x1, Pallas kernels: 13.8 us -> 3.57 us  [arranged(): pl.pallas_call(functools.partial(arrange_kernel, shards, group, win), out...]
    pallas_call x1, Pallas kernels: 83.6 us -> 92.3 us  [front(): pl.pallas_call(functools.partial(front_kernel, group, size), out_shape=[s...]
    unnamed x22 -> x0, local copies, waits for them, and re-layouts: 4.59 us -> none
    pallas_call x2, Pallas kernels: 126 us -> 129 us  [linked_backward(): pl.pallas_call(functools.partial(linked_kernel, biased, group, size, orde...]
    reshape x4 -> x0, local copies, waits for them, and re-layouts: 3.12 us -> none  [the longest x3 3.1 us: per_device(): g.astype(F32).reshape(1, width)]
where the time goes in v5:
time: 240 us
  Pallas kernels  239 us (100%)
    pallas_call x2, Pallas kernels, linked_backward(): pl.pallas_call(functools.partial(linked_kernel, biased, group, size, orde...  129 us
    pallas_call x1, Pallas kernels, front(): pl.pallas_call(functools.partial(front_kernel, group, size), out_shape=[s...  92.3 us
    pallas_call x1, Pallas kernels, feed(): pl.pallas_call(functools.partial(feed_kernel, order), grid=(shards,), out...  13.7 us

profile of v5, /device:TPU:0, one launch (start us, length us, event | category | flops | bytes accessed | tf_op | source)
XLA Modules:
  0.0 239.8 jit_solution(9554764257301188930)
XLA Ops:
  0.6 92.3 %front.1 = (bf16[256,768]{1,0:T(8,128)(2,1)}, f32[256,768]{1,0:T(8,128)}, bf16[256,768]{1,0:T(8,128)(2,1)}, f32[256,768]{1,0:T(8,128)}, bf16[256,768]{1,0:T(8,12...) custom-call(s32[2]{0:T(128)} %refs_0_.5, ...), custom_call_target="tpu_custom_call" | custom-call | tf_op jit(solution)/shard_map/front/pallas_call | solution.py:1109
  92.9 13.7 %feed.1 = (bf16[256,768]{1,0:T(8,128)(2,1)}, f32[256,768]{1,0:T(8,128)}, f32[1,768]{1,0:T(1,128)}, bf16[4,768,1536]{2,1,0:T(8,128)(2,1)}) custom-call(f32[256,768]{1,0:T(8,128)} %get-tuple-element.69.y_ref, bf16[256,768]{1,0:T(8,128)(2,1)} %get-tuple-element.70.n_ref, bf16[256,768]{1,0:T(8,128)(2,1)} %bitcast.41, bf16[2,768,2048]{2,1,0:T(8,128)(2,1)} %win_ref.1, ...), custom_call_target="tpu_custom_call" | custom-call | flops 7247757312 | bytes 25165824 | tf_op jit(solution)/shard_map/feed/pallas_call | solution.py:498
  106.6 49.3 %cross_backward.1 = (f32[256,768]{1,0:T(8,128)}, f32[1,768]{1,0:T(1,128)}, bf16[4,2,2,2,96,768]{5,4,3,2,1,0:T(8,128)(2,1)}, bf16[4,128,768]{2,1,0:T(8,128)(2,1)}...) custom-call(s32[2]{0:T(128)} %refs_0_.4, f32[256,768]{1,0:T(8,128)} %get-tuple-element.72.refs_1_, bf16[768]{0:T(1024)(128)(2,1)} %refs_2_.2, ...), custom_call_target="tpu_custom_call" | custom-call | tf_op jit(solution)/shard_map/cross_backward/pallas_call | solution.py:1562
  155.9 80.2 %self_backward.1 = (f32[256,768]{1,0:T(8,128)}, f32[128,768]{1,0:T(8,128)}, f32[96,512]{1,0:T(8,128)}, f32[96,768]{1,0:T(8,128)}, f32[96,768]{1,0:T(8,128)}, /*index=5*/f32[32,256]{1,0:T(8,128)}) custom-call(s32[2]{0:T(128)} %refs_0_.5, f32[256,768]{1,0:T(8,128)} %get-tuple-element.85.refs_1_, bf16[768]{0:T(1024)(128)(2,1)} %refs_2_.3, ...), custom_call_target="tpu_custom_call" | custom-call | tf_op jit(solution)/shard_map/self_backward/pallas_call | solution.py:1562
  236.1 3.6 %arrange.1 = (f32[2,128,768]{2,1,0:T(8,128)}, f32[2,128,768]{2,1,0:T(8,128)}, f32[2,96,512]{2,1,0:T(8,128)}, f32[96,512]{1,0:T(8,128)}, f32[3,32]{1,0:T(4,128)},...) custom-call(s32[1]{0:T(128)} %bitcast.12.me_ref, ...), custom_call_target="tpu_custom_call" | custom-call | tf_op jit(solution)/shard_map/arrange/pallas_call | solution.py:1615

commit v6 on v5

--- a/solution.py
+++ b/solution.py
@@ -448,25 +448,10 @@
     )(*args)
 
 
-def feed_kernel(
-    order, y_ref, n_ref, cot_ref, win_ref, wout_ref, gain_ref, out_ref, dy_ref, gg_ref, w_ref,
-    acc_ref, dn_ref, nt_ref, ct_ref,
-):
-    step = pl.program_id(0)
-    part = wout_ref.shape[0]
-
-    @pl.when(step == 0)
-    def _():
-        put_rows(nt_ref, n_ref[...].T, order)
-        put_rows(ct_ref, cot_ref[...].T, order)
-        acc_ref[...] = y_ref[...]
-        dn_ref[...] = jnp.zeros_like(dn_ref)
-
-    n = n_ref[...]
-    cot = cot_ref[...]
-    g = nn(n, win_ref[0])
-    u = nn(n, win_ref[1])
-    dh = nt(cot, wout_ref[...])
+def feed_tile(n, cot, w_gate, w_up, w_out):
+    g = nn(n, w_gate)
+    u = nn(n, w_up)
+    dh = nt(cot, w_out)
     scale = math.sqrt(2.0 / math.pi)
     square = g * g
     t = jnp.tanh(scale * (g + 0.044715 * square * g))
@@ -474,8 +459,24 @@
     gelu = g * half
     hid = (gelu * u).astype(BF16)
     slope = half + 0.5 * g * (1.0 - t * t) * (scale * (1.0 + 3 * 0.044715 * square))
-    dg = (dh * u * slope).astype(BF16)
-    du = (dh * gelu).astype(BF16)
+    return hid, (dh * u * slope).astype(BF16), (dh * gelu).astype(BF16)
+
+
+def feed_kernel(
+    order, y_ref, n_ref, cot_ref, win_ref, wout_ref, gain_ref, out_ref, dy_ref, gg_ref, w_ref,
+    acc_ref, dn_ref, nt_ref, ct_ref,
+):
+    step = pl.program_id(0)
+    part = wout_ref.shape[0]
+
+    @pl.when(step == 0)
+    def _():
+        put_rows(nt_ref, n_ref[...].T, order)
+        put_rows(ct_ref, cot_ref[...].T, order)
+        acc_ref[...] = y_ref[...]
+        dn_ref[...] = jnp.zeros_like(dn_ref)
+
+    hid, dg, du = feed_tile(n_ref[...], cot_ref[...], win_ref[0], win_ref[1], wout_ref[...])
     acc_ref[...] += nn(hid, wout_ref[...])
     dn_ref[...] += nt(dg, win_ref[0]) + nt(du, win_ref[1])
     w_ref[0, :, :part] = nn(nt_ref[...], dg).astype(BF16)
@@ -736,6 +737,9 @@
             def _(slot=slot):
                 self.tot[c] = self.whole(c).astype(BF16)
                 self.along(item, slot, c).start()
+
+    def third(self, c):
+        item, k = c // 4, c % 4
 
         @pl.when(k == 2)
         def _():
@@ -1223,7 +1227,9 @@
         feed_ref, x_ref, rows_ref, gain2_ref, gain3_ref, *refs = refs
         grad_ref, mem_ref, feed_out, given_out, own_out, small_out, *refs = refs
     else:
-        y_ref, dprev_ref, gg_ref, w_ref, later_ref, mem_ref, given_out, *refs = refs
+        feed_out_ref, y_ref, y2_ref, n3_ref, feed_gain_ref, *refs = refs
+        dprev_ref, gg_ref, w_ref, later_ref, mem_ref, given_out, *refs = refs
+        result_ref, gg3_ref, hid_out, *refs = refs
     buffers, held_sem, refs = refs[:held_count], refs[held_count], refs[held_count + 1 :]
     nq_ref, nk_ref, c_ref, wo_ref, q_ref, k_ref, v_ref, lse_ref, wq_ref, wkv_ref = buffers[:10]
     bias_ref = buffers[-1]
@@ -1241,7 +1247,9 @@
     if biased:
         ds_ref, ext_ref, diag_ref, sr, ms, mr = refs
     else:
-        (w_sem,) = refs
+        cot_ref, feed_in_ref = dy_ref, given_ref
+        w_sem, dy_ref, dn_ref, n3t_ref, ct_ref, wff_ref, hid_ref, win_ref, wout_ref, *refs = refs
+        f_sem, hid_sem = refs
     shards, rows, pw = q_ref.shape
     seqs = len_ref.shape[0]
     block = rows // seqs
@@ -1261,8 +1269,30 @@
     if biased:
         exchanges[0].buf[...] = rows_ref[...]
         exchanges[0].start()
-    for place in range(AHEAD):
-        sums.load(given_ref, place)
+        for place in range(AHEAD):
+            sums.load(given_ref, place)
+    else:
+        part = wout_ref.shape[1]
+
+        def feed_weights(k):
+            columns = pl.ds(pl.multiple_of(links.owner(k) * part, part), part)
+            slot = k % 2
+            return (
+                pltpu.make_async_copy(
+                    feed_in_ref.at[:, :, columns], win_ref.at[slot], f_sem.at[slot, 0]
+                ),
+                pltpu.make_async_copy(
+                    feed_out_ref.at[columns, :], wout_ref.at[slot], f_sem.at[slot, 1]
+                ),
+            )
+
+        def hid_copy(k):
+            return pltpu.make_async_copy(
+                hid_ref.at[k % 2], hid_out.at[links.owner(k)], hid_sem.at[k]
+            )
+
+        for copy in feed_weights(0):
+            copy.start()
     fetch(3).start()
     for k in range(shards):
         for j in range(4, held_count):
@@ -1272,9 +1302,6 @@
 
     def stage(name, place):
         if name == "load":
-            if not biased:
-                sums.load(given_ref, place)
-                return
 
             @pl.when(place < 4)
             def _():
@@ -1282,12 +1309,11 @@
 
             @pl.when(place >= 4)
             def _():
-                feed_sums.load(feed_ref, place - 4, 2 * feed_sums.cols)
+                feed_sums.load(feed_ref, place - 4)
 
             return
         if not biased:
-            run = getattr(sums, name)
-            run(place, given_ref) if name == "core" else run(place)
+            getattr(sums, name)(4 * (place % 2) + place // 2)
             return
 
         @pl.when(place < 4)
@@ -1298,7 +1324,7 @@
         def _():
             c = place - 4
             if name == "core":
-                feed_sums.core(c, feed_ref, 2 * feed_sums.cols)
+                feed_sums.core(c, feed_ref)
             else:
                 getattr(feed_sums, name)(c)
 
@@ -1307,7 +1333,9 @@
             getattr(sums, name)(place - 4)
 
     places = 12 if biased else sums.chunks
-    late = (("load", -AHEAD), ("core", 0), ("first", 1), ("second", 3))
+    late = (("core", 1), ("first", 3), ("second", 5), ("third", 7))
+    if biased:
+        late = (("load", -AHEAD), *late)
 
     def tick(t):
         for name, behind in late:
@@ -1316,12 +1344,58 @@
             @pl.when((place >= 0) & (place < (8 if name == "load" else places)))
             def _(name=name, place=place):
                 stage(name, place)
+
+    if not biased:
+        share = nqt_ref.shape[0] // 8
+        put_rows(n3t_ref, n3_ref[...].T, order)
+        put_rows(ct_ref, cot_ref[...].T, order)
+        dprev_ref[...] = y2_ref[...]
+        dn_ref[...] = jnp.zeros_like(dn_ref)
+
+        def feed_body(k, carry):
+            @pl.when(k + 1 < shards)
+            def _():
+                for copy in feed_weights(k + 1):
+                    copy.start()
+
+            for copy in feed_weights(k):
+                copy.wait()
+            slot = k % 2
+            w_gate, w_up, w_out = win_ref[slot, 0], win_ref[slot, 1], wout_ref[slot]
+            hid, dg, du = feed_tile(n3_ref[...], cot_ref[...], w_gate, w_up, w_out)
+            for item, right in enumerate((dg, du)):
+
+                def rows_of(side, right=right):
+                    rows = pl.ds(pl.multiple_of(side * 4 * share, 4 * share), 4 * share)
+                    return nn(n3t_ref[rows, :], right).astype(BF16).reshape(2, 2, share, part)
+
+                c = 4 * item + k
+                wff_ref[c] = rows_of(1 - links.core)
+                sums.over_core(c, wff_ref.at[c]).start()
+                sums.own[c] = rows_of(links.core)
+
+            @pl.when(k >= 2)
+            def _():
+                hid_copy(k - 2).wait()
+
+            hid_ref[slot] = nn(ct_ref[...], hid).astype(BF16).reshape(2, 2, 2, share, part)
+            hid_copy(k).start()
+            dprev_ref[...] += nn(hid, w_out)
+            dn_ref[...] += nt(dg, w_gate) + nt(du, w_up)
+            tick(k)
+            return carry
+
+        lax.fori_loop(0, shards, feed_body, 0)
+        result_ref[...] = dprev_ref[...].astype(BF16)
+        dy, gg3_ref[...] = norm_grads(y2_ref[...], row(feed_gain_ref), dn_ref[...])
+        dy_ref[...] = cot_ref[...].astype(F32) + dy
 
     da = dy_ref[...].astype(BF16)
     if biased:
         ext_ref[:, :block] = jnp.zeros((block, block), F32)
         far = lax.broadcasted_iota(jnp.int32, ext_ref.shape, 1) < start
     fetch(3).wait()
+    first_tick = 0 if biased else shards
 
     for s in range(seqs):
         mine = slice(s * block, (s + 1) * block)
@@ -1400,7 +1474,7 @@
                     for side in range(2):
                         wtmp_ref[h, side] = weight_rows(side)
                     pltpu.make_async_copy(wtmp_ref.at[h], w_ref.at[h], w_sem.at[h]).start()
-            tick(4 * s + k)
+            tick(first_tick + 4 * s + k)
             return carry
 
         w_rows = nqt_ref.shape[0] // 8
@@ -1423,7 +1497,7 @@
         else:
             later_ref[...] = acck_ref[...].astype(BF16).reshape(shards, block, -1)
 
-    steps = range(4 * seqs, places + late[-1][1])
+    steps = range(first_tick + 4 * seqs, places + late[-1][1])
     if not biased:
         dy, gg = norm_grads(y_ref[...], row(gain_ref), accq_ref[...])
         dprev_ref[...] = dy_ref[...] + dy
@@ -1435,6 +1509,8 @@
             given_out[item] = sums.finish(item)
         for h in range(shards):
             pltpu.make_async_copy(wtmp_ref.at[h], w_ref.at[h], w_sem.at[h]).wait()
+        for k in range(2, shards):
+            hid_copy(k).wait()
     else:
         gain1 = gain1 / row(gain_ref)
         width = gain1.shape[1]
@@ -1497,13 +1573,14 @@
     block, full, win = rows // seqs, keys // seqs, group * size
     cols = 4 * win
     share = width // 8
-    split = lambda w: w.reshape(shards, 2, 2, 2, share, -1)
     held = [nq, nk, c, wo, q, k, v, lse, wq, wkv]
     if biased:
         held.append(extras[1])
-        extras = [split(extras[0]), *extras[2:]]
-    args = [lens, dy, gain, split(given), *held, *extras]
-    part = split(extras[0] if biased else given).shape[-1] // 3
+        extras = [extras[0], *extras[2:]]
+        part = extras[0].shape[-1]
+    else:
+        part = given.shape[2] // shards
+    args = [lens, dy, gain, given, *held, *extras]
     if biased:
         lines = -(-3 * width // (2 * block) // 8) * 8
         diag_rows = -(-shards * group // 8) * 8
@@ -1523,6 +1600,9 @@
             sds((shards, block, width), BF16),
             sds((block, width), F32),
             sds((2, share, part), F32),
+            sds((rows, width), BF16),
+            sds((1, width), F32),
+            sds((shards, 2, 2, 2, share, part), BF16),
         ]
     scratch = [pltpu.VMEM(a.shape, a.dtype) for a in held]
     scratch += [
@@ -1541,8 +1621,8 @@
         scratch += Sums.scratch(4, share, part)
     for _ in range(3 if biased else 1):
         scratch += Rows.scratch(block, width)
+    dma = pltpu.SemaphoreType.DMA
     if biased:
-        dma = pltpu.SemaphoreType.DMA
         scratch += [
             pltpu.VMEM((shards, group * block, full), BF16),
             pltpu.VMEM((block, full + block), F32),
@@ -1552,13 +1632,25 @@
             dma((7,)),
         ]
     else:
-        scratch.append(pltpu.SemaphoreType.DMA((shards,)))
+        scratch += [
+            dma((shards,)),
+            pltpu.VMEM((rows, width), F32),
+            pltpu.VMEM((rows, width), F32),
+            pltpu.VMEM((width, rows), BF16),
+            pltpu.VMEM((width, rows), BF16),
+            pltpu.VMEM((8, 2, 2, share, part), BF16),
+            pltpu.VMEM((2, 2, 2, 2, share, part), BF16),
+            pltpu.VMEM((2, 2, width, part), BF16),
+            pltpu.VMEM((2, part, width), BF16),
+            dma((2, 2)),
+            dma((shards,)),
+        ]
     anywhere = pl.BlockSpec(memory_space=pl.ANY)
     in_specs = [smem(), vmem(), vmem(), anywhere] + [anywhere] * len(held)
-    in_specs += [anywhere if biased else vmem()] + [vmem()] * (len(extras) - 1)
+    in_specs += [anywhere] + [vmem()] * (len(extras) - 1)
     out_specs = [vmem()] * len(out_shape)
     if not biased:
-        out_specs[2] = anywhere
+        out_specs[2] = out_specs[-1] = anywhere
     return pl.pallas_call(
         functools.partial(linked_kernel, biased, group, size, order),
         out_shape=out_shape,
@@ -1704,24 +1796,27 @@
         *saved2, y2, n3 = attend_forward(
             enc_lengths, n2, memory_all, y1, wq2, wkv2, wo2, feed_gain, None, group, size
         )
-    result, dy2, gain3, feed_w = feed(
-        y2, n3, out_cotangent.reshape(rows, width), feed_in, feed_out, feed_gain, shards, order
-    )
     gain_rows = width // (2 * block)
+    cot = out_cotangent.reshape(rows, width)
     if tight:
-        dy1, gain2, cross_w, memory_later, memory_first, feed_in_grad = linked_backward(
-            enc_lengths, n2, memory_all, saved2, wq2, wkv2, wo2, dy2, cross_gain, feed_w, [y1],
-            False, group, size, order,
+        (
+            dy1, gain2, cross_w, memory_later, memory_first, feed_in_grad, result, gain3, hid_w,
+        ) = linked_backward(
+            enc_lengths, n2, memory_all, saved2, wq2, wkv2, wo2, cot, cross_gain, feed_in,
+            [feed_out, y1, y2, n3, feed_gain], False, group, size, order,
         )
         input_grad, memory_last, feed_out_grad, cross_w, self_w, small = linked_backward(
             dec_lengths, n1, n1_all, saved1, wq1, wkv1, wo1, dy1, self_gain, cross_w,
-            [feed_w, bias, x, memory_later, gain2, gain3], True, group, size, order,
+            [hid_w, bias, x, memory_later, gain2, gain3], True, group, size, order,
         )
         return arranged(
             me, result, input_grad, memory_first, memory_last, feed_in_grad, feed_out_grad,
             cross_w, self_w, small, shards, group, win,
         )
     else:
+        result, dy2, gain3, feed_w = feed(
+            y2, n3, cot, feed_in, feed_out, feed_gain, shards, order
+        )
         memory_part, gain2, cross_w, dy1 = attend_backward(
             enc_lengths, me, n2, memory_all, saved2, wq2, wkv2, wo2, dy2, cross_gain, y1,
             False, group, size, order,

time: 240 us -> 238 us (level)
  Pallas kernels: 239 us -> 236 us
    pallas_call x1 -> x0, Pallas kernels: 13.7 us -> none  [feed(): pl.pallas_call(functools.partial(feed_kernel, order), grid=(shards,), out...]
    pallas_call x2, Pallas kernels: 129 us -> 140 us  [linked_backward(): pl.pallas_call(functools.partial(linked_kernel, biased, group, size, orde...]
where the time goes in v6:
time: 238 us
  Pallas kernels  236 us (99%)
    pallas_call x2, Pallas kernels, linked_backward(): pl.pallas_call(functools.partial(linked_kernel, biased, group, size, orde...  140 us
    pallas_call x1, Pallas kernels, front(): pl.pallas_call(functools.partial(front_kernel, group, size), out_shape=[s...  92.3 us

profile of v6, /device:TPU:0, one launch (start us, length us, event | category | flops | bytes accessed | tf_op | source)
XLA Modules:
  0.0 237.6 jit_solution(18243239842352745680)
XLA Ops:
  0.6 92.3 %front.1 = (bf16[256,768]{1,0:T(8,128)(2,1)}, f32[256,768]{1,0:T(8,128)}, bf16[256,768]{1,0:T(8,128)(2,1)}, f32[256,768]{1,0:T(8,128)}, bf16[256,768]{1,0:T(8,12...) custom-call(s32[2]{0:T(128)} %refs_0_.5, ...), custom_call_target="tpu_custom_call" | custom-call | tf_op jit(solution)/shard_map/front/pallas_call | solution.py:1113
  93.0 61.3 %cross_backward.1 = (f32[256,768]{1,0:T(8,128)}, f32[1,768]{1,0:T(1,128)}, bf16[4,2,2,2,96,768]{5,4,3,2,1,0:T(8,128)(2,1)}, bf16[4,128,768]{2,1,0:T(8,128)(2,1)}...) custom-call(s32[2]{0:T(128)} %refs_0_.4, ...), custom_call_target="tpu_custom_call" | custom-call | tf_op jit(solution)/shard_map/cross_backward/pallas_call | solution.py:1654
  154.3 78.9 %self_backward.1 = (f32[256,768]{1,0:T(8,128)}, f32[128,768]{1,0:T(8,128)}, f32[96,512]{1,0:T(8,128)}, f32[96,768]{1,0:T(8,128)}, f32[96,768]{1,0:T(8,128)}, /*index=5*/f32[32,256]{1,0:T(8,128)}) custom-call(s32[2]{0:T(128)} %refs_0_.5, f32[256,768]{1,0:T(8,128)} %get-tuple-element.82.refs_1_, bf16[768]{0:T(1024)(128)(2,1)} %refs_2_.3, ...), custom_call_target="tpu_custom_call" | custom-call | tf_op jit(solution)/shard_map/self_backward/pallas_call | solution.py:1654
  233.2 0.0 copy-start
  233.2 3.6 %arrange.1 = (f32[2,128,768]{2,1,0:T(8,128)}, f32[2,128,768]{2,1,0:T(8,128)}, f32[2,96,512]{2,1,0:T(8,128)}, f32[96,512]{1,0:T(8,128)}, f32[3,32]{1,0:T(4,128)},...) custom-call(s32[1]{0:T(128)} %bitcast.15.me_ref, ...), custom_call_target="tpu_custom_call" | custom-call | tf_op jit(solution)/shard_map/arrange/pallas_call | solution.py:1707
  236.8 0.0 copy-done
  236.8 0.7 copy.33
Async XLA Ops:
  233.2 3.6 %copy-start = (bf16[256,768]{1,0:T(8,128)(2,1)S(1)}, bf16[256,768]{1,0:T(8,128)(2,1)}, u32[]{:S(2)}) copy-start(bf16[256,768]{1,0:T(8,128)(2,1)} %get-tuple-element.81) | copy-start | bytes 1179652

commit v7 on v6

--- a/solution.py
+++ b/solution.py
@@ -850,8 +850,8 @@
         device = links.to_far if slot == 1 else links.to_pair
         return remote(mine, into, self.ss.at[s, slot], self.rs.at[s, slot], device)
 
-    def start(self):
-        for s in range(self.seqs):
+    def start(self, those=(0, 1)):
+        for s in those:
             for slot in (1, 0):
                 self.copy(s, slot).start()
 
@@ -931,9 +931,10 @@
     n_ref[...] = (x * rms(x) * row(self_gain_ref)).astype(BF16)
     for s in range(seqs):
         nall_ref[s, pl.ds(start, block), :] = n_ref[s * block : (s + 1) * block, :]
+    rows_one.start((0,))
     w1.arrive(0)
     w1.arrive(1)
-    rows_one.start()
+    rows_one.start((1,))
     w1.arrive(2)
     for copy in heard:
         copy.wait_recv()

time: 238 us -> 235 us (0.987)
  Pallas kernels: 236 us -> 233 us
where the time goes in v7:
time: 235 us
  Pallas kernels  233 us (99%)
    pallas_call x2, Pallas kernels, linked_backward(): pl.pallas_call(functools.partial(linked_kernel, biased, group, size, orde...  138 us
    pallas_call x1, Pallas kernels, front(): pl.pallas_call(functools.partial(front_kernel, group, size), out_shape=[s...  91.9 us

profile of v7, /device:TPU:0, one launch (start us, length us, event | category | flops | bytes accessed | tf_op | source)
XLA Modules:
  0.0 234.9 jit_solution(10412813395642262991)
XLA Ops:
  0.6 91.9 %front.1 = (bf16[256,768]{1,0:T(8,128)(2,1)}, f32[256,768]{1,0:T(8,128)}, bf16[256,768]{1,0:T(8,128)(2,1)}, f32[256,768]{1,0:T(8,128)}, bf16[256,768]{1,0:T(8,12...) custom-call(s32[2]{0:T(128)} %refs_0_.5, ...), custom_call_target="tpu_custom_call" | custom-call | tf_op jit(solution)/shard_map/front/pallas_call | solution.py:1114
  92.5 60.7 %cross_backward.1 = (f32[256,768]{1,0:T(8,128)}, f32[1,768]{1,0:T(1,128)}, bf16[4,2,2,2,96,768]{5,4,3,2,1,0:T(8,128)(2,1)}, bf16[4,128,768]{2,1,0:T(8,128)(2,1)}...) custom-call(s32[2]{0:T(128)} %refs_0_.4, ...), custom_call_target="tpu_custom_call" | custom-call | tf_op jit(solution)/shard_map/cross_backward/pallas_call | solution.py:1655
  153.2 77.3 %self_backward.1 = (f32[256,768]{1,0:T(8,128)}, f32[128,768]{1,0:T(8,128)}, f32[96,512]{1,0:T(8,128)}, f32[96,768]{1,0:T(8,128)}, f32[96,768]{1,0:T(8,128)}, /*index=5*/f32[32,256]{1,0:T(8,128)}) custom-call(s32[2]{0:T(128)} %refs_0_.5, f32[256,768]{1,0:T(8,128)} %get-tuple-element.82.refs_1_, bf16[768]{0:T(1024)(128)(2,1)} %refs_2_.3, ...), custom_call_target="tpu_custom_call" | custom-call | tf_op jit(solution)/shard_map/self_backward/pallas_call | solution.py:1655
  230.5 0.0 copy-start
  230.5 3.6 %arrange.1 = (f32[2,128,768]{2,1,0:T(8,128)}, f32[2,128,768]{2,1,0:T(8,128)}, f32[2,96,512]{2,1,0:T(8,128)}, f32[96,512]{1,0:T(8,128)}, f32[3,32]{1,0:T(4,128)},...) custom-call(s32[1]{0:T(128)} %bitcast.15.me_ref, ...), custom_call_target="tpu_custom_call" | custom-call | tf_op jit(solution)/shard_map/arrange/pallas_call | solution.py:1708
  234.1 0.0 copy-done
  234.1 0.7 copy.33
Async XLA Ops:
  230.5 3.6 %copy-start = (bf16[256,768]{1,0:T(8,128)(2,1)S(1)}, bf16[256,768]{1,0:T(8,128)(2,1)}, u32[]{:S(2)}) copy-start(bf16[256,768]{1,0:T(8,128)(2,1)} %get-tuple-element.81) | copy-start | bytes 1179652
